TPU v7x, 512 devices: a whole 4x8x8 slice. The times are simulated.
512 devices in a mesh: wide: 32 (over x, y_hi, core), narrow: 16 (over z, y_lo).
Axes of the slice: x: 4, y: 8 (y_hi: 4, y_lo: 2; y = y_hi * 2 + y_lo), z: 8, core: 2. Of those that a mesh axis runs over, the one named last changes fastest.
Arguments:
- volume: bfloat16 [32, 128, 64, 128], P(None, 'wide', 'narrow'), may hold values from -6 to 6
- cotangent: bfloat16 [32, 128, 64, 128], P(None, 'wide', 'narrow'), may hold values from -6 to 6
- conv_first: bfloat16 [3, 3, 3, 32, 32], replicated, may hold values from -0.21875 to 0.21875
- conv_second: bfloat16 [3, 3, 3, 32, 64], replicated, may hold values from -0.21875 to 0.21875
- conv_bottom: bfloat16 [3, 3, 3, 64, 128], replicated, may hold values from -0.3125 to 0.3125
- lift_weight: bfloat16 [64, 128], replicated, may hold values from -2 to 2
- conv_decode: bfloat16 [3, 3, 3, 64, 32], replicated, may hold values from -0.15625 to 0.15625
- conv_final: bfloat16 [3, 3, 3, 32, 32], replicated, may hold values from -0.21875 to 0.21875
Outputs:
- features_out: bfloat16 [32, 128, 64, 128], P(None, 'wide', 'narrow')
- input_grad: bfloat16 [32, 128, 64, 128], P(None, 'wide', 'narrow')
All inputs are finite; a program needn't handle non-finite values.
Results may differ from a plain program's by a relative error of at most 0.013.
Values may be sent and summed in bfloat16 or wider, within the bound.
No kernel may reach another device: no remote copies, remote signals or barrier semaphores. Data moves between devices by JAX's collectives and lax.ppermute only.
A program may use at most 64 MiB of HBM per device.

v0:
```python
import jax
import jax.numpy as jnp
from jax import lax
from jax.sharding import PartitionSpec as P


def extended(cells, sides, width):
    for axis, dim in sides:
        count = lax.axis_size(axis)
        ends = count - 1
        head = lax.slice_in_dim(cells, 0, width, axis=dim)
        tail = lax.slice_in_dim(cells, cells.shape[dim] - width, cells.shape[dim], axis=dim)
        cells = jnp.concatenate(
            [
                lax.ppermute(tail, axis, [(i, (i + 1) % count) for i in range(ends)]),
                cells,
                lax.ppermute(head, axis, [((i + 1) % count, i) for i in range(ends)]),
            ],
            axis=dim,
        )
    return cells


def conv_valid(padded, kernel):
    padded = jnp.pad(padded, ((0, 0), (0, 0), (0, 0), (1, 1)))
    out = lax.conv_general_dilated(
        padded[None],
        kernel,
        (1, 1, 1),
        "VALID",
        dimension_numbers=("NCDHW", "DHWIO", "NCDHW"),
        preferred_element_type=jnp.float32,
    )
    return out[0]


def flipped(kernel):
    return jnp.flip(kernel, (0, 1, 2)).transpose(0, 1, 2, 4, 3)


def blocks(field):
    chans, xs, ys, zs = field.shape
    return field.astype(jnp.float32).reshape(chans, xs // 2, 2, ys // 2, 2, zs // 2, 2)


def pool_mean(field):
    return jnp.mean(blocks(field), axis=(2, 4, 6))


def pool_sum(field):
    return jnp.sum(blocks(field), axis=(2, 4, 6))


def upsample(field):
    return jnp.repeat(jnp.repeat(jnp.repeat(field, 2, 1), 2, 2), 2, 3)


def silu(value):
    return value * jax.nn.sigmoid(value)


def slope(value):
    sigma = jax.nn.sigmoid(value)
    return sigma * (1.0 + value * (1.0 - sigma))


def pointwise(matrix, field):
    chans, xs, ys, zs = field.shape
    flat = field.reshape(chans, xs * ys * zs)
    out = jnp.dot(matrix, flat, preferred_element_type=jnp.float32)
    return out.reshape(matrix.shape[0], xs, ys, zs)


def shards(
    volume, cotangent, conv_first, conv_second, conv_bottom, lift_weight, conv_decode, conv_final
):
    bf = jnp.bfloat16
    f32 = jnp.float32
    edged = extended(volume, (("wide", 1), ("narrow", 2)), 1)
    pre_first = conv_valid(edged, conv_first)
    hidden_first = silu(pre_first).astype(bf)
    pooled_first = pool_mean(hidden_first).astype(bf)
    edged_second = extended(pooled_first, (("wide", 1), ("narrow", 2)), 1)
    pre_second = conv_valid(edged_second, conv_second)
    hidden_second = silu(pre_second).astype(bf)
    pooled_second = pool_mean(hidden_second).astype(bf)
    edged_bottom = extended(pooled_second, (("wide", 1), ("narrow", 2)), 1)
    pre_bottom = conv_valid(edged_bottom, conv_bottom)
    hidden_bottom = silu(pre_bottom).astype(bf)
    joined_second = (
        upsample(pointwise(lift_weight, hidden_bottom)) + hidden_second.astype(f32)
    ).astype(bf)
    edged_decode = extended(joined_second, (("wide", 1), ("narrow", 2)), 1)
    pre_decode = conv_valid(edged_decode, conv_decode)
    hidden_decode = silu(pre_decode).astype(bf)
    joined_first = (upsample(hidden_decode).astype(f32) + hidden_first.astype(f32)).astype(bf)
    joined_wide = extended(joined_first, (("wide", 1), ("narrow", 2)), 1)
    features_out = conv_valid(joined_wide, conv_final).astype(bf)
    edged_grad = extended(cotangent, (("wide", 1), ("narrow", 2)), 1)
    grad_joined = conv_valid(edged_grad, flipped(conv_final)).astype(bf)
    grad_decode = (pool_sum(grad_joined) * slope(pre_decode)).astype(bf)
    edged_decode_grad = extended(grad_decode, (("wide", 1), ("narrow", 2)), 1)
    grad_second_up = conv_valid(edged_decode_grad, flipped(conv_decode)).astype(bf)
    grad_lift = pool_sum(grad_second_up).astype(bf)
    grad_bottom = (pointwise(lift_weight.T, grad_lift) * slope(pre_bottom)).astype(bf)
    edged_bottom_grad = extended(grad_bottom, (("wide", 1), ("narrow", 2)), 1)
    grad_pool_second = conv_valid(edged_bottom_grad, flipped(conv_bottom))
    grad_second = (
        (grad_second_up.astype(f32) + upsample(grad_pool_second) / 8.0) * slope(pre_second)
    ).astype(bf)
    edged_second_grad = extended(grad_second, (("wide", 1), ("narrow", 2)), 1)
    grad_pool_first = conv_valid(edged_second_grad, flipped(conv_second))
    grad_first = (
        (grad_joined.astype(f32) + upsample(grad_pool_first) / 8.0) * slope(pre_first)
    ).astype(bf)
    edged_first_grad = extended(grad_first, (("wide", 1), ("narrow", 2)), 1)
    input_grad = conv_valid(edged_first_grad, flipped(conv_first)).astype(bf)
    return (features_out, input_grad)


def solution(mesh):
    placed = (
        P(None, "wide", "narrow", None),
        P(None, "wide", "narrow", None),
        P(),
        P(),
        P(),
        P(),
        P(),
        P(),
    )
    return jax.shard_map(
        shards,
        mesh=mesh,
        in_specs=placed,
        out_specs=(P(None, "wide", "narrow", None), P(None, "wide", "narrow", None)),
        check_vma=False,
    )
```

profile of v0, /device:TPU:206, one launch (start us, length us, event | category | flops | bytes accessed | tf_op | source)
XLA Modules:
  0.0 261.4 jit_solution(9147401575154147936)
XLA Ops:
  1.5 5.0 %collective-permute-start.1 = (bf16[32,1,4,128]{3,2,1,0:T(4,128)(2,1)S(1)}, bf16[32,1,4,128]{3,2,1,0:T(4,128)(2,1)S(1)}, u32[]{:S(2)}, u32[]{:S(2)}) collective-permute-start(bf16[32,1,4,128]{3,2,1,0:T(4,128)(2,1)S(1)} %get-tuple-element.38), channel_id=1, source_target_pairs={{16,0},{32,16},{48,32},{64,48},{80,64},{96,80},{112,96},{128,112},... | collective-permute-start | bytes 98312 | tf_op jit(solution)/shard_map/ppermute | solution.py:17
  6.5 1.9 collective-permute-start
  9.2 6.7 %collective-permute-start.21 = (bf16[32,1,4,128]{3,2,1,0:T(4,128)(2,1)S(1)}, bf16[32,1,4,128]{3,2,1,0:T(4,128)(2,1)S(1)}, u32[]{:S(2)}, u32[]{:S(2)}) collective-permute-start(bf16[32,1,4,128]{3,2,1,0:T(4,128)(2,1)S(1)} %get-tuple-element.32), channel_id=1, source_target_pairs={{16,0},{32,16},{48,32},{64,48},{80,64},{96,80},{112,96},{128,112},... | collective-permute-start | bytes 98312 | tf_op jit(solution)/shard_map/ppermute | solution.py:17
  15.9 1.9 collective-permute-start.20
  19.0 6.3 %collective-permute-start.2 = (bf16[32,6,1,128]{3,2,1,0:T(2,128)(2,1)S(1)}, bf16[32,6,1,128]{3,2,1,0:T(2,128)(2,1)S(1)}, u32[]{:S(2)}, u32[]{:S(2)}) collective-permute-start(bf16[32,6,1,128]{3,2,1,0:T(2,128)(2,1)S(1)} %get-tuple-element.26), channel_id=1, source_target_pairs={{0,1},{1,2},{2,3},{3,4},{4,5},{5,6},{6,7},{7,8},{8,9},{9,10},{10,1... | collective-permute-start | bytes 147464 | tf_op jit(solution)/shard_map/ppermute | solution.py:15
  25.3 1.9 collective-permute-start.3
  27.5 6.4 %collective-permute-done.3 = bf16[32,6,1,128]{3,2,1,0:T(2,128)(2,1)S(1)} collective-permute-done((bf16[32,6,1,128]{3,2,1,0:T(2,128)(2,1)S(1)}, bf16[32,6,1,128]{3,2,1,0:T(2,128)(2,1)S(1)}, u32[]{:S(2)}, u32[]{:S(2)}) %collective-permute-start.3) | collective-permute-done | bytes 49184 | tf_op jit(solution)/shard_map/ppermute | solution.py:17
  36.0 3.2 %reshape.229 = bf16[32,6,6,1,8,17]{5,4,2,1,0,3:T(8,128)(2,1)S(1)} reshape(bf16[32,6,6,1,136]{4,2,1,0,3:T(8,128)(2,1)} %pad.45) | data formatting | bytes 626688 | tf_op jit(solution)/shard_map/conv_general_dilated | solution.py:26
  39.2 3.9 %copy.280 = bf16[32,6,6,1,8,17]{0,4,5,2,1,3:T(8,128)(2,1)} copy(bf16[32,6,6,1,8,17]{5,4,2,1,0,3:T(8,128)(2,1)S(1)} %reshape.229) | data formatting | bytes 626688 | tf_op jit(solution)/shard_map/conv_general_dilated | solution.py:26
  44.0 3.4 %fusion.42 = f32[4,4,8,17,32]{4,2,3,1,0:T(8,128)S(1)} fusion(bf16[3,3,3,32,32]{4,3,2,1,0:T(8,128)(2,1)S(1)} %copy-done.8, bf16[32,6,6,1,7,2]{0,4,5,2,1,3:T(8,128)(2,1)S(1)} %slice.152, bf16[32,6,6,1,8,17]{0,4,5,2,1,3:T(8,128)(2,1)} %copy.280, pred[8,17]{0,1:T(8,128)(4,1)S(1)} %copy-done.12), kind=kOutput, calls=%fused_computation.37 | convolution fusion | flops 121444352 | bytes 679560 | tf_op jit(solution)/shard_map/conv_general_dilated | solution.py:26
  48.7 2.1 collective-permute-start.4
  50.7 6.7 %collective-permute-start.5 = (bf16[32,1,2,64]{3,0,2,1:T(8,128)(2,1)S(1)}, bf16[32,1,2,64]{3,0,2,1:T(8,128)(2,1)S(1)}, u32[]{:S(2)}, u32[]{:S(2)}) collective-permute-start(bf16[32,1,2,64]{3,0,2,1:T(8,128)(2,1)S(1)} %get-tuple-element.53), channel_id=1, source_target_pairs={{16,0},{32,16},{48,32},{64,48},{80,64},{96,80},{112,96},{128,112},... | collective-permute-start | bytes 24584 | tf_op jit(solution)/shard_map/ppermute | solution.py:17
  58.8 1.9 collective-permute-start.6
  60.8 3.9 %collective-permute-start.7 = (bf16[32,4,1,64]{3,0,2,1:T(8,128)(2,1)S(1)}, bf16[32,4,1,64]{3,0,2,1:T(8,128)(2,1)S(1)}, u32[]{:S(2)}, u32[]{:S(2)}) collective-permute-start(bf16[32,4,1,64]{3,0,2,1:T(8,128)(2,1)S(1)} %get-tuple-element.49), channel_id=1, source_target_pairs={{1,0},{2,1},{3,2},{4,3},{5,4},{6,5},{7,6},{8,7},{9,8},{10,9},{11,1... | collective-permute-start | bytes 49160 | tf_op jit(solution)/shard_map/ppermute | solution.py:17
  64.8 3.9 %collective-permute-done.7 = bf16[32,4,1,64]{3,0,2,1:T(8,128)(2,1)S(1)} collective-permute-done((bf16[32,4,1,64]{3,0,2,1:T(8,128)(2,1)S(1)}, bf16[32,4,1,64]{3,0,2,1:T(8,128)(2,1)S(1)}, u32[]{:S(2)}, u32[]{:S(2)}) %collective-permute-start.7) | collective-permute-done | bytes 16416 | tf_op jit(solution)/shard_map/ppermute | solution.py:17
  70.6 5.5 %collective-permute-start.9 = (bf16[64,1,1,32]{0,3,2,1:T(8,128)(2,1)S(1)}, bf16[64,1,1,32]{0,3,2,1:T(8,128)(2,1)S(1)}, u32[]{:S(2)}, u32[]{:S(2)}) collective-permute-start(bf16[64,1,1,32]{0,3,2,1:T(8,128)(2,1)S(1)} %fusion.174), channel_id=1, source_target_pairs={{16,0},{32,16},{48,32},{64,48},{80,64},{96,80},{112,96},{128,112},... | collective-permute-start | bytes 12296 | tf_op jit(solution)/shard_map/ppermute | solution.py:17
  76.0 1.9 collective-permute-start.8
  80.1 3.9 %collective-permute-start.23 = (bf16[32,6,1,128]{3,2,1,0:T(2,128)(2,1)S(1)}, bf16[32,6,1,128]{3,2,1,0:T(2,128)(2,1)S(1)}, u32[]{:S(2)}, u32[]{:S(2)}) collective-permute-start(bf16[32,6,1,128]{3,2,1,0:T(2,128)(2,1)S(1)} %get-tuple-element.23), channel_id=1, source_target_pairs={{1,0},{2,1},{3,2},{4,3},{5,4},{6,5},{7,6},{8,7},{9,8},{10,9},{11,1... | collective-permute-start | bytes 147464 | tf_op jit(solution)/shard_map/ppermute | solution.py:17
  84.1 2.3 collective-permute-start.11
  86.5 5.8 %collective-permute-start.10 = (bf16[64,3,1,32]{0,3,2,1:T(8,128)(2,1)S(1)}, bf16[64,3,1,32]{0,3,2,1:T(8,128)(2,1)S(1)}, u32[]{:S(2)}, u32[]{:S(2)}) collective-permute-start(bf16[64,3,1,32]{0,3,2,1:T(8,128)(2,1)S(1)} %pad_maximum_fusion.10), channel_id=1, source_target_pairs={{0,1},{1,2},{2,3},{3,4},{4,5},{5,6},{6,7},{7,8},{8,9},{9,10},{10,1... | collective-permute-start | bytes 36872 | tf_op jit(solution)/shard_map/ppermute | solution.py:15
  93.5 3.1 %reshape.230 = bf16[32,6,6,1,8,17]{5,4,2,1,0,3:T(8,128)(2,1)} reshape(bf16[32,6,6,1,136]{4,2,1,0,3:T(8,128)(2,1)S(1)} %pad.55) | data formatting | bytes 626688 | tf_op jit(solution)/shard_map/conv_general_dilated | solution.py:26
  96.6 4.2 %copy.307 = bf16[32,6,6,1,8,17]{0,4,5,2,1,3:T(8,128)(2,1)S(1)} copy(bf16[32,6,6,1,8,17]{5,4,2,1,0,3:T(8,128)(2,1)} %reshape.230) | data formatting | bytes 626688 | tf_op jit(solution)/shard_map/conv_general_dilated | solution.py:26
  104.1 6.7 %collective-permute-start.13 = (bf16[64,1,2,64]{0,2,3,1:T(2,128)(2,1)S(1)}, bf16[64,1,2,64]{0,2,3,1:T(2,128)(2,1)S(1)}, u32[]{:S(2)}, u32[]{:S(2)}) collective-permute-start(bf16[64,1,2,64]{0,2,3,1:T(2,128)(2,1)S(1)} %get-tuple-element.47), channel_id=1, source_target_pairs={{16,0},{32,16},{48,32},{64,48},{80,64},{96,80},{112,96},{128,112},... | collective-permute-start | bytes 49160 | tf_op jit(solution)/shard_map/ppermute | solution.py:17
  110.7 2.6 %fusion.45 = bf16[4,4,8,17,32]{4,2,3,1,0:T(8,128)(2,1)S(1)} fusion(bf16[3,3,3,32,32]{4,3,2,1,0:T(8,128)(2,1)} %param.15, bf16[32,6,6,1,7,2]{0,4,5,2,1,3:T(8,128)(2,1)S(1)} %slice.175, bf16[32,6,6,1,8,17]{0,4,5,2,1,3:T(8,128)(2,1)S(1)} %copy.307, pred[8,17]{0,1:T(8,128)(4,1)S(1)} %copy-done.12), kind=kOutput, calls=%fused_computation.38 | convolution fusion | flops 121513984 | bytes 540296 | tf_op jit(solution)/shard_map/conv_general_dilated | solution.py:26
  117.1 3.9 %collective-permute-start.15 = (bf16[64,4,1,64]{0,2,3,1:T(2,128)(2,1)}, bf16[64,4,1,64]{0,2,3,1:T(2,128)(2,1)}, u32[]{:S(2)}, u32[]{:S(2)}) collective-permute-start(bf16[64,4,1,64]{0,2,3,1:T(2,128)(2,1)} %get-tuple-element.37), channel_id=1, source_target_pairs={{1,0},{2,1},{3,2},{4,3},{5,4},{6,5},{7,6},{8,7},{9,8},{10,9},{11,1... | collective-permute-start | bytes 98312 | tf_op jit(solution)/shard_map/ppermute | solution.py:17
  122.3 4.2 %collective-permute-done.15 = bf16[64,4,1,64]{0,2,3,1:T(2,128)(2,1)} collective-permute-done((bf16[64,4,1,64]{0,2,3,1:T(2,128)(2,1)}, bf16[64,4,1,64]{0,2,3,1:T(2,128)(2,1)}, u32[]{:S(2)}, u32[]{:S(2)}) %collective-permute-start.15) | collective-permute-done | bytes 32800 | tf_op jit(solution)/shard_map/ppermute | solution.py:17
  131.0 6.7 %collective-permute-start.25 = (bf16[32,1,2,64]{3,0,2,1:T(8,128)(2,1)S(1)}, bf16[32,1,2,64]{3,0,2,1:T(8,128)(2,1)S(1)}, u32[]{:S(2)}, u32[]{:S(2)}) collective-permute-start(bf16[32,1,2,64]{3,0,2,1:T(8,128)(2,1)S(1)} %get-tuple-element.51), channel_id=1, source_target_pairs={{16,0},{32,16},{48,32},{64,48},{80,64},{96,80},{112,96},{128,112},... | collective-permute-start | bytes 24584 | tf_op jit(solution)/shard_map/ppermute | solution.py:17
  139.1 1.9 collective-permute-start.26
  141.0 3.9 %collective-permute-start.27 = (bf16[32,4,1,64]{3,0,2,1:T(8,128)(2,1)S(1)}, bf16[32,4,1,64]{3,0,2,1:T(8,128)(2,1)S(1)}, u32[]{:S(2)}, u32[]{:S(2)}) collective-permute-start(bf16[32,4,1,64]{3,0,2,1:T(8,128)(2,1)S(1)} %get-tuple-element.43), channel_id=1, source_target_pairs={{1,0},{2,1},{3,2},{4,3},{5,4},{6,5},{7,6},{8,7},{9,8},{10,9},{11,1... | collective-permute-start | bytes 49160 | tf_op jit(solution)/shard_map/ppermute | solution.py:17
  145.0 4.0 %collective-permute-done.27 = bf16[32,4,1,64]{3,0,2,1:T(8,128)(2,1)S(1)} collective-permute-done((bf16[32,4,1,64]{3,0,2,1:T(8,128)(2,1)S(1)}, bf16[32,4,1,64]{3,0,2,1:T(8,128)(2,1)S(1)}, u32[]{:S(2)}, u32[]{:S(2)}) %collective-permute-start.27) | collective-permute-done | bytes 16416 | tf_op jit(solution)/shard_map/ppermute | solution.py:17
  150.8 5.5 %collective-permute-start.29 = (bf16[128,1,1,32]{0,3,2,1:T(8,128)(2,1)S(1)}, bf16[128,1,1,32]{0,3,2,1:T(8,128)(2,1)S(1)}, u32[]{:S(2)}, u32[]{:S(2)}) collective-permute-start(bf16[128,1,1,32]{0,3,2,1:T(8,128)(2,1)S(1)} %fusion.60), channel_id=1, source_target_pairs={{16,0},{32,16},{48,32},{64,48},{80,64},{96,80},{112,96},{128,112},... | collective-permute-start | bytes 24584 | tf_op jit(solution)/shard_map/ppermute | solution.py:17
  156.3 1.9 collective-permute-start.28
  158.2 6.0 %collective-permute-done.28 = bf16[128,1,1,32]{0,3,2,1:T(8,128)(2,1)S(1)} collective-permute-done((bf16[128,1,1,32]{0,3,2,1:T(8,128)(2,1)S(1)}, bf16[128,1,1,32]{0,3,2,1:T(8,128)(2,1)S(1)}, u32[]{:S(2)}, u32[]{:S(2)}) %collective-permute-start.28) | collective-permute-done | bytes 8224 | tf_op jit(solution)/shard_map/ppermute | solution.py:15
  166.2 6.0 %collective-permute-start.30 = (bf16[128,3,1,32]{0,3,2,1:T(8,128)(2,1)S(1)}, bf16[128,3,1,32]{0,3,2,1:T(8,128)(2,1)S(1)}, u32[]{:S(2)}, u32[]{:S(2)}) collective-permute-start(bf16[128,3,1,32]{0,3,2,1:T(8,128)(2,1)S(1)} %pad_maximum_fusion.11), channel_id=1, source_target_pairs={{0,1},{1,2},{2,3},{3,4},{4,5},{5,6},{6,7},{7,8},{8,9},{9,10},{10,1... | collective-permute-start | bytes 73736 | tf_op jit(solution)/shard_map/ppermute | solution.py:15
  176.4 6.7 %collective-permute-start.33 = (bf16[64,1,2,64]{0,2,3,1:T(2,128)(2,1)S(1)}, bf16[64,1,2,64]{0,2,3,1:T(2,128)(2,1)S(1)}, u32[]{:S(2)}, u32[]{:S(2)}) collective-permute-start(bf16[64,1,2,64]{0,2,3,1:T(2,128)(2,1)S(1)} %get-tuple-element.41), channel_id=1, source_target_pairs={{16,0},{32,16},{48,32},{64,48},{80,64},{96,80},{112,96},{128,112},... | collective-permute-start | bytes 49160 | tf_op jit(solution)/shard_map/ppermute | solution.py:17
  185.0 6.3 %collective-permute-start.34 = (bf16[64,4,1,64]{0,2,3,1:T(2,128)(2,1)S(1)}, bf16[64,4,1,64]{0,2,3,1:T(2,128)(2,1)S(1)}, u32[]{:S(2)}, u32[]{:S(2)}) collective-permute-start(bf16[64,4,1,64]{0,2,3,1:T(2,128)(2,1)S(1)} %get-tuple-element.30), channel_id=1, source_target_pairs={{0,1},{1,2},{2,3},{3,4},{4,5},{5,6},{6,7},{7,8},{8,9},{9,10},{10,1... | collective-permute-start | bytes 98312 | tf_op jit(solution)/shard_map/ppermute | solution.py:15
  191.4 2.1 collective-permute-start.35
  194.7 5.8 %collective-permute-done.35 = bf16[64,4,1,64]{0,2,3,1:T(2,128)(2,1)S(1)} collective-permute-done((bf16[64,4,1,64]{0,2,3,1:T(2,128)(2,1)S(1)}, bf16[64,4,1,64]{0,2,3,1:T(2,128)(2,1)S(1)}, u32[]{:S(2)}, u32[]{:S(2)}) %collective-permute-start.35) | collective-permute-done | bytes 32800 | tf_op jit(solution)/shard_map/ppermute | solution.py:17
  205.0 6.7 %collective-permute-start.37 = (bf16[32,1,4,128]{3,0,2,1:T(8,128)(2,1)S(1)}, bf16[32,1,4,128]{3,0,2,1:T(8,128)(2,1)S(1)}, u32[]{:S(2)}, u32[]{:S(2)}) collective-permute-start(bf16[32,1,4,128]{3,0,2,1:T(8,128)(2,1)S(1)} %get-tuple-element.29), channel_id=1, source_target_pairs={{16,0},{32,16},{48,32},{64,48},{80,64},{96,80},{112,96},{128,112},... | collective-permute-start | bytes 98312 | tf_op jit(solution)/shard_map/ppermute | solution.py:17
  213.6 6.7 %collective-permute-start.17 = (bf16[32,1,4,128]{3,0,2,1:T(8,128)(2,1)S(1)}, bf16[32,1,4,128]{3,0,2,1:T(8,128)(2,1)S(1)}, u32[]{:S(2)}, u32[]{:S(2)}) collective-permute-start(bf16[32,1,4,128]{3,0,2,1:T(8,128)(2,1)S(1)} %get-tuple-element.35), channel_id=1, source_target_pairs={{16,0},{32,16},{48,32},{64,48},{80,64},{96,80},{112,96},{128,112},... | collective-permute-start | bytes 98312 | tf_op jit(solution)/shard_map/ppermute | solution.py:17
  222.2 3.9 %collective-permute-start.39 = (bf16[32,6,1,128]{3,0,2,1:T(8,128)(2,1)S(1)}, bf16[32,6,1,128]{3,0,2,1:T(8,128)(2,1)S(1)}, u32[]{:S(2)}, u32[]{:S(2)}) collective-permute-start(bf16[32,6,1,128]{3,0,2,1:T(8,128)(2,1)S(1)} %get-tuple-element.21), channel_id=1, source_target_pairs={{1,0},{2,1},{3,2},{4,3},{5,4},{6,5},{7,6},{8,7},{9,8},{10,9},{11,1... | collective-permute-start | bytes 147464 | tf_op jit(solution)/shard_map/ppermute | solution.py:17
  226.2 4.0 %collective-permute-start.18 = (bf16[32,6,1,128]{3,0,2,1:T(8,128)(2,1)S(1)}, bf16[32,6,1,128]{3,0,2,1:T(8,128)(2,1)S(1)}, u32[]{:S(2)}, u32[]{:S(2)}) collective-permute-start(bf16[32,6,1,128]{3,0,2,1:T(8,128)(2,1)S(1)} %get-tuple-element.24), channel_id=1, source_target_pairs={{0,1},{1,2},{2,3},{3,4},{4,5},{5,6},{6,7},{7,8},{8,9},{9,10},{10,1... | collective-permute-start | bytes 147464 | tf_op jit(solution)/shard_map/ppermute | solution.py:15
  232.7 5.7 %collective-permute-done.19 = bf16[32,6,1,128]{3,0,2,1:T(8,128)(2,1)S(1)} collective-permute-done((bf16[32,6,1,128]{3,0,2,1:T(8,128)(2,1)S(1)}, bf16[32,6,1,128]{3,0,2,1:T(8,128)(2,1)S(1)}, u32[]{:S(2)}, u32[]{:S(2)}) %collective-permute-start.19) | collective-permute-done | bytes 49184 | tf_op jit(solution)/shard_map/ppermute | solution.py:17
  239.6 3.0 %reshape.132 = bf16[32,6,6,1,8,17]{5,4,0,2,1,3:T(8,128)(2,1)S(1)} reshape(bf16[32,6,6,1,136]{4,0,2,1,3:T(8,128)(2,1)} %pad.53) | data formatting | bytes 626688 | tf_op jit(solution)/shard_map/conv_general_dilated | solution.py:26
  242.7 3.0 %copy.303 = bf16[32,6,6,1,8,17]{0,4,5,2,1,3:T(8,128)(2,1)} copy(bf16[32,6,6,1,8,17]{5,4,0,2,1,3:T(8,128)(2,1)S(1)} %reshape.132) | data formatting | bytes 626688 | tf_op jit(solution)/shard_map/conv_general_dilated | solution.py:26
  246.6 3.4 %fusion.48 = bf16[4,4,8,17,32]{4,2,3,1,0:T(8,128)(2,1)S(1)} fusion(bf16[3,3,3,32,32]{4,3,2,1,0:T(8,128)(2,1)} %param.15, bf16[32,6,6,1,7,2]{0,4,5,2,1,3:T(8,128)(2,1)S(1)} %slice.171, bf16[32,6,6,1,8,17]{0,4,5,2,1,3:T(8,128)(2,1)} %copy.303, pred[8,17]{0,1:T(8,128)(4,1)S(1)} %copy-done.12), kind=kOutput, calls=%fused_computation.39 | convolution fusion | flops 121513984 | bytes 540296 | tf_op jit(solution)/shard_map/conv_general_dilated | solution.py:26
  253.1 3.0 %copy.327 = bf16[32,6,6,1,8,17]{0,4,5,2,1,3:T(8,128)(2,1)} copy(bf16[32,6,6,1,8,17]{5,4,0,2,1,3:T(8,128)(2,1)S(1)} %reshape.169) | data formatting | bytes 626688 | tf_op jit(solution)/shard_map/conv_general_dilated | solution.py:26
  257.1 3.0 %fusion.51 = bf16[4,4,8,17,32]{4,2,3,1,0:T(8,128)(2,1)S(1)} fusion(bf16[3,3,3,32,32]{4,3,2,1,0:T(8,128)(2,1)S(1)} %copy-done.9, bf16[32,6,6,1,7,2]{0,4,5,2,1,3:T(8,128)(2,1)S(1)} %slice.194, bf16[32,6,6,1,8,17]{0,4,5,2,1,3:T(8,128)(2,1)} %copy.327, pred[8,17]{0,1:T(8,128)(4,1)S(1)} %copy-done.12), kind=kOutput, calls=%fused_computation.40 | convolution fusion | flops 121513984 | bytes 540296 | tf_op jit(solution)/shard_map/conv_general_dilated | solution.py:26
  (207 shorter events, 56.8 us)
Async XLA Ops:
  0.6 100.5 %copy-start = (bf16[3,3,3,64,128]{4,3,2,1,0:T(8,128)(2,1)S(1)}, bf16[3,3,3,64,128]{4,3,2,1,0:T(8,128)(2,1)}, u32[]{:S(2)}) copy-start(bf16[3,3,3,64,128]{4,3,2,1,0:T(8,128)(2,1)} %param.12) | copy-start | bytes 1327108
  1.5 17.3 %collective-permute-start.1 = (bf16[32,1,4,128]{3,2,1,0:T(4,128)(2,1)S(1)}, bf16[32,1,4,128]{3,2,1,0:T(4,128)(2,1)S(1)}, u32[]{:S(2)}, u32[]{:S(2)}) collective-permute-start(bf16[32,1,4,128]{3,2,1,0:T(4,128)(2,1)S(1)} %get-tuple-element.38), channel_id=1, source_target_pairs={{16,0},{32,16},{48,32},{64,48},{80,64},{96,80},{112,96},{128,112},... | collective-permute-start | bytes 98312 | tf_op jit(solution)/shard_map/ppermute | solution.py:17
  6.5 11.3 %collective-permute-start = (bf16[32,1,4,128]{3,2,1,0:T(4,128)(2,1)S(1)}, bf16[32,1,4,128]{3,2,1,0:T(4,128)(2,1)S(1)}, u32[]{:S(2)}, u32[]{:S(2)}) collective-permute-start(bf16[32,1,4,128]{3,2,1,0:T(4,128)(2,1)S(1)} %get-tuple-element.39), channel_id=1, source_target_pairs={{0,16},{16,32},{32,48},{48,64},{64,80},{80,96},{96,112},{112,128},... | collective-permute-start | bytes 98312 | tf_op jit(solution)/shard_map/ppermute | solution.py:15
  9.2 55.5 %collective-permute-start.21 = (bf16[32,1,4,128]{3,2,1,0:T(4,128)(2,1)S(1)}, bf16[32,1,4,128]{3,2,1,0:T(4,128)(2,1)S(1)}, u32[]{:S(2)}, u32[]{:S(2)}) collective-permute-start(bf16[32,1,4,128]{3,2,1,0:T(4,128)(2,1)S(1)} %get-tuple-element.32), channel_id=1, source_target_pairs={{16,0},{32,16},{48,32},{64,48},{80,64},{96,80},{112,96},{128,112},... | collective-permute-start | bytes 98312 | tf_op jit(solution)/shard_map/ppermute | solution.py:17
  15.9 11.3 %collective-permute-start.20 = (bf16[32,1,4,128]{3,2,1,0:T(4,128)(2,1)S(1)}, bf16[32,1,4,128]{3,2,1,0:T(4,128)(2,1)S(1)}, u32[]{:S(2)}, u32[]{:S(2)}) collective-permute-start(bf16[32,1,4,128]{3,2,1,0:T(4,128)(2,1)S(1)} %get-tuple-element.33), channel_id=1, source_target_pairs={{0,16},{16,32},{32,48},{48,64},{64,80},{80,96},{96,112},{112,128},... | collective-permute-start | bytes 98312 | tf_op jit(solution)/shard_map/ppermute | solution.py:15
  19.0 8.5 %collective-permute-start.2 = (bf16[32,6,1,128]{3,2,1,0:T(2,128)(2,1)S(1)}, bf16[32,6,1,128]{3,2,1,0:T(2,128)(2,1)S(1)}, u32[]{:S(2)}, u32[]{:S(2)}) collective-permute-start(bf16[32,6,1,128]{3,2,1,0:T(2,128)(2,1)S(1)} %get-tuple-element.26), channel_id=1, source_target_pairs={{0,1},{1,2},{2,3},{3,4},{4,5},{5,6},{6,7},{7,8},{8,9},{9,10},{10,1... | collective-permute-start | bytes 147464 | tf_op jit(solution)/shard_map/ppermute | solution.py:15
  25.3 8.6 %collective-permute-start.3 = (bf16[32,6,1,128]{3,2,1,0:T(2,128)(2,1)S(1)}, bf16[32,6,1,128]{3,2,1,0:T(2,128)(2,1)S(1)}, u32[]{:S(2)}, u32[]{:S(2)}) collective-permute-start(bf16[32,6,1,128]{3,2,1,0:T(2,128)(2,1)S(1)} %get-tuple-element.27), channel_id=1, source_target_pairs={{1,0},{2,1},{3,2},{4,3},{5,4},{6,5},{7,6},{8,7},{9,8},{10,9},{11,1... | collective-permute-start | bytes 147464 | tf_op jit(solution)/shard_map/ppermute | solution.py:17
  48.0 9.4 %copy-start.1 = (bf16[32,4,4,128]{3,2,1,0:T(4,128)(2,1)S(1)}, bf16[32,4,4,128]{3,2,1,0:T(4,128)(2,1)}, u32[]{:S(2)}) copy-start(bf16[32,4,4,128]{3,2,1,0:T(4,128)(2,1)} %param.9) | copy-start | bytes 393220
  48.6 20.7 %copy-start.6 = (bf16[3,3,3,32,64]{4,3,2,1,0:T(8,128)(2,1)S(1)}, bf16[3,3,3,32,64]{4,3,2,1,0:T(8,128)(2,1)}, u32[]{:S(2)}) copy-start(bf16[3,3,3,32,64]{4,3,2,1,0:T(8,128)(2,1)} %param.11) | copy-start | bytes 331780
  48.6 20.7 %copy-start.13 = (pred[8,9]{0,1:T(8,128)(4,1)S(1)}, pred[8,9]{0,1:T(8,128)(4,1)}, u32[]{:S(2)}) copy-start(pred[8,9]{0,1:T(8,128)(4,1)} %constant.82) | copy-start | bytes 220
  48.7 8.8 %collective-permute-start.4 = (bf16[32,1,2,64]{3,0,2,1:T(8,128)(2,1)S(1)}, bf16[32,1,2,64]{3,0,2,1:T(8,128)(2,1)S(1)}, u32[]{:S(2)}, u32[]{:S(2)}) collective-permute-start(bf16[32,1,2,64]{3,0,2,1:T(8,128)(2,1)S(1)} %get-tuple-element.52), channel_id=1, source_target_pairs={{0,16},{16,32},{32,48},{48,64},{64,80},{80,96},{96,112},{112,128},... | collective-permute-start | bytes 24584 | tf_op jit(solution)/shard_map/ppermute | solution.py:15
  50.7 8.1 %collective-permute-start.5 = (bf16[32,1,2,64]{3,0,2,1:T(8,128)(2,1)S(1)}, bf16[32,1,2,64]{3,0,2,1:T(8,128)(2,1)S(1)}, u32[]{:S(2)}, u32[]{:S(2)}) collective-permute-start(bf16[32,1,2,64]{3,0,2,1:T(8,128)(2,1)S(1)} %get-tuple-element.53), channel_id=1, source_target_pairs={{16,0},{32,16},{48,32},{64,48},{80,64},{96,80},{112,96},{128,112},... | collective-permute-start | bytes 24584 | tf_op jit(solution)/shard_map/ppermute | solution.py:17
  58.8 5.9 %collective-permute-start.6 = (bf16[32,4,1,64]{3,0,2,1:T(8,128)(2,1)S(1)}, bf16[32,4,1,64]{3,0,2,1:T(8,128)(2,1)S(1)}, u32[]{:S(2)}, u32[]{:S(2)}) collective-permute-start(bf16[32,4,1,64]{3,0,2,1:T(8,128)(2,1)S(1)} %get-tuple-element.48), channel_id=1, source_target_pairs={{0,1},{1,2},{2,3},{3,4},{4,5},{5,6},{6,7},{7,8},{8,9},{9,10},{10,1... | collective-permute-start | bytes 49160 | tf_op jit(solution)/shard_map/ppermute | solution.py:15
  60.8 7.9 %collective-permute-start.7 = (bf16[32,4,1,64]{3,0,2,1:T(8,128)(2,1)S(1)}, bf16[32,4,1,64]{3,0,2,1:T(8,128)(2,1)S(1)}, u32[]{:S(2)}, u32[]{:S(2)}) collective-permute-start(bf16[32,4,1,64]{3,0,2,1:T(8,128)(2,1)S(1)} %get-tuple-element.49), channel_id=1, source_target_pairs={{1,0},{2,1},{3,2},{4,3},{5,4},{6,5},{7,6},{8,7},{9,8},{10,9},{11,1... | collective-permute-start | bytes 49160 | tf_op jit(solution)/shard_map/ppermute | solution.py:17
  70.6 13.4 %collective-permute-start.9 = (bf16[64,1,1,32]{0,3,2,1:T(8,128)(2,1)S(1)}, bf16[64,1,1,32]{0,3,2,1:T(8,128)(2,1)S(1)}, u32[]{:S(2)}, u32[]{:S(2)}) collective-permute-start(bf16[64,1,1,32]{0,3,2,1:T(8,128)(2,1)S(1)} %fusion.174), channel_id=1, source_target_pairs={{16,0},{32,16},{48,32},{64,48},{80,64},{96,80},{112,96},{128,112},... | collective-permute-start | bytes 12296 | tf_op jit(solution)/shard_map/ppermute | solution.py:17
  76.0 8.1 %collective-permute-start.8 = (bf16[64,1,1,32]{0,3,2,1:T(8,128)(2,1)S(1)}, bf16[64,1,1,32]{0,3,2,1:T(8,128)(2,1)S(1)}, u32[]{:S(2)}, u32[]{:S(2)}) collective-permute-start(bf16[64,1,1,32]{0,3,2,1:T(8,128)(2,1)S(1)} %fusion.174), channel_id=1, source_target_pairs={{0,16},{16,32},{32,48},{48,64},{64,80},{80,96},{96,112},{112,128},... | collective-permute-start | bytes 12296 | tf_op jit(solution)/shard_map/ppermute | solution.py:15
  78.1 14.2 %collective-permute-start.22 = (bf16[32,6,1,128]{3,2,1,0:T(2,128)(2,1)S(1)}, bf16[32,6,1,128]{3,2,1,0:T(2,128)(2,1)S(1)}, u32[]{:S(2)}, u32[]{:S(2)}) collective-permute-start(bf16[32,6,1,128]{3,2,1,0:T(2,128)(2,1)S(1)} %get-tuple-element.22), channel_id=1, source_target_pairs={{0,1},{1,2},{2,3},{3,4},{4,5},{5,6},{6,7},{7,8},{8,9},{9,10},{10,1... | collective-permute-start | bytes 147464 | tf_op jit(solution)/shard_map/ppermute | solution.py:15
  80.1 12.3 %collective-permute-start.23 = (bf16[32,6,1,128]{3,2,1,0:T(2,128)(2,1)S(1)}, bf16[32,6,1,128]{3,2,1,0:T(2,128)(2,1)S(1)}, u32[]{:S(2)}, u32[]{:S(2)}) collective-permute-start(bf16[32,6,1,128]{3,2,1,0:T(2,128)(2,1)S(1)} %get-tuple-element.23), channel_id=1, source_target_pairs={{1,0},{2,1},{3,2},{4,3},{5,4},{6,5},{7,6},{8,7},{9,8},{10,9},{11,1... | collective-permute-start | bytes 147464 | tf_op jit(solution)/shard_map/ppermute | solution.py:17
  84.1 16.8 %collective-permute-start.11 = (bf16[64,3,1,32]{0,3,2,1:T(8,128)(2,1)S(1)}, bf16[64,3,1,32]{0,3,2,1:T(8,128)(2,1)S(1)}, u32[]{:S(2)}, u32[]{:S(2)}) collective-permute-start(bf16[64,3,1,32]{0,3,2,1:T(8,128)(2,1)S(1)} %pad_maximum_fusion.10), channel_id=1, source_target_pairs={{1,0},{2,1},{3,2},{4,3},{5,4},{6,5},{7,6},{8,7},{9,8},{10,9},{11,1... | collective-permute-start | bytes 36872 | tf_op jit(solution)/shard_map/ppermute | solution.py:17
  86.5 14.5 %collective-permute-start.10 = (bf16[64,3,1,32]{0,3,2,1:T(8,128)(2,1)S(1)}, bf16[64,3,1,32]{0,3,2,1:T(8,128)(2,1)S(1)}, u32[]{:S(2)}, u32[]{:S(2)}) collective-permute-start(bf16[64,3,1,32]{0,3,2,1:T(8,128)(2,1)S(1)} %pad_maximum_fusion.10), channel_id=1, source_target_pairs={{0,1},{1,2},{2,3},{3,4},{4,5},{5,6},{6,7},{7,8},{8,9},{9,10},{10,1... | collective-permute-start | bytes 36872 | tf_op jit(solution)/shard_map/ppermute | solution.py:15
  102.1 11.9 %collective-permute-start.12 = (bf16[64,1,2,64]{0,2,3,1:T(2,128)(2,1)S(1)}, bf16[64,1,2,64]{0,2,3,1:T(2,128)(2,1)S(1)}, u32[]{:S(2)}, u32[]{:S(2)}) collective-permute-start(bf16[64,1,2,64]{0,2,3,1:T(2,128)(2,1)S(1)} %get-tuple-element.46), channel_id=1, source_target_pairs={{0,16},{16,32},{32,48},{48,64},{64,80},{80,96},{96,112},{112,128},... | collective-permute-start | bytes 49160 | tf_op jit(solution)/shard_map/ppermute | solution.py:15
  104.1 10.0 %collective-permute-start.13 = (bf16[64,1,2,64]{0,2,3,1:T(2,128)(2,1)S(1)}, bf16[64,1,2,64]{0,2,3,1:T(2,128)(2,1)S(1)}, u32[]{:S(2)}, u32[]{:S(2)}) collective-permute-start(bf16[64,1,2,64]{0,2,3,1:T(2,128)(2,1)S(1)} %get-tuple-element.47), channel_id=1, source_target_pairs={{16,0},{32,16},{48,32},{64,48},{80,64},{96,80},{112,96},{128,112},... | collective-permute-start | bytes 49160 | tf_op jit(solution)/shard_map/ppermute | solution.py:17
  115.2 7.1 %collective-permute-start.14 = (bf16[64,4,1,64]{0,2,3,1:T(2,128)(2,1)}, bf16[64,4,1,64]{0,2,3,1:T(2,128)(2,1)S(1)}, u32[]{:S(2)}, u32[]{:S(2)}) collective-permute-start(bf16[64,4,1,64]{0,2,3,1:T(2,128)(2,1)} %get-tuple-element.36), channel_id=1, source_target_pairs={{0,1},{1,2},{2,3},{3,4},{4,5},{5,6},{6,7},{7,8},{8,9},{9,10},{10,1... | collective-permute-start | bytes 98312 | tf_op jit(solution)/shard_map/ppermute | solution.py:15
  117.1 9.3 %collective-permute-start.15 = (bf16[64,4,1,64]{0,2,3,1:T(2,128)(2,1)}, bf16[64,4,1,64]{0,2,3,1:T(2,128)(2,1)}, u32[]{:S(2)}, u32[]{:S(2)}) collective-permute-start(bf16[64,4,1,64]{0,2,3,1:T(2,128)(2,1)} %get-tuple-element.37), channel_id=1, source_target_pairs={{1,0},{2,1},{3,2},{4,3},{5,4},{6,5},{7,6},{8,7},{9,8},{10,9},{11,1... | collective-permute-start | bytes 98312 | tf_op jit(solution)/shard_map/ppermute | solution.py:17
  121.4 6.7 %copy-start.14 = (pred[8,9]{0,1:T(8,128)(4,1)S(1)}, pred[8,9]{0,1:T(8,128)(4,1)}, u32[]{:S(2)}) copy-start(pred[8,9]{0,1:T(8,128)(4,1)} %constant.82) | copy-start | bytes 220
  128.9 20.7 %copy-start.5 = (bf16[3,3,3,64,32]{3,4,2,1,0:T(8,128)(2,1)S(1)}, bf16[3,3,3,64,32]{3,4,2,1,0:T(8,128)(2,1)}, u32[]{:S(2)}) copy-start(bf16[3,3,3,64,32]{3,4,2,1,0:T(8,128)(2,1)} %param.14) | copy-start | bytes 331780
  129.1 8.6 %collective-permute-start.24 = (bf16[32,1,2,64]{3,0,2,1:T(8,128)(2,1)S(1)}, bf16[32,1,2,64]{3,0,2,1:T(8,128)(2,1)S(1)}, u32[]{:S(2)}, u32[]{:S(2)}) collective-permute-start(bf16[32,1,2,64]{3,0,2,1:T(8,128)(2,1)S(1)} %get-tuple-element.50), channel_id=1, source_target_pairs={{0,16},{16,32},{32,48},{48,64},{64,80},{80,96},{96,112},{112,128},... | collective-permute-start | bytes 24584 | tf_op jit(solution)/shard_map/ppermute | solution.py:15
  131.0 8.1 %collective-permute-start.25 = (bf16[32,1,2,64]{3,0,2,1:T(8,128)(2,1)S(1)}, bf16[32,1,2,64]{3,0,2,1:T(8,128)(2,1)S(1)}, u32[]{:S(2)}, u32[]{:S(2)}) collective-permute-start(bf16[32,1,2,64]{3,0,2,1:T(8,128)(2,1)S(1)} %get-tuple-element.51), channel_id=1, source_target_pairs={{16,0},{32,16},{48,32},{64,48},{80,64},{96,80},{112,96},{128,112},... | collective-permute-start | bytes 24584 | tf_op jit(solution)/shard_map/ppermute | solution.py:17
  139.1 5.9 %collective-permute-start.26 = (bf16[32,4,1,64]{3,0,2,1:T(8,128)(2,1)S(1)}, bf16[32,4,1,64]{3,0,2,1:T(8,128)(2,1)S(1)}, u32[]{:S(2)}, u32[]{:S(2)}) collective-permute-start(bf16[32,4,1,64]{3,0,2,1:T(8,128)(2,1)S(1)} %get-tuple-element.42), channel_id=1, source_target_pairs={{0,1},{1,2},{2,3},{3,4},{4,5},{5,6},{6,7},{7,8},{8,9},{9,10},{10,1... | collective-permute-start | bytes 49160 | tf_op jit(solution)/shard_map/ppermute | solution.py:15
  141.0 7.9 %collective-permute-start.27 = (bf16[32,4,1,64]{3,0,2,1:T(8,128)(2,1)S(1)}, bf16[32,4,1,64]{3,0,2,1:T(8,128)(2,1)S(1)}, u32[]{:S(2)}, u32[]{:S(2)}) collective-permute-start(bf16[32,4,1,64]{3,0,2,1:T(8,128)(2,1)S(1)} %get-tuple-element.43), channel_id=1, source_target_pairs={{1,0},{2,1},{3,2},{4,3},{5,4},{6,5},{7,6},{8,7},{9,8},{10,9},{11,1... | collective-permute-start | bytes 49160 | tf_op jit(solution)/shard_map/ppermute | solution.py:17
  149.6 24.3 %copy-start.16 = (pred[8,5]{0,1:T(8,128)(4,1)S(1)}, pred[8,5]{0,1:T(8,128)(4,1)}, u32[]{:S(2)}) copy-start(pred[8,5]{0,1:T(8,128)(4,1)} %constant.83) | copy-start | bytes 124
  150.8 7.4 %collective-permute-start.29 = (bf16[128,1,1,32]{0,3,2,1:T(8,128)(2,1)S(1)}, bf16[128,1,1,32]{0,3,2,1:T(8,128)(2,1)S(1)}, u32[]{:S(2)}, u32[]{:S(2)}) collective-permute-start(bf16[128,1,1,32]{0,3,2,1:T(8,128)(2,1)S(1)} %fusion.60), channel_id=1, source_target_pairs={{16,0},{32,16},{48,32},{64,48},{80,64},{96,80},{112,96},{128,112},... | collective-permute-start | bytes 24584 | tf_op jit(solution)/shard_map/ppermute | solution.py:17
  156.3 8.0 %collective-permute-start.28 = (bf16[128,1,1,32]{0,3,2,1:T(8,128)(2,1)S(1)}, bf16[128,1,1,32]{0,3,2,1:T(8,128)(2,1)S(1)}, u32[]{:S(2)}, u32[]{:S(2)}) collective-permute-start(bf16[128,1,1,32]{0,3,2,1:T(8,128)(2,1)S(1)} %fusion.60), channel_id=1, source_target_pairs={{0,16},{16,32},{32,48},{48,64},{64,80},{80,96},{96,112},{112,128},... | collective-permute-start | bytes 24584 | tf_op jit(solution)/shard_map/ppermute | solution.py:15
  164.3 8.0 %collective-permute-start.31 = (bf16[128,3,1,32]{0,3,2,1:T(8,128)(2,1)S(1)}, bf16[128,3,1,32]{0,3,2,1:T(8,128)(2,1)S(1)}, u32[]{:S(2)}, u32[]{:S(2)}) collective-permute-start(bf16[128,3,1,32]{0,3,2,1:T(8,128)(2,1)S(1)} %pad_maximum_fusion.11), channel_id=1, source_target_pairs={{1,0},{2,1},{3,2},{4,3},{5,4},{6,5},{7,6},{8,7},{9,8},{10,9},{11,1... | collective-permute-start | bytes 73736 | tf_op jit(solution)/shard_map/ppermute | solution.py:17
  166.2 7.5 %collective-permute-start.30 = (bf16[128,3,1,32]{0,3,2,1:T(8,128)(2,1)S(1)}, bf16[128,3,1,32]{0,3,2,1:T(8,128)(2,1)S(1)}, u32[]{:S(2)}, u32[]{:S(2)}) collective-permute-start(bf16[128,3,1,32]{0,3,2,1:T(8,128)(2,1)S(1)} %pad_maximum_fusion.11), channel_id=1, source_target_pairs={{0,1},{1,2},{2,3},{3,4},{4,5},{5,6},{6,7},{7,8},{8,9},{9,10},{10,1... | collective-permute-start | bytes 73736 | tf_op jit(solution)/shard_map/ppermute | solution.py:15
  174.4 8.6 %collective-permute-start.32 = (bf16[64,1,2,64]{0,2,3,1:T(2,128)(2,1)S(1)}, bf16[64,1,2,64]{0,2,3,1:T(2,128)(2,1)S(1)}, u32[]{:S(2)}, u32[]{:S(2)}) collective-permute-start(bf16[64,1,2,64]{0,2,3,1:T(2,128)(2,1)S(1)} %get-tuple-element.40), channel_id=1, source_target_pairs={{0,16},{16,32},{32,48},{48,64},{64,80},{80,96},{96,112},{112,128},... | collective-permute-start | bytes 49160 | tf_op jit(solution)/shard_map/ppermute | solution.py:15
  176.4 8.2 %collective-permute-start.33 = (bf16[64,1,2,64]{0,2,3,1:T(2,128)(2,1)S(1)}, bf16[64,1,2,64]{0,2,3,1:T(2,128)(2,1)S(1)}, u32[]{:S(2)}, u32[]{:S(2)}) collective-permute-start(bf16[64,1,2,64]{0,2,3,1:T(2,128)(2,1)S(1)} %get-tuple-element.41), channel_id=1, source_target_pairs={{16,0},{32,16},{48,32},{64,48},{80,64},{96,80},{112,96},{128,112},... | collective-permute-start | bytes 49160 | tf_op jit(solution)/shard_map/ppermute | solution.py:17
  185.0 9.7 %collective-permute-start.34 = (bf16[64,4,1,64]{0,2,3,1:T(2,128)(2,1)S(1)}, bf16[64,4,1,64]{0,2,3,1:T(2,128)(2,1)S(1)}, u32[]{:S(2)}, u32[]{:S(2)}) collective-permute-start(bf16[64,4,1,64]{0,2,3,1:T(2,128)(2,1)S(1)} %get-tuple-element.30), channel_id=1, source_target_pairs={{0,1},{1,2},{2,3},{3,4},{4,5},{5,6},{6,7},{7,8},{8,9},{9,10},{10,1... | collective-permute-start | bytes 98312 | tf_op jit(solution)/shard_map/ppermute | solution.py:15
  191.4 9.2 %collective-permute-start.35 = (bf16[64,4,1,64]{0,2,3,1:T(2,128)(2,1)S(1)}, bf16[64,4,1,64]{0,2,3,1:T(2,128)(2,1)S(1)}, u32[]{:S(2)}, u32[]{:S(2)}) collective-permute-start(bf16[64,4,1,64]{0,2,3,1:T(2,128)(2,1)S(1)} %get-tuple-element.31), channel_id=1, source_target_pairs={{1,0},{2,1},{3,2},{4,3},{5,4},{6,5},{7,6},{8,7},{9,8},{10,9},{11,1... | collective-permute-start | bytes 98312 | tf_op jit(solution)/shard_map/ppermute | solution.py:17
  194.4 7.0 %copy-start.7 = (bf16[3,3,3,32,64]{4,3,2,1,0:T(8,128)(2,1)S(1)}, bf16[3,3,3,32,64]{4,3,2,1,0:T(8,128)(2,1)}, u32[]{:S(2)}) copy-start(bf16[3,3,3,32,64]{4,3,2,1,0:T(8,128)(2,1)} %param.11) | copy-start | bytes 331780
  203.1 17.2 %collective-permute-start.36 = (bf16[32,1,4,128]{3,0,2,1:T(8,128)(2,1)S(1)}, bf16[32,1,4,128]{3,0,2,1:T(8,128)(2,1)S(1)}, u32[]{:S(2)}, u32[]{:S(2)}) collective-permute-start(bf16[32,1,4,128]{3,0,2,1:T(8,128)(2,1)S(1)} %get-tuple-element.28), channel_id=1, source_target_pairs={{0,16},{16,32},{32,48},{48,64},{64,80},{80,96},{96,112},{112,128},... | collective-permute-start | bytes 98312 | tf_op jit(solution)/shard_map/ppermute | solution.py:15
  205.0 15.3 %collective-permute-start.37 = (bf16[32,1,4,128]{3,0,2,1:T(8,128)(2,1)S(1)}, bf16[32,1,4,128]{3,0,2,1:T(8,128)(2,1)S(1)}, u32[]{:S(2)}, u32[]{:S(2)}) collective-permute-start(bf16[32,1,4,128]{3,0,2,1:T(8,128)(2,1)S(1)} %get-tuple-element.29), channel_id=1, source_target_pairs={{16,0},{32,16},{48,32},{64,48},{80,64},{96,80},{112,96},{128,112},... | collective-permute-start | bytes 98312 | tf_op jit(solution)/shard_map/ppermute | solution.py:17
  211.7 14.5 %collective-permute-start.16 = (bf16[32,1,4,128]{3,0,2,1:T(8,128)(2,1)S(1)}, bf16[32,1,4,128]{3,0,2,1:T(8,128)(2,1)S(1)}, u32[]{:S(2)}, u32[]{:S(2)}) collective-permute-start(bf16[32,1,4,128]{3,0,2,1:T(8,128)(2,1)S(1)} %get-tuple-element.34), channel_id=1, source_target_pairs={{0,16},{16,32},{32,48},{48,64},{64,80},{80,96},{96,112},{112,128},... | collective-permute-start | bytes 98312 | tf_op jit(solution)/shard_map/ppermute | solution.py:15
  213.6 12.6 %collective-permute-start.17 = (bf16[32,1,4,128]{3,0,2,1:T(8,128)(2,1)S(1)}, bf16[32,1,4,128]{3,0,2,1:T(8,128)(2,1)S(1)}, u32[]{:S(2)}, u32[]{:S(2)}) collective-permute-start(bf16[32,1,4,128]{3,0,2,1:T(8,128)(2,1)S(1)} %get-tuple-element.35), channel_id=1, source_target_pairs={{16,0},{32,16},{48,32},{64,48},{80,64},{96,80},{112,96},{128,112},... | collective-permute-start | bytes 98312 | tf_op jit(solution)/shard_map/ppermute | solution.py:17
  220.3 11.9 %collective-permute-start.38 = (bf16[32,6,1,128]{3,0,2,1:T(8,128)(2,1)S(1)}, bf16[32,6,1,128]{3,0,2,1:T(8,128)(2,1)S(1)}, u32[]{:S(2)}, u32[]{:S(2)}) collective-permute-start(bf16[32,6,1,128]{3,0,2,1:T(8,128)(2,1)S(1)} %get-tuple-element.20), channel_id=1, source_target_pairs={{0,1},{1,2},{2,3},{3,4},{4,5},{5,6},{6,7},{7,8},{8,9},{9,10},{10,1... | collective-permute-start | bytes 147464 | tf_op jit(solution)/shard_map/ppermute | solution.py:15
  222.2 10.0 %collective-permute-start.39 = (bf16[32,6,1,128]{3,0,2,1:T(8,128)(2,1)S(1)}, bf16[32,6,1,128]{3,0,2,1:T(8,128)(2,1)S(1)}, u32[]{:S(2)}, u32[]{:S(2)}) collective-permute-start(bf16[32,6,1,128]{3,0,2,1:T(8,128)(2,1)S(1)} %get-tuple-element.21), channel_id=1, source_target_pairs={{1,0},{2,1},{3,2},{4,3},{5,4},{6,5},{7,6},{8,7},{9,8},{10,9},{11,1... | collective-permute-start | bytes 147464 | tf_op jit(solution)/shard_map/ppermute | solution.py:17
  226.2 6.4 %collective-permute-start.18 = (bf16[32,6,1,128]{3,0,2,1:T(8,128)(2,1)S(1)}, bf16[32,6,1,128]{3,0,2,1:T(8,128)(2,1)S(1)}, u32[]{:S(2)}, u32[]{:S(2)}) collective-permute-start(bf16[32,6,1,128]{3,0,2,1:T(8,128)(2,1)S(1)} %get-tuple-element.24), channel_id=1, source_target_pairs={{0,1},{1,2},{2,3},{3,4},{4,5},{5,6},{6,7},{7,8},{8,9},{9,10},{10,1... | collective-permute-start | bytes 147464 | tf_op jit(solution)/shard_map/ppermute | solution.py:15
  230.2 8.1 %collective-permute-start.19 = (bf16[32,6,1,128]{3,0,2,1:T(8,128)(2,1)S(1)}, bf16[32,6,1,128]{3,0,2,1:T(8,128)(2,1)S(1)}, u32[]{:S(2)}, u32[]{:S(2)}) collective-permute-start(bf16[32,6,1,128]{3,0,2,1:T(8,128)(2,1)S(1)} %get-tuple-element.25), channel_id=1, source_target_pairs={{1,0},{2,1},{3,2},{4,3},{5,4},{6,5},{7,6},{8,7},{9,8},{10,9},{11,1... | collective-permute-start | bytes 147464 | tf_op jit(solution)/shard_map/ppermute | solution.py:17
  (9 other events, 30.8 us)
where the time goes:
time: 263 us; the launch traced here: 261 us
  starting transfers between devices  150 us (57%)
  local copies, waits for them, and re-layouts  43.6 us (17%)
  waiting for transfers between devices  42.3 us (16%)
  matrix products  16.4 us (6%)
  other arithmetic  7.22 us (3%)
    ppermute x20, starting transfers between devices, extended(): lax.ppermute(head, axis, [((i + 1) % count, i) for i in range(ends)])  92.3 us
    ppermute x20, starting transfers between devices, extended(): lax.ppermute(tail, axis, [(i, (i + 1) % count) for i in range(ends)])  57.4 us
    ppermute x20, waiting for transfers between devices, extended(): lax.ppermute(head, axis, [((i + 1) % count, i) for i in range(ends)])  34.4 us
    conv_general_dilated x33, local copies, waits for them, and re-layouts, conv_valid(): lax.conv_general_dilated(padded[None], kernel, (1, 1, 1), 'VALID', dimens...  29 us
    conv_general_dilated x10, matrix products, conv_valid(): lax.conv_general_dilated(padded[None], kernel, (1, 1, 1), 'VALID', dimens...  16.1 us
    ppermute x20, waiting for transfers between devices, extended(): lax.ppermute(tail, axis, [(i, (i + 1) % count) for i in range(ends)])  7.92 us
  transfers between devices with their start and end apart: 40, of which 13 were waited for; matrix products, arithmetic and copies ran while one was open for 12% of the time, Pallas kernels for 0%

commit v1 on v0

v1 whole, which is shorter than its diff:
```python
import functools

import jax
import jax.numpy as jnp
from jax import lax
from jax.experimental import pallas as pl
from jax.experimental.pallas import tpu as pltpu
from jax.sharding import PartitionSpec as P

bf = jnp.bfloat16
f32 = jnp.float32


def forward_matrix(kernel):
    chans, outs = kernel.shape[3:]
    return kernel.transpose(2, 4, 0, 1, 3).reshape(3 * outs, 9 * chans)


def backward_matrix(kernel):
    chans, outs = kernel.shape[3:]
    return jnp.flip(kernel, (0, 1, 2)).transpose(2, 3, 0, 1, 4).reshape(3 * chans, 9 * outs)


def dot(a, b):
    return jnp.dot(a, b, preferred_element_type=f32)


def lanes(rows, cols=128):
    return lax.broadcasted_iota(jnp.int32, (rows, cols), 1)


def sigma(value):
    return 1.0 / (1.0 + jnp.exp(-value))


def silu(value):
    return value * sigma(value)


def slope(value):
    s = sigma(value)
    return s * (1.0 + value * (1.0 - s))


def zsum(prod, outs, span):
    pos = lanes(outs) & (span - 1)
    first, last = pos == 0, pos == span - 1
    tiles = []
    for start in range(0, prod.shape[1], 128):
        cut = slice(start, start + 128)
        below = pltpu.roll(prod[:outs, cut], 1, 1)
        above = pltpu.roll(prod[2 * outs :, cut], 127, 1)
        tiles.append(
            prod[outs : 2 * outs, cut]
            + jnp.where(first, 0.0, below)
            + jnp.where(last, 0.0, above)
        )
    return tiles


def rows_of(tiles):
    return jnp.concatenate(tiles, axis=0)


def cols_of(tiles):
    return jnp.concatenate(tiles, axis=1)


def flag(block, count):
    return jnp.where((block >= 0) & (block < count), 1.0, 0.0).astype(f32)


def selection(rows, cols, target):
    r = lax.broadcasted_iota(jnp.int32, (rows, cols), 0)
    c = lax.broadcasted_iota(jnp.int32, (rows, cols), 1)
    return jnp.where(target(r, c), 1.0, 0.0).astype(bf)


def pair_pool():
    return selection(1024, 128, lambda r, c: (r >> 9) * 64 + ((r & 127) >> 1) == c)


def pair_up():
    return selection(
        128, 256, lambda r, c: (r >> 6 == c >> 7) & ((r & 63) == (c & 127) >> 1)
    )


def block_up():
    return selection(
        128, 512, lambda r, c: (r >> 5 == c >> 7) & ((r & 31) == (c & 63) >> 1)
    )


def split(value):
    high = value.astype(bf)
    low = (value - high.astype(f32)).astype(bf)
    return rows_of([high, low])


def exact_up(value, matrix):
    rows = value.shape[0]
    out = dot(split(value), matrix)
    return out[:rows] + out[rows:]


def cross(left, right):
    low = lanes(left.shape[0]) < 64
    out = jnp.where(
        low, pltpu.roll(left.astype(f32), 64, 1), pltpu.roll(right.astype(f32), 64, 1)
    )
    return out.astype(left.dtype)


def neighbours(tiles, keep):
    chans = tiles[0].shape[0]
    seg = lanes(chans) >> 5
    masked = [t.astype(f32) * k for t, k in zip(tiles, keep)]
    cache = {}

    def rolled(q, amount):
        if (q, amount) not in cache:
            cache[q, amount] = (
                masked[q] if amount == 0 else pltpu.roll(masked[q], amount, 1)
            )
        return cache[q, amount]

    taps = []
    for dx in range(3):
        for dy in range(3):
            out = None
            for t in range(4):
                x, y = t // 2 + dx, t % 2 + dy
                q, s = (x // 2) * 2 + y // 2, (x % 2) * 2 + y % 2
                piece = rolled(q, (t - s) * 32 % 128)
                out = piece if out is None else jnp.where(seg == t, piece, out)
            taps.append(out.astype(bf))
    return rows_of(taps)


def quadrant_keep(chans, base_x, base_y, count_x, count_y):
    pos = lanes(chans)
    a, b = pos >> 6, (pos >> 5) & 1
    keep = []
    for q in range(4):
        x, y = base_x + 2 * (q // 2) + a, base_y + 2 * (q % 2) + b
        inside = (x >= 0) & (x < count_x) & (y >= 0) & (y < count_y)
        keep.append(jnp.where(inside, 1.0, 0.0).astype(f32))
    return keep


def place(pos_ref):
    return pos_ref[0], pos_ref[1]


def columns(field, x, y):
    return rows_of([field[x + dx, y + dy] for dx in range(3) for dy in range(3)])


def encode(
    counts, pos, vol, vol_l, vol_r, cot, cot_l, cot_r, first, second, final_b,
    hid, pre, gj, content2, p2, ev, ec, h8,
):
    w, n = place(pos)
    ev[0:3], ev[3:7], ev[7:10] = vol_l[...], vol[...], vol_r[...]
    ec[0:2], ec[2:6], ec[6:8] = cot_l[...], cot[...], cot_r[...]

    def row(x, keep):
        prod = dot(first[...], cols_of([columns(ev, x, y) for y in range(8)]))
        for y, value in enumerate(zsum(prod, 32, 128)):
            h = silu(value).astype(bf)
            h8[x, y] = h
            if keep and 1 <= y <= 6:
                hid[x - 1, y - 1] = h
                pre[x - 1, y - 1] = value

    row(0, False)
    pl.loop(1, 7)(lambda x: row(x, True))
    row(7, False)

    @pl.loop(0, 6)
    def _(x):
        prod = dot(final_b[...], cols_of([columns(ec, x, y) for y in range(6)]))
        for y, value in enumerate(zsum(prod, 32, 128)):
            gj[x, y] = value.astype(bf)

    pool = pair_pool()
    pick = lambda field, x, y: cols_of(
        [field[x + i, y + j] for j in range(2) for i in range(2)]
    )
    sums = rows_of(
        [cols_of([pick(gj, 1 + 2 * x, 1), pick(gj, 1 + 2 * x, 3)]) for x in range(2)]
    )
    content2[128:192] = dot(sums, pool).astype(bf)

    parts = rows_of(
        [
            cols_of([pick(h8, 2 * x, 2 * y), pick(h8, 2 * x, 2 * y + 2)])
            for x in range(4)
            for y in range(3)
        ]
    )
    pooled = dot(parts, pool) * 0.125
    low = lanes(32) < 64
    fx = [flag(w - 1, counts[0]), 1.0, 1.0, flag(w + 1, counts[0])]
    fl, fr = flag(n - 1, counts[1]), flag(n + 1, counts[1])
    fy = [jnp.where(low, fl, 1.0), jnp.ones((32, 128), f32), jnp.where(low, 1.0, fr)]
    tile = [
        [
            (pooled[(x * 3 + y) * 32 : (x * 3 + y + 1) * 32] * fy[y] * fx[x]).astype(bf)
            for y in range(3)
        ]
        for x in range(4)
    ]
    stack = [rows_of([tile[x + dx][y] for dx in range(3) for y in range(3)]) for x in range(2)]
    pre2 = zsum(dot(second[...], cols_of(stack)), 64, 64)
    spread = selection(256, 128, lambda r, c: (r & 63) >> 1 == (c & 31))
    hidden2 = cols_of([silu(v).astype(bf) for v in pre2])
    p2[...] = (dot(hidden2, spread) * 0.125).astype(bf)
    for x in range(2):
        content2[64 * x : 64 * x + 64] = pre2[x].astype(bf)


def bottom(counts, pos, got, weight, lift, out):
    w, n = place(pos)
    bx, by = 2 * ((w + 1) // 2) - 2, 2 * ((n + 1) // 2) - 2
    keep = quadrant_keep(64, bx, by, *counts)
    taps = neighbours([got[q, 192:256] for q in range(4)], keep)
    (pre,) = zsum(dot(weight[...], taps), 128, 32)
    lifted = dot(lift[...], silu(pre).astype(bf))
    up = exact_up(lifted, block_up())
    grad = slope(pre)
    odd = (lanes(128) >> 5) & 1 == 1
    turned = jnp.where(odd, pltpu.roll(grad, 96, 1), pltpu.roll(grad, 32, 1)).astype(bf)
    for t in range(4):
        out[t, 512:640] = turned
    for s in range(4):
        for x in range(2):
            hidden = silu(got[s, 64 * x : 64 * x + 64].astype(f32)).astype(bf)
            joined = (up[:, 128 * s : 128 * s + 128] + hidden.astype(f32)).astype(bf)
            at = (2 * s + x) * 64
            for t in range(4):
                out[t, at : at + 64] = joined
        sums = got[s, 128:192]
        for t in range(4):
            out[t, 640 + 64 * s : 704 + 64 * s] = sums


def spread_quadrants(got, start, rows, base_x, base_y, counts, store):
    for row in range(8):
        for pair in range(4):
            q, s = (row // 4) * 2 + pair // 2, ((row % 4) // 2) * 2 + pair % 2
            at = start + (2 * s + row % 2) * rows
            tile = got[q, at : at + rows]
            edge = None
            if row // 2 in (0, 3):
                edge = flag(base_x + row // 2, counts[0])
            if pair in (0, 3):
                other = flag(base_y + pair, counts[1])
                edge = other if edge is None else edge * other
            if edge is not None:
                tile = (tile.astype(f32) * edge).astype(bf)
            store(row, pair, tile)


def decode(
    counts, pos, got, hid, weight, weight_b, lift_t, final,
    feat, out, dom, mid, sums, pd, gd, gs, jf,
):
    w, n = place(pos)
    ra, rb = w & 1, n & 1
    bx, by = w - ra - 1, n - rb - 1

    def put(row, pair, tile):
        dom[row, pair] = tile

    def put_sum(row, pair, tile):
        sums[row, pair] = tile

    spread_quadrants(got, 0, 64, bx, by, counts, put)
    spread_quadrants(got, 640, 32, bx, by, counts, put_sum)

    @pl.loop(0, 8)
    def _(row):
        for o in range(3):
            mid[row, o] = cross(dom[row, o], dom[row, o + 1])

    @pl.loop(0, 6)
    def _(i):
        stack = []
        for o in range(3):
            taps = []
            for dx in range(3):
                taps += [dom[i + dx, o], mid[i + dx, o], dom[i + dx, o + 1]]
            stack.append(rows_of(taps))
        for o, value in enumerate(zsum(dot(weight[...], cols_of(stack)), 32, 64)):
            pd[i, o] = value
            total = cross(sums[i + 1, o].astype(f32), sums[i + 1, o + 1].astype(f32))
            gd[i, o] = (total * slope(value)).astype(bf)

    @pl.loop(0, 4)
    def _(j):
        stack = []
        for p in range(2):
            taps = []
            for dx in range(3):
                left, right = gd[j + dx, p], gd[j + dx, p + 1]
                taps += [left, cross(left, right), right]
            stack.append(rows_of(taps))
        for p, value in enumerate(zsum(dot(weight_b[...], cols_of(stack)), 64, 64)):
            gs[j, p] = value.astype(bf)

    parts = cols_of(
        [gs[2 * a + x, b] for a in range(2) for b in range(2) for x in range(2)]
    )
    gather = selection(1024, 128, lambda r, c: (r >> 8) * 32 + ((r & 63) >> 1) == c)
    grad_lift = dot(parts, gather).astype(bf)
    seg = lanes(128) >> 5
    grad = got[0, 512:640].astype(f32)
    for q in range(1, 4):
        grad = jnp.where(seg == q, got[q, 512:640].astype(f32), grad)
    grad_bottom = (dot(lift_t[...], grad_lift) * grad).astype(bf)
    for t in range(4):
        out[t, 0:128] = grad_bottom
        for x in range(2):
            out[t, 128 + 64 * x : 192 + 64 * x] = gs[2 * ra + x, rb]

    hidden = rows_of(
        [silu(pd[2 * ra + r, rb + o]).astype(bf) for r in range(4) for o in range(2)]
    )
    up = dot(hidden, pair_up())
    fx = [flag(w - 1, counts[0]), None, None, None, None, flag(w + 1, counts[0])]
    fy = [flag(n - 1, counts[1]), None, None, None, None, flag(n + 1, counts[1])]
    for x in range(6):
        for y in range(6):
            r, m = (x + 1) // 2, (y + 1) // 2
            at = (2 * r + m // 2) * 32
            value = up[at : at + 32, 128 * (m % 2) : 128 * (m % 2) + 128]
            value = value + hid[x, y].astype(f32)
            for edge in (fx[x], fy[y]):
                value = value if edge is None else value * edge
            jf[x, y] = value.astype(bf)

    @pl.loop(0, 4)
    def _(x):
        prod = dot(final[...], cols_of([columns(jf, x, y) for y in range(4)]))
        for y, value in enumerate(zsum(prod, 32, 128)):
            feat[x, y] = value.astype(bf)


def deep_gradient(counts, pos, got, early, weight, out):
    w, n = place(pos)
    bx, by = 2 * ((w + 1) // 2) - 2, 2 * ((n + 1) // 2) - 2
    keep = quadrant_keep(128, bx, by, *counts)
    taps = neighbours([got[q, 0:128] for q in range(4)], keep)
    (pooled,) = zsum(dot(weight[...], taps), 64, 32)
    up = exact_up(pooled * 0.125, block_up())
    for s in range(4):
        for x in range(2):
            grad = slope(early[s, 64 * x : 64 * x + 64].astype(f32))
            above = got[s, 128 + 64 * x : 192 + 64 * x].astype(f32)
            value = ((above + up[:, 128 * s : 128 * s + 128]) * grad).astype(bf)
            at = (2 * s + x) * 64
            for t in range(4):
                out[t, at : at + 64] = value


def finish(counts, pos, got, gj, pre, second_b, first_b, out, dom, gf):
    w, n = place(pos)
    ra, rb = w & 1, n & 1

    def put(row, pair, tile):
        dom[row, pair] = tile

    spread_quadrants(got, 0, 64, w - ra - 1, n - rb - 1, counts, put)
    own = [[dom[2 * ra + row, rb + p] for p in range(3)] for row in range(6)]
    mixed = [[cross(line[o], line[o + 1]) for o in range(2)] for line in own]
    grads = []
    for r in range(4):
        stack = []
        for o in range(2):
            taps = []
            for dx in range(3):
                taps += [own[r + dx][o], mixed[r + dx][o], own[r + dx][o + 1]]
            stack.append(rows_of(taps))
        grads += zsum(dot(second_b[...], cols_of(stack)), 32, 64)
    up = exact_up(rows_of(grads) * 0.125, pair_up())
    fx = [flag(w - 1, counts[0]), None, None, None, None, flag(w + 1, counts[0])]
    fy = [flag(n - 1, counts[1]), None, None, None, None, flag(n + 1, counts[1])]
    for x in range(6):
        for y in range(6):
            r, m = (x + 1) // 2, (y + 1) // 2
            at = (2 * r + m // 2) * 32
            value = up[at : at + 32, 128 * (m % 2) : 128 * (m % 2) + 128]
            value = (value + gj[x, y].astype(f32)) * slope(pre[x, y])
            for edge in (fx[x], fy[y]):
                value = value if edge is None else value * edge
            gf[x, y] = value.astype(bf)

    @pl.loop(0, 4)
    def _(x):
        prod = dot(first_b[...], cols_of([columns(gf, x, y) for y in range(4)]))
        for y, value in enumerate(zsum(prod, 32, 128)):
            out[x, y] = value.astype(bf)


def call(body, counts, outs, scratch, *args):
    smem = pl.BlockSpec(memory_space=pltpu.SMEM)
    vmem = pl.BlockSpec(memory_space=pltpu.VMEM)
    return pl.pallas_call(
        functools.partial(body, counts),
        out_shape=[jax.ShapeDtypeStruct(s, d) for s, d in outs],
        in_specs=[smem] + [vmem] * (len(args) - 1),
        out_specs=[vmem] * len(outs),
        scratch_shapes=[pltpu.VMEM(s, d) for s, d in scratch],
        compiler_params=pltpu.CompilerParams(vmem_limit_bytes=48 * 1024 * 1024),
        name=body.__name__,
    )(*args)


def send(cells, axis, step):
    count = lax.axis_size(axis)
    pairs = [(i, i + step) for i in range(count) if 0 <= i + step < count]
    return lax.ppermute(cells, axis, pairs)


def widened(cells, axis, dim, width):
    size = cells.shape[dim]
    head = lax.slice_in_dim(cells, 0, width, axis=dim)
    tail = lax.slice_in_dim(cells, size - width, size, axis=dim)
    return send(tail, axis, 1), send(head, axis, -1)


def shards(
    volume, cotangent, conv_first, conv_second, conv_bottom, lift_weight, conv_decode, conv_final
):
    counts = (lax.axis_size("wide"), lax.axis_size("narrow"))
    pos = jnp.stack([lax.axis_index("wide"), lax.axis_index("narrow")]).astype(jnp.int32)

    def gathered(content, shift):
        groups = [
            [
                ((i + a) % counts[0]) * counts[1] + (j + b) % counts[1]
                for a in range(2)
                for b in range(2)
            ]
            for i in range(shift, counts[0] + shift, 2)
            for j in range(shift, counts[1] + shift, 2)
        ]
        return lax.all_to_all(
            content, ("wide", "narrow"), 0, 0, axis_index_groups=groups
        )

    vol = volume.transpose(1, 2, 0, 3)
    cot = cotangent.transpose(1, 2, 0, 3)
    vl, vr = widened(vol, "narrow", 1, 3)
    cl, cr = widened(cot, "narrow", 1, 2)
    vol = jnp.concatenate([vl, vol, vr], axis=1)
    cot = jnp.concatenate([cl, cot, cr], axis=1)
    vol_l, vol_r = widened(vol, "wide", 0, 3)
    cot_l, cot_r = widened(cot, "wide", 0, 2)

    full = (6, 6, 32, 128)
    hid, pre, gj, content, p2 = call(
        encode, counts,
        [(full, bf), (full, f32), (full, bf), ((192, 128), bf), ((64, 128), bf)],
        [((10, 10, 32, 128), bf), ((8, 8, 32, 128), bf), ((8, 8, 32, 128), bf)],
        pos, vol, vol_l, vol_r, cot, cot_l, cot_r,
        forward_matrix(conv_first), forward_matrix(conv_second), backward_matrix(conv_final),
    )
    four = gathered(jnp.broadcast_to(p2, (4, 64, 128)), 0)
    seg = lax.broadcasted_iota(jnp.int32, (64, 128), 1) // 32
    packed = four[0]
    for q in range(1, 4):
        packed = jnp.where(seg == q, four[q], packed)
    content = jnp.concatenate([content, packed], axis=0)
    early = gathered(jnp.broadcast_to(content, (4, 256, 128)), 1)
    (content,) = call(
        bottom, counts, [((4, 896, 128), bf)], [],
        pos, early, forward_matrix(conv_bottom), lift_weight,
    )
    got = gathered(content, 0)
    cells = (4, 4, 32, 128)
    features, content = call(
        decode, counts, [(cells, bf), ((4, 256, 128), bf)],
        [
            ((8, 4, 64, 128), bf), ((8, 3, 64, 128), bf), ((8, 4, 32, 128), bf),
            ((6, 3, 32, 128), f32), ((6, 3, 32, 128), bf), ((4, 2, 64, 128), bf),
            (full, bf),
        ],
        pos, got, hid, forward_matrix(conv_decode), backward_matrix(conv_decode),
        lift_weight.T, forward_matrix(conv_final),
    )
    got = gathered(content, 1)
    (content,) = call(
        deep_gradient, counts, [((4, 512, 128), bf)], [],
        pos, got, early, backward_matrix(conv_bottom),
    )
    got = gathered(content, 0)
    (grad,) = call(
        finish, counts, [(cells, bf)], [((8, 4, 64, 128), bf), (full, bf)],
        pos, got, gj, pre, backward_matrix(conv_second), backward_matrix(conv_first),
    )
    return features.transpose(2, 0, 1, 3), grad.transpose(2, 0, 1, 3)


def solution(mesh):
    field = P(None, "wide", "narrow", None)
    return jax.shard_map(
        shards,
        mesh=mesh,
        in_specs=(field, field) + (P(),) * 6,
        out_specs=(field, field),
        check_vma=False,
    )
```

time: 263 us -> 132 us (0.50)
  the two profiles are of different devices: /device:TPU:206 before, /device:TPU:1 now
where the time goes in v1:
time: 132 us; the launch traced here: 131 us
  starting transfers between devices  60.7 us (46%)
  waiting for transfers between devices  34.6 us (26%)
  Pallas kernels  20.1 us (15%)
  local copies, waits for them, and re-layouts  14.6 us (11%)
    all_to_all x5, starting transfers between devices, gathered(): lax.all_to_all(content, ('wide', 'narrow'), 0, 0, axis_index_groups=groups)  35.1 us
    ppermute x8, starting transfers between devices, send(): return lax.ppermute(cells, axis, pairs)  25.6 us
    all_to_all x5, waiting for transfers between devices, gathered(): lax.all_to_all(content, ('wide', 'narrow'), 0, 0, axis_index_groups=groups)  25.5 us
    pallas_call x5, Pallas kernels, call(): pl.pallas_call(functools.partial(body, counts), out_shape=[jax.ShapeDtype...  20.1 us
    ppermute x8, waiting for transfers between devices, send(): return lax.ppermute(cells, axis, pairs)  9.11 us
    reshape x7, local copies, waits for them, and re-layouts, forward_matrix(): return kernel.transpose(2, 4, 0, 1, 3).reshape(3 * outs, 9 * chans)  5.12 us
    unnamed x21, local copies, waits for them, and re-layouts  3.52 us
  transfers between devices with their start and end apart: 13, of which 7 were waited for; matrix products, arithmetic and copies ran while one was open for 9% of the time, Pallas kernels for 0%

profile of v1, /device:TPU:1, one launch (start us, length us, event | category | flops | bytes accessed | tf_op | source)
XLA Modules:
  0.0 131.2 jit_solution(4663651080762485451)
XLA Ops:
  0.6 1.0 copy.48
  1.7 4.0 %collective-permute-start = (bf16[4,3,32,128]{3,2,1,0:T(8,128)(2,1)S(1)}, bf16[4,3,32,128]{3,2,1,0:T(8,128)(2,1)S(1)}, u32[]{:S(2)}, u32[]{:S(2)}) collective-permute-start(bf16[4,3,32,128]{3,2,1,0:T(8,128)(2,1)S(1)} %get-tuple-element.26), channel_id=1, source_target_pairs={{0,1},{1,2},{2,3},{3,4},{4,5},{5,6},{6,7},{7,8},{8,9},{9,10},{10,1... | collective-permute-start | bytes 294920 | tf_op jit(solution)/shard_map/ppermute | solution.py:424
  5.7 1.3 collective-permute-start.1
  7.0 0.9 copy.47
  7.9 4.5 %collective-permute-start.4 = (bf16[4,2,32,128]{3,2,1,0:T(8,128)(2,1)S(1)}, bf16[4,2,32,128]{3,2,1,0:T(8,128)(2,1)S(1)}, u32[]{:S(2)}, u32[]{:S(2)}) collective-permute-start(bf16[4,2,32,128]{3,2,1,0:T(8,128)(2,1)S(1)} %get-tuple-element.24), channel_id=1, source_target_pairs={{0,1},{1,2},{2,3},{3,4},{4,5},{5,6},{6,7},{7,8},{8,9},{9,10},{10,1... | collective-permute-start | bytes 196616 | tf_op jit(solution)/shard_map/ppermute | solution.py:424
  12.5 1.3 collective-permute-start.5
  13.8 5.0 %collective-permute-done.5 = bf16[4,2,32,128]{3,2,1,0:T(8,128)(2,1)S(1)} collective-permute-done((bf16[4,2,32,128]{3,2,1,0:T(8,128)(2,1)S(1)}, bf16[4,2,32,128]{3,2,1,0:T(8,128)(2,1)S(1)}, u32[]{:S(2)}, u32[]{:S(2)}) %collective-permute-start.5) | collective-permute-done | bytes 65568 | tf_op jit(solution)/shard_map/ppermute | solution.py:424
  19.0 6.0 %collective-permute-start.2 = (bf16[3,10,32,128]{3,2,1,0:T(8,128)(2,1)S(1)}, bf16[3,10,32,128]{3,2,1,0:T(8,128)(2,1)S(1)}, u32[]{:S(2)}, u32[]{:S(2)}) collective-permute-start(bf16[3,10,32,128]{3,2,1,0:T(8,128)(2,1)S(1)} %get-tuple-element.21), channel_id=1, source_target_pairs={{0,16},{16,32},{32,48},{48,64},{64,80},{80,96},{96,112},{112,128},... | collective-permute-start | bytes 737288 | tf_op jit(solution)/shard_map/ppermute | solution.py:424
  25.1 1.9 %collective-permute-start.3 = (bf16[3,10,32,128]{3,2,1,0:T(8,128)(2,1)S(1)}, bf16[3,10,32,128]{3,2,1,0:T(8,128)(2,1)S(1)}, u32[]{:S(2)}, u32[]{:S(2)}) collective-permute-start(bf16[3,10,32,128]{3,2,1,0:T(8,128)(2,1)S(1)} %get-tuple-element.20), channel_id=1, source_target_pairs={{16,0},{32,16},{48,32},{64,48},{80,64},{96,80},{112,96},{128,112},... | collective-permute-start | bytes 737288 | tf_op jit(solution)/shard_map/ppermute | solution.py:424
  27.0 0.7 fusion.4
  27.7 4.7 %collective-permute-start.6 = (bf16[2,8,32,128]{3,2,1,0:T(8,128)(2,1)}, bf16[2,8,32,128]{3,2,1,0:T(8,128)(2,1)S(1)}, u32[]{:S(2)}, u32[]{:S(2)}) collective-permute-start(bf16[2,8,32,128]{3,2,1,0:T(8,128)(2,1)} %get-tuple-element.23), channel_id=1, source_target_pairs={{0,16},{16,32},{32,48},{48,64},{64,80},{80,96},{96,112},{112,128},... | collective-permute-start | bytes 393224 | tf_op jit(solution)/shard_map/ppermute | solution.py:424
  32.3 1.9 %collective-permute-start.7 = (bf16[2,8,32,128]{3,2,1,0:T(8,128)(2,1)S(1)}, bf16[2,8,32,128]{3,2,1,0:T(8,128)(2,1)S(1)}, u32[]{:S(2)}, u32[]{:S(2)}) collective-permute-start(bf16[2,8,32,128]{3,2,1,0:T(8,128)(2,1)S(1)} %get-tuple-element.22), channel_id=1, source_target_pairs={{16,0},{32,16},{48,32},{64,48},{80,64},{96,80},{112,96},{128,112},... | collective-permute-start | bytes 393224 | tf_op jit(solution)/shard_map/ppermute | solution.py:424
  34.5 0.2 reshape.35
  34.9 0.2 copy.29
  35.0 0.2 reshape.36.final_b
  35.2 0.2 copy.27
  35.4 0.2 reshape.34.first
  35.6 4.1 %collective-permute-done.7.cot_r = bf16[2,8,32,128]{3,2,1,0:T(8,128)(2,1)S(1)} collective-permute-done((bf16[2,8,32,128]{3,2,1,0:T(8,128)(2,1)S(1)}, bf16[2,8,32,128]{3,2,1,0:T(8,128)(2,1)S(1)}, u32[]{:S(2)}, u32[]{:S(2)}) %collective-permute-start.7) | collective-permute-done | bytes 131104 | tf_op jit(solution)/shard_map/ppermute | solution.py:424
  39.7 6.5 %encode.1 = (bf16[6,6,32,128]{3,2,1,0:T(8,128)(2,1)S(1)}, f32[6,6,32,128]{3,2,1,0:T(8,128)S(1)}, bf16[6,6,32,128]{3,2,1,0:T(8,128)(2,1)S(1)}, bf16[192,128]{1,0:T(8,128)(2,1)S(1)}, bf16[64,128]{1,0:T(8,128)(2,1)S(1)}) custom-call(s32[2]{0:T(128)S(1)} %pad_add_fusion.pos, bf16[4,10,32,128]{3,2,1,0:T(8,128)(2,1)S(1)} %pad_maximum_fusion.vol, ...), custom_call_target="tpu_custom_call" | custom-call | tf_op jit(solution)/shard_map/encode/pallas_call | solution.py:410
  46.2 0.6 broadcast_in_dim.6
  46.8 4.2 %all-to-all-start = ((bf16[4,64,128]{2,1,0:T(8,128)(2,1)}), bf16[4,64,128]{2,1,0:T(8,128)(2,1)S(1)}, u32[]{:S(2)}, u32[]{:S(2)}) async-start(bf16[4,64,128]{2,1,0:T(8,128)(2,1)} %broadcast_in_dim.6), calls=%async_computation | async-start | bytes 131072 | tf_op jit(solution)/shard_map/all_to_all | solution.py:450
  51.1 3.3 %all-to-all-done = bf16[4,64,128]{2,1,0:T(8,128)(2,1)S(1)} async-done(((bf16[4,64,128]{2,1,0:T(8,128)(2,1)}), bf16[4,64,128]{2,1,0:T(8,128)(2,1)S(1)}, u32[]{:S(2)}, u32[]{:S(2)}) %all-to-all-start) | async-done | bytes 65568 | tf_op jit(solution)/shard_map/all_to_all | solution.py:450
  54.4 0.7 broadcast_in_dim.7
  55.1 14.2 %all-to-all-start.1 = ((bf16[4,256,128]{2,1,0:T(8,128)(2,1)}), bf16[4,256,128]{2,1,0:T(8,128)(2,1)S(1)}, u32[]{:S(2)}, u32[]{:S(2)}) async-start(bf16[4,256,128]{2,1,0:T(8,128)(2,1)} %broadcast_in_dim.7), calls=%async_computation.1 | async-start | bytes 524288 | tf_op jit(solution)/shard_map/all_to_all | solution.py:450
  69.3 2.3 %copy.43 = bf16[3,128,3,3,64]{4,3,2,1,0:T(4,128)(2,1)S(1)} copy(bf16[3,128,3,3,64]{1,4,0,3,2:T(8,128)(2,1)} %bitcast.49) | data formatting | bytes 884736 | tf_op jit(solution)/shard_map/reshape | solution.py:16
  71.6 0.8 reshape.44.weight
  72.4 2.2 %all-to-all-done.1.got.early = bf16[4,256,128]{2,1,0:T(8,128)(2,1)S(1)} async-done(((bf16[4,256,128]{2,1,0:T(8,128)(2,1)}), bf16[4,256,128]{2,1,0:T(8,128)(2,1)S(1)}, u32[]{:S(2)}, u32[]{:S(2)}) %all-to-all-start.1) | async-done | bytes 262176 | tf_op jit(solution)/shard_map/all_to_all | solution.py:450
  74.6 2.3 %bottom.1 = bf16[4,896,128]{2,1,0:T(8,128)(2,1)} custom-call(s32[2]{0:T(128)S(1)} %pad_add_fusion.pos, bf16[4,256,128]{2,1,0:T(8,128)(2,1)S(1)} %all-to-all-done.1.got.early, bf16[384,576]{1,0:T(8,128)(2,1)S(1)} %reshape.44.weight, bf16[64,128]{1,0:T(8,128)(2,1)S(1)} %copy-done), custom_call_target="tpu_custom_call" | custom-call | tf_op jit(solution)/shard_map/bottom/pallas_call | solution.py:410
  76.9 3.6 %all-to-all-start.2 = ((bf16[4,896,128]{2,1,0:T(8,128)(2,1)}), bf16[4,896,128]{2,1,0:T(8,128)(2,1)S(1)}, u32[]{:S(2)}, u32[]{:S(2)}) async-start(bf16[4,896,128]{2,1,0:T(8,128)(2,1)} %bottom.1), calls=%async_computation.2 | async-start | bytes 1835008 | tf_op jit(solution)/shard_map/all_to_all | solution.py:450
  80.9 0.2 reshape.39
  81.2 0.2 copy.33
  81.4 0.2 reshape.38.weight
  81.6 0.9 copy.36
  82.5 1.2 reshape.40.final
  83.7 8.0 %all-to-all-done.2.got = bf16[4,896,128]{2,1,0:T(8,128)(2,1)S(1)} async-done(((bf16[4,896,128]{2,1,0:T(8,128)(2,1)}), bf16[4,896,128]{2,1,0:T(8,128)(2,1)S(1)}, u32[]{:S(2)}, u32[]{:S(2)}) %all-to-all-start.2) | async-done | bytes 917536 | tf_op jit(solution)/shard_map/all_to_all | solution.py:450
  91.8 6.7 %decode.1 = (bf16[4,4,32,128]{3,2,1,0:T(8,128)(2,1)S(1)}, bf16[4,256,128]{2,1,0:T(8,128)(2,1)}) custom-call(s32[2]{0:T(128)S(1)} %pad_add_fusion.pos, bf16[4,896,128]{2,1,0:T(8,128)(2,1)S(1)} %all-to-all-done.2.got, bf16[6,6,32,128]{3,2,1,0:T(8,128)(2,1)S(1)} %get-tuple-element.11.hid, bf16[96,576]{1,0:T(8,128)(2,1)S(1)} %reshape.38.weight, ...), custom_call_target="tpu_custom_call" | custom-call | tf_op jit(solution)/shard_map/decode/pallas_call | solution.py:410
  98.5 7.6 %all-to-all-start.3 = ((bf16[4,256,128]{2,1,0:T(8,128)(2,1)}), bf16[4,256,128]{2,1,0:T(8,128)(2,1)S(1)}, u32[]{:S(2)}, u32[]{:S(2)}) async-start(bf16[4,256,128]{2,1,0:T(8,128)(2,1)} %get-tuple-element.13), calls=%async_computation.3 | async-start | bytes 524288 | tf_op jit(solution)/shard_map/all_to_all | solution.py:450
  106.1 0.4 copy.38
  106.5 0.4 reshape.41.weight
  106.9 5.7 %all-to-all-done.3.got = bf16[4,256,128]{2,1,0:T(8,128)(2,1)S(1)} async-done(((bf16[4,256,128]{2,1,0:T(8,128)(2,1)}), bf16[4,256,128]{2,1,0:T(8,128)(2,1)S(1)}, u32[]{:S(2)}, u32[]{:S(2)}) %all-to-all-start.3) | async-done | bytes 262176 | tf_op jit(solution)/shard_map/all_to_all | solution.py:450
  112.6 2.0 %deep_gradient.1 = bf16[4,512,128]{2,1,0:T(8,128)(2,1)} custom-call(s32[2]{0:T(128)S(1)} %pad_add_fusion.pos, bf16[4,256,128]{2,1,0:T(8,128)(2,1)S(1)} %all-to-all-done.3.got, bf16[4,256,128]{2,1,0:T(8,128)(2,1)S(1)} %all-to-all-done.1.got.early, bf16[192,1152]{1,0:T(8,128)(2,1)S(1)} %reshape.41.weight), custom_call_target="tpu_custom_call" | custom-call | tf_op jit(solution)/shard_map/deep_gradient/pallas_call | solution.py:410
  114.6 5.5 %all-to-all-start.4 = ((bf16[4,512,128]{2,1,0:T(8,128)(2,1)}), bf16[4,512,128]{2,1,0:T(8,128)(2,1)S(1)}, u32[]{:S(2)}, u32[]{:S(2)}) async-start(bf16[4,512,128]{2,1,0:T(8,128)(2,1)} %deep_gradient.1), calls=%async_computation.4 | async-start | bytes 1048576 | tf_op jit(solution)/shard_map/all_to_all | solution.py:450
  120.2 0.2 reshape.42.second_b
  120.7 0.2 reshape.43.first_b
  120.9 0.7 copy.41
  121.6 6.3 %all-to-all-done.4.got = bf16[4,512,128]{2,1,0:T(8,128)(2,1)S(1)} async-done(((bf16[4,512,128]{2,1,0:T(8,128)(2,1)}), bf16[4,512,128]{2,1,0:T(8,128)(2,1)S(1)}, u32[]{:S(2)}, u32[]{:S(2)}) %all-to-all-start.4) | async-done | bytes 524320 | tf_op jit(solution)/shard_map/all_to_all | solution.py:450
  127.9 2.6 %finish.1 = bf16[4,4,32,128]{3,2,1,0:T(8,128)(2,1)S(1)} custom-call(s32[2]{0:T(128)S(1)} %pad_add_fusion.pos, bf16[4,512,128]{2,1,0:T(8,128)(2,1)S(1)} %all-to-all-done.4.got, bf16[6,6,32,128]{3,2,1,0:T(8,128)(2,1)S(1)} %get-tuple-element.14.gj, f32[6,6,32,128]{3,2,1,0:T(8,128)S(1)} %get-tuple-element.15.pre, bf16[96,576]{1,0:T(8,128)(2,1)S(1)} %reshape.42.second_b, ...), custom_call_target="tpu_custom_call" | custom-call | tf_op jit(solution)/shard_map/finish/pallas_call | solution.py:410
  130.5 0.7 copy.42
  (44 shorter events, 1.4 us)
Async XLA Ops:
  0.6 13.1 %copy-start.3 = (bf16[3,3,3,32,32]{4,3,2,1,0:T(8,128)(2,1)S(1)}, bf16[3,3,3,32,32]{4,3,2,1,0:T(8,128)(2,1)}, u32[]{:S(2)}) copy-start(bf16[3,3,3,32,32]{4,3,2,1,0:T(8,128)(2,1)} %param.15) | copy-start | bytes 165892
  1.7 17.3 %collective-permute-start = (bf16[4,3,32,128]{3,2,1,0:T(8,128)(2,1)S(1)}, bf16[4,3,32,128]{3,2,1,0:T(8,128)(2,1)S(1)}, u32[]{:S(2)}, u32[]{:S(2)}) collective-permute-start(bf16[4,3,32,128]{3,2,1,0:T(8,128)(2,1)S(1)} %get-tuple-element.26), channel_id=1, source_target_pairs={{0,1},{1,2},{2,3},{3,4},{4,5},{5,6},{6,7},{7,8},{8,9},{9,10},{10,1... | collective-permute-start | bytes 294920 | tf_op jit(solution)/shard_map/ppermute | solution.py:424
  5.7 13.2 %collective-permute-start.1 = (bf16[4,3,32,128]{3,2,1,0:T(8,128)(2,1)S(1)}, bf16[4,3,32,128]{3,2,1,0:T(8,128)(2,1)S(1)}, u32[]{:S(2)}, u32[]{:S(2)}) collective-permute-start(bf16[4,3,32,128]{3,2,1,0:T(8,128)(2,1)S(1)} %get-tuple-element.27), channel_id=1, source_target_pairs={{1,0},{2,1},{3,2},{4,3},{5,4},{6,5},{7,6},{8,7},{9,8},{10,9},{11,1... | collective-permute-start | bytes 294920 | tf_op jit(solution)/shard_map/ppermute | solution.py:424
  7.9 5.9 %collective-permute-start.4 = (bf16[4,2,32,128]{3,2,1,0:T(8,128)(2,1)S(1)}, bf16[4,2,32,128]{3,2,1,0:T(8,128)(2,1)S(1)}, u32[]{:S(2)}, u32[]{:S(2)}) collective-permute-start(bf16[4,2,32,128]{3,2,1,0:T(8,128)(2,1)S(1)} %get-tuple-element.24), channel_id=1, source_target_pairs={{0,1},{1,2},{2,3},{3,4},{4,5},{5,6},{6,7},{7,8},{8,9},{9,10},{10,1... | collective-permute-start | bytes 196616 | tf_op jit(solution)/shard_map/ppermute | solution.py:424
  12.5 6.4 %collective-permute-start.5 = (bf16[4,2,32,128]{3,2,1,0:T(8,128)(2,1)S(1)}, bf16[4,2,32,128]{3,2,1,0:T(8,128)(2,1)S(1)}, u32[]{:S(2)}, u32[]{:S(2)}) collective-permute-start(bf16[4,2,32,128]{3,2,1,0:T(8,128)(2,1)S(1)} %get-tuple-element.25), channel_id=1, source_target_pairs={{1,0},{2,1},{3,2},{4,3},{5,4},{6,5},{7,6},{8,7},{9,8},{10,9},{11,1... | collective-permute-start | bytes 196616 | tf_op jit(solution)/shard_map/ppermute | solution.py:424
  18.9 15.4 %copy-start.4 = (bf16[3,3,3,32,64]{4,3,2,1,0:T(8,128)(2,1)S(1)}, bf16[3,3,3,32,64]{4,3,2,1,0:T(8,128)(2,1)}, u32[]{:S(2)}) copy-start(bf16[3,3,3,32,64]{4,3,2,1,0:T(8,128)(2,1)} %param.11) | copy-start | bytes 331780
  19.0 20.6 %collective-permute-start.2 = (bf16[3,10,32,128]{3,2,1,0:T(8,128)(2,1)S(1)}, bf16[3,10,32,128]{3,2,1,0:T(8,128)(2,1)S(1)}, u32[]{:S(2)}, u32[]{:S(2)}) collective-permute-start(bf16[3,10,32,128]{3,2,1,0:T(8,128)(2,1)S(1)} %get-tuple-element.21), channel_id=1, source_target_pairs={{0,16},{16,32},{32,48},{48,64},{64,80},{80,96},{96,112},{112,128},... | collective-permute-start | bytes 737288 | tf_op jit(solution)/shard_map/ppermute | solution.py:424
  25.1 14.6 %collective-permute-start.3 = (bf16[3,10,32,128]{3,2,1,0:T(8,128)(2,1)S(1)}, bf16[3,10,32,128]{3,2,1,0:T(8,128)(2,1)S(1)}, u32[]{:S(2)}, u32[]{:S(2)}) collective-permute-start(bf16[3,10,32,128]{3,2,1,0:T(8,128)(2,1)S(1)} %get-tuple-element.20), channel_id=1, source_target_pairs={{16,0},{32,16},{48,32},{64,48},{80,64},{96,80},{112,96},{128,112},... | collective-permute-start | bytes 737288 | tf_op jit(solution)/shard_map/ppermute | solution.py:424
  27.7 7.5 %copy-start.6 = (bf16[3,3,3,32,32]{4,3,2,1,0:T(8,128)(2,1)S(1)}, bf16[3,3,3,32,32]{4,3,2,1,0:T(8,128)(2,1)}, u32[]{:S(2)}) copy-start(bf16[3,3,3,32,32]{4,3,2,1,0:T(8,128)(2,1)} %param.10) | copy-start | bytes 165892
  27.7 8.0 %collective-permute-start.6 = (bf16[2,8,32,128]{3,2,1,0:T(8,128)(2,1)}, bf16[2,8,32,128]{3,2,1,0:T(8,128)(2,1)S(1)}, u32[]{:S(2)}, u32[]{:S(2)}) collective-permute-start(bf16[2,8,32,128]{3,2,1,0:T(8,128)(2,1)} %get-tuple-element.23), channel_id=1, source_target_pairs={{0,16},{16,32},{32,48},{48,64},{64,80},{80,96},{96,112},{112,128},... | collective-permute-start | bytes 393224 | tf_op jit(solution)/shard_map/ppermute | solution.py:424
  32.3 7.4 %collective-permute-start.7 = (bf16[2,8,32,128]{3,2,1,0:T(8,128)(2,1)S(1)}, bf16[2,8,32,128]{3,2,1,0:T(8,128)(2,1)S(1)}, u32[]{:S(2)}, u32[]{:S(2)}) collective-permute-start(bf16[2,8,32,128]{3,2,1,0:T(8,128)(2,1)S(1)} %get-tuple-element.22), channel_id=1, source_target_pairs={{16,0},{32,16},{48,32},{64,48},{80,64},{96,80},{112,96},{128,112},... | collective-permute-start | bytes 393224 | tf_op jit(solution)/shard_map/ppermute | solution.py:424
  46.8 7.5 %all-to-all-start = ((bf16[4,64,128]{2,1,0:T(8,128)(2,1)}), bf16[4,64,128]{2,1,0:T(8,128)(2,1)S(1)}, u32[]{:S(2)}, u32[]{:S(2)}) async-start(bf16[4,64,128]{2,1,0:T(8,128)(2,1)} %broadcast_in_dim.6), calls=%async_computation | async-start | bytes 131072 | tf_op jit(solution)/shard_map/all_to_all | solution.py:450
  55.1 19.5 %all-to-all-start.1 = ((bf16[4,256,128]{2,1,0:T(8,128)(2,1)}), bf16[4,256,128]{2,1,0:T(8,128)(2,1)S(1)}, u32[]{:S(2)}, u32[]{:S(2)}) async-start(bf16[4,256,128]{2,1,0:T(8,128)(2,1)} %broadcast_in_dim.7), calls=%async_computation.1 | async-start | bytes 524288 | tf_op jit(solution)/shard_map/all_to_all | solution.py:450
  71.6 3.0 %copy-start = (bf16[64,128]{1,0:T(8,128)(2,1)S(1)}, bf16[64,128]{1,0:T(8,128)(2,1)}, u32[]{:S(2)}) copy-start(bf16[64,128]{1,0:T(8,128)(2,1)} %lift.1) | copy-start | bytes 49156
  76.9 3.8 %copy-start.2 = (bf16[3,3,3,64,32]{3,4,2,1,0:T(8,128)(2,1)S(1)}, bf16[3,3,3,64,32]{3,4,2,1,0:T(8,128)(2,1)}, u32[]{:S(2)}) copy-start(bf16[3,3,3,64,32]{3,4,2,1,0:T(8,128)(2,1)} %param.14) | copy-start | bytes 331780
  76.9 14.9 %all-to-all-start.2 = ((bf16[4,896,128]{2,1,0:T(8,128)(2,1)}), bf16[4,896,128]{2,1,0:T(8,128)(2,1)S(1)}, u32[]{:S(2)}, u32[]{:S(2)}) async-start(bf16[4,896,128]{2,1,0:T(8,128)(2,1)} %bottom.1), calls=%async_computation.2 | async-start | bytes 1835008 | tf_op jit(solution)/shard_map/all_to_all | solution.py:450
  82.5 23.6 %copy-start.1 = (bf16[3,3,3,64,128]{4,3,2,1,0:T(8,128)(2,1)S(1)}, bf16[3,3,3,64,128]{4,3,2,1,0:T(8,128)(2,1)}, u32[]{:S(2)}) copy-start(bf16[3,3,3,64,128]{4,3,2,1,0:T(8,128)(2,1)} %param.12) | copy-start | bytes 1327108
  98.5 14.1 %all-to-all-start.3 = ((bf16[4,256,128]{2,1,0:T(8,128)(2,1)}), bf16[4,256,128]{2,1,0:T(8,128)(2,1)S(1)}, u32[]{:S(2)}, u32[]{:S(2)}) async-start(bf16[4,256,128]{2,1,0:T(8,128)(2,1)} %get-tuple-element.13), calls=%async_computation.3 | async-start | bytes 524288 | tf_op jit(solution)/shard_map/all_to_all | solution.py:450
  106.9 13.2 %copy-start.5 = (bf16[3,3,3,32,64]{4,3,2,1,0:T(8,128)(2,1)S(1)}, bf16[3,3,3,32,64]{4,3,2,1,0:T(8,128)(2,1)}, u32[]{:S(2)}) copy-start(bf16[3,3,3,32,64]{4,3,2,1,0:T(8,128)(2,1)} %param.11) | copy-start | bytes 331780
  114.6 5.9 %copy-start.7 = (bf16[3,3,3,32,32]{4,3,2,1,0:T(8,128)(2,1)S(1)}, bf16[3,3,3,32,32]{4,3,2,1,0:T(8,128)(2,1)}, u32[]{:S(2)}) copy-start(bf16[3,3,3,32,32]{4,3,2,1,0:T(8,128)(2,1)} %param.10) | copy-start | bytes 165892
  114.6 13.3 %all-to-all-start.4 = ((bf16[4,512,128]{2,1,0:T(8,128)(2,1)}), bf16[4,512,128]{2,1,0:T(8,128)(2,1)S(1)}, u32[]{:S(2)}, u32[]{:S(2)}) async-start(bf16[4,512,128]{2,1,0:T(8,128)(2,1)} %deep_gradient.1), calls=%async_computation.4 | async-start | bytes 1048576 | tf_op jit(solution)/shard_map/all_to_all | solution.py:450

commit v2 on v1

--- a/solution.py
+++ b/solution.py
@@ -19,6 +19,16 @@
 def backward_matrix(kernel):
     chans, outs = kernel.shape[3:]
     return jnp.flip(kernel, (0, 1, 2)).transpose(2, 3, 0, 1, 4).reshape(3 * chans, 9 * outs)
+
+
+def forward_strips(kernel):
+    chans, outs = kernel.shape[3:]
+    return kernel.transpose(0, 2, 4, 1, 3).reshape(3, 3 * outs, 3 * chans)
+
+
+def backward_strips(kernel):
+    chans, outs = kernel.shape[3:]
+    return jnp.flip(kernel, (0, 1, 2)).transpose(0, 2, 3, 1, 4).reshape(3, 3 * chans, 3 * outs)
 
 
 def dot(a, b):
@@ -153,54 +163,78 @@
     return pos_ref[0], pos_ref[1]
 
 
-def columns(field, x, y):
-    return rows_of([field[x + dx, y + dy] for dx in range(3) for dy in range(3)])
+def square_matrix(strips, out):
+    blank = jnp.zeros((96, 128), bf)
+    tail = jnp.zeros((96, 32), bf)
+    plain = [cols_of([strips[dx], tail]) for dx in range(3)]
+    moved = [pltpu.roll(t.astype(f32), 32, 1).astype(bf) for t in plain]
+    for i in range(2):
+        for j in range(2):
+            for u in range(4):
+                tile = (moved if j else plain)[u - i] if 0 <= u - i < 3 else blank
+                at = 96 * (2 * i + j)
+                out[at : at + 96, 128 * u : 128 * u + 128] = tile
+
+
+def squares(weight, field, x, count):
+    taps = [
+        rows_of([field[x + u, y + v] for u in range(4) for v in range(4)])
+        for y in range(0, count, 2)
+    ]
+    prod = dot(weight[...], cols_of(taps))
+    for k in range(4):
+        tiles = zsum(prod[96 * k : 96 * k + 96], 32, 128)
+        for at, tile in enumerate(tiles):
+            yield k // 2, 2 * at + k % 2, tile
+
+
+def picked(field, x, y):
+    return cols_of([field[x + i, y + j] for j in range(2) for i in range(2)])
+
+
+def adjoint(counts, pos, cot, cot_l, cot_r, strips, gj, total, ec, matrix):
+    square_matrix(strips, matrix)
+    ec[0:2], ec[2:6], ec[6:8] = cot_l[...], cot[...], cot_r[...]
+
+    @pl.loop(0, 3)
+    def _(i):
+        for dx, y, value in squares(matrix, ec, 2 * i, 6):
+            gj[2 * i + dx, y] = value.astype(bf)
+
+    sums = rows_of(
+        [
+            cols_of([picked(gj, 1 + 2 * x, 1), picked(gj, 1 + 2 * x, 3)])
+            for x in range(2)
+        ]
+    )
+    total[...] = dot(sums, pair_pool()).astype(bf)
 
 
 def encode(
-    counts, pos, vol, vol_l, vol_r, cot, cot_l, cot_r, first, second, final_b,
-    hid, pre, gj, content2, p2, ev, ec, h8,
+    counts, pos, vol, vol_l, vol_r, strips, second,
+    hid, pre, early, p2, ev, h8, pre8, matrix,
 ):
+    square_matrix(strips, matrix)
     w, n = place(pos)
     ev[0:3], ev[3:7], ev[7:10] = vol_l[...], vol[...], vol_r[...]
-    ec[0:2], ec[2:6], ec[6:8] = cot_l[...], cot[...], cot_r[...]
-
-    def row(x, keep):
-        prod = dot(first[...], cols_of([columns(ev, x, y) for y in range(8)]))
-        for y, value in enumerate(zsum(prod, 32, 128)):
-            h = silu(value).astype(bf)
-            h8[x, y] = h
-            if keep and 1 <= y <= 6:
-                hid[x - 1, y - 1] = h
-                pre[x - 1, y - 1] = value
-
-    row(0, False)
-    pl.loop(1, 7)(lambda x: row(x, True))
-    row(7, False)
-
-    @pl.loop(0, 6)
-    def _(x):
-        prod = dot(final_b[...], cols_of([columns(ec, x, y) for y in range(6)]))
-        for y, value in enumerate(zsum(prod, 32, 128)):
-            gj[x, y] = value.astype(bf)
-
-    pool = pair_pool()
-    pick = lambda field, x, y: cols_of(
-        [field[x + i, y + j] for j in range(2) for i in range(2)]
-    )
-    sums = rows_of(
-        [cols_of([pick(gj, 1 + 2 * x, 1), pick(gj, 1 + 2 * x, 3)]) for x in range(2)]
-    )
-    content2[128:192] = dot(sums, pool).astype(bf)
-
+
+    @pl.loop(0, 4)
+    def _(i):
+        for dx, y, value in squares(matrix, ev, 2 * i, 8):
+            h8[2 * i + dx, y] = silu(value).astype(bf)
+            if 1 <= y <= 6:
+                pre8[2 * i + dx, y - 1] = value
+
+    hid[...] = h8[1:7, 1:7]
+    pre[...] = pre8[1:7]
     parts = rows_of(
         [
-            cols_of([pick(h8, 2 * x, 2 * y), pick(h8, 2 * x, 2 * y + 2)])
+            cols_of([picked(h8, 2 * x, 2 * y), picked(h8, 2 * x, 2 * y + 2)])
             for x in range(4)
             for y in range(3)
         ]
     )
-    pooled = dot(parts, pool) * 0.125
+    pooled = dot(parts, pair_pool()) * 0.125
     low = lanes(32) < 64
     fx = [flag(w - 1, counts[0]), 1.0, 1.0, flag(w + 1, counts[0])]
     fl, fr = flag(n - 1, counts[1]), flag(n + 1, counts[1])
@@ -216,9 +250,11 @@
     pre2 = zsum(dot(second[...], cols_of(stack)), 64, 64)
     spread = selection(256, 128, lambda r, c: (r & 63) >> 1 == (c & 31))
     hidden2 = cols_of([silu(v).astype(bf) for v in pre2])
-    p2[...] = (dot(hidden2, spread) * 0.125).astype(bf)
+    pooled2 = (dot(hidden2, spread) * 0.125).astype(bf)
+    for t in range(4):
+        p2[t] = pooled2
     for x in range(2):
-        content2[64 * x : 64 * x + 64] = pre2[x].astype(bf)
+        early[64 * x : 64 * x + 64] = pre2[x].astype(bf)
 
 
 def bottom(counts, pos, got, weight, lift, out):
@@ -230,10 +266,15 @@
     lifted = dot(lift[...], silu(pre).astype(bf))
     up = exact_up(lifted, block_up())
     grad = slope(pre)
-    odd = (lanes(128) >> 5) & 1 == 1
-    turned = jnp.where(odd, pltpu.roll(grad, 96, 1), pltpu.roll(grad, 32, 1)).astype(bf)
+    ra, rb = w & 1, n & 1
+    own = (1 - ra) * 2 + 1 - rb
+    seg = lanes(32) >> 5
+    packed = None
+    for k in range(4):
+        moved = pltpu.roll(grad[32 * k : 32 * k + 32], ((k - own) * 32) & 127, 1)
+        packed = moved if packed is None else jnp.where(seg == k, moved, packed)
     for t in range(4):
-        out[t, 512:640] = turned
+        out[t, 512:544] = packed.astype(bf)
     for s in range(4):
         for x in range(2):
             hidden = silu(got[s, 64 * x : 64 * x + 64].astype(f32)).astype(bf)
@@ -241,16 +282,21 @@
             at = (2 * s + x) * 64
             for t in range(4):
                 out[t, at : at + 64] = joined
-        sums = got[s, 128:192]
-        for t in range(4):
-            out[t, 640 + 64 * s : 704 + 64 * s] = sums
-
-
-def spread_quadrants(got, start, rows, base_x, base_y, counts, store):
+    for r in range(3):
+        row = 1 - ra + r
+        for b in range(2):
+            start = pl.multiple_of(128 + 32 * (row & 1), 32)
+            sums = got[(row >> 1) * 2 + b, pl.ds(start, 32)]
+            for t in range(4):
+                out[t, 544 + 64 * r + 32 * b : 576 + 64 * r + 32 * b] = sums
+
+
+def spread_quadrants(got, place_of, rows, base_x, base_y, counts, store):
     for row in range(8):
         for pair in range(4):
-            q, s = (row // 4) * 2 + pair // 2, ((row % 4) // 2) * 2 + pair % 2
-            at = start + (2 * s + row % 2) * rows
+            q, at = (row // 4) * 2 + pair // 2, place_of(row, pair)
+            if at is None:
+                continue
             tile = got[q, at : at + rows]
             edge = None
             if row // 2 in (0, 3):
@@ -264,8 +310,7 @@
 
 
 def decode(
-    counts, pos, got, hid, weight, weight_b, lift_t, final,
-    feat, out, dom, mid, sums, pd, gd, gs, jf,
+    counts, pos, got, weight, weight_b, lift_t, out, hidden, dom, mid, sums, pd, gd, gs
 ):
     w, n = place(pos)
     ra, rb = w & 1, n & 1
@@ -275,10 +320,18 @@
         dom[row, pair] = tile
 
     def put_sum(row, pair, tile):
-        sums[row, pair] = tile
-
-    spread_quadrants(got, 0, 64, bx, by, counts, put)
-    spread_quadrants(got, 640, 32, bx, by, counts, put_sum)
+        sums[row - 1, pair] = tile
+
+    def joined_at(row, pair):
+        return (((row % 4) // 2 * 2 + pair % 2) * 2 + row % 2) * 64
+
+    def sum_at(row, pair):
+        if row in (0, 7):
+            return None
+        return 544 + ((row - 1) % 3) * 64 + pair % 2 * 32
+
+    spread_quadrants(got, joined_at, 64, bx, by, counts, put)
+    spread_quadrants(got, sum_at, 32, bx, by, counts, put_sum)
 
     @pl.loop(0, 8)
     def _(row):
@@ -295,7 +348,7 @@
             stack.append(rows_of(taps))
         for o, value in enumerate(zsum(dot(weight[...], cols_of(stack)), 32, 64)):
             pd[i, o] = value
-            total = cross(sums[i + 1, o].astype(f32), sums[i + 1, o + 1].astype(f32))
+            total = cross(sums[i, o].astype(f32), sums[i, o + 1].astype(f32))
             gd[i, o] = (total * slope(value)).astype(bf)
 
     @pl.loop(0, 4)
@@ -315,22 +368,37 @@
     )
     gather = selection(1024, 128, lambda r, c: (r >> 8) * 32 + ((r & 63) >> 1) == c)
     grad_lift = dot(parts, gather).astype(bf)
-    seg = lanes(128) >> 5
-    grad = got[0, 512:640].astype(f32)
-    for q in range(1, 4):
-        grad = jnp.where(seg == q, got[q, 512:640].astype(f32), grad)
-    grad_bottom = (dot(lift_t[...], grad_lift) * grad).astype(bf)
+    seg = lanes(32) >> 5
+    packs = [got[q, 512:544].astype(f32) for q in range(4)]
+    grads = []
+    for k in range(4):
+        grad = None
+        for q in range(4):
+            piece = pltpu.roll(packs[q], (q - k) * 32 % 128, 1) if q != k else packs[q]
+            grad = piece if grad is None else jnp.where(seg == q, piece, grad)
+        grads.append(grad)
+    grad_bottom = (dot(lift_t[...], grad_lift) * rows_of(grads)).astype(bf)
     for t in range(4):
         out[t, 0:128] = grad_bottom
         for x in range(2):
             out[t, 128 + 64 * x : 192 + 64 * x] = gs[2 * ra + x, rb]
-
-    hidden = rows_of(
-        [silu(pd[2 * ra + r, rb + o]).astype(bf) for r in range(4) for o in range(2)]
-    )
-    up = dot(hidden, pair_up())
+    for r in range(4):
+        for o in range(2):
+            at = (2 * r + o) * 32
+            hidden[at : at + 32] = silu(pd[2 * ra + r, rb + o]).astype(bf)
+
+
+def edges(pos, counts):
+    w, n = place(pos)
     fx = [flag(w - 1, counts[0]), None, None, None, None, flag(w + 1, counts[0])]
     fy = [flag(n - 1, counts[1]), None, None, None, None, flag(n + 1, counts[1])]
+    return fx, fy
+
+
+def output(counts, pos, hidden, hid, strips, feat, jf, matrix):
+    square_matrix(strips, matrix)
+    up = dot(hidden[...], pair_up())
+    fx, fy = edges(pos, counts)
     for x in range(6):
         for y in range(6):
             r, m = (x + 1) // 2, (y + 1) // 2
@@ -341,14 +409,13 @@
                 value = value if edge is None else value * edge
             jf[x, y] = value.astype(bf)
 
-    @pl.loop(0, 4)
-    def _(x):
-        prod = dot(final[...], cols_of([columns(jf, x, y) for y in range(4)]))
-        for y, value in enumerate(zsum(prod, 32, 128)):
-            feat[x, y] = value.astype(bf)
-
-
-def deep_gradient(counts, pos, got, early, weight, out):
+    @pl.loop(0, 2)
+    def _(i):
+        for dx, y, value in squares(matrix, jf, 2 * i, 4):
+            feat[2 * i + dx, y] = value.astype(bf)
+
+
+def deep_gradient(counts, pos, got, early, weight, out, mine):
     w, n = place(pos)
     bx, by = 2 * ((w + 1) // 2) - 2, 2 * ((n + 1) // 2) - 2
     keep = quadrant_keep(128, bx, by, *counts)
@@ -360,20 +427,37 @@
             grad = slope(early[s, 64 * x : 64 * x + 64].astype(f32))
             above = got[s, 128 + 64 * x : 192 + 64 * x].astype(f32)
             value = ((above + up[:, 128 * s : 128 * s + 128]) * grad).astype(bf)
-            at = (2 * s + x) * 64
-            for t in range(4):
-                out[t, at : at + 64] = value
-
-
-def finish(counts, pos, got, gj, pre, second_b, first_b, out, dom, gf):
+            mine[2 * s + x] = value
+    ra, rb = w & 1, n & 1
+    for t in range(4):
+        for k in range(2):
+            a = jnp.where(ra == t // 2, k, 1 - ra)
+            b = jnp.where(rb == t % 2, k, 1 - rb)
+            for x in range(2):
+                at = (2 * k + x) * 64
+                out[t, at : at + 64] = mine[(2 * a + b) * 2 + x]
+
+
+def finish(counts, pos, got, mine, gj, pre, second_b, strips, out, dom, gf, matrix):
+    square_matrix(strips, matrix)
     w, n = place(pos)
     ra, rb = w & 1, n & 1
 
-    def put(row, pair, tile):
-        dom[row, pair] = tile
-
-    spread_quadrants(got, 0, 64, w - ra - 1, n - rb - 1, counts, put)
-    own = [[dom[2 * ra + row, rb + p] for p in range(3)] for row in range(6)]
+    def put(x, y, tiles):
+        inside = flag(w + x - 1, counts[0]) * flag(n + y - 1, counts[1])
+        for i, tile in enumerate(tiles):
+            dom[2 * x + i, y] = (tile.astype(f32) * inside).astype(bf)
+
+    far_x, far_y = 2 * (1 - ra), 2 * (1 - rb)
+    part = lambda q, k: [got[q, (2 * k + i) * 64 : (2 * k + i) * 64 + 64] for i in range(2)]
+    for a in range(2):
+        for b in range(2):
+            put(a + ra, b + rb, [mine[(2 * a + b) * 2 + i] for i in range(2)])
+    for k in range(2):
+        put(far_x, k + rb, part(2 * (1 - ra) + rb, k))
+        put(k + ra, far_y, part(2 * ra + 1 - rb, k))
+    put(far_x, far_y, part(2 * (1 - ra) + 1 - rb, 0))
+    own = [[dom[row, p] for p in range(3)] for row in range(6)]
     mixed = [[cross(line[o], line[o + 1]) for o in range(2)] for line in own]
     grads = []
     for r in range(4):
@@ -385,8 +469,7 @@
             stack.append(rows_of(taps))
         grads += zsum(dot(second_b[...], cols_of(stack)), 32, 64)
     up = exact_up(rows_of(grads) * 0.125, pair_up())
-    fx = [flag(w - 1, counts[0]), None, None, None, None, flag(w + 1, counts[0])]
-    fy = [flag(n - 1, counts[1]), None, None, None, None, flag(n + 1, counts[1])]
+    fx, fy = edges(pos, counts)
     for x in range(6):
         for y in range(6):
             r, m = (x + 1) // 2, (y + 1) // 2
@@ -397,11 +480,10 @@
                 value = value if edge is None else value * edge
             gf[x, y] = value.astype(bf)
 
-    @pl.loop(0, 4)
-    def _(x):
-        prod = dot(first_b[...], cols_of([columns(gf, x, y) for y in range(4)]))
-        for y, value in enumerate(zsum(prod, 32, 128)):
-            out[x, y] = value.astype(bf)
+    @pl.loop(0, 2)
+    def _(i):
+        for dx, y, value in squares(matrix, gf, 2 * i, 4):
+            out[2 * i + dx, y] = value.astype(bf)
 
 
 def call(body, counts, outs, scratch, *args):
@@ -415,6 +497,7 @@
         scratch_shapes=[pltpu.VMEM(s, d) for s, d in scratch],
         compiler_params=pltpu.CompilerParams(vmem_limit_bytes=48 * 1024 * 1024),
         name=body.__name__,
+        cost_estimate=pl.CostEstimate(flops=400000000, bytes_accessed=2000000, transcendentals=0),
     )(*args)
 
 
@@ -460,46 +543,51 @@
     vol_l, vol_r = widened(vol, "wide", 0, 3)
     cot_l, cot_r = widened(cot, "wide", 0, 2)
 
-    full = (6, 6, 32, 128)
-    hid, pre, gj, content, p2 = call(
+    matrix = ((384, 512), bf)
+    full, cells = (6, 6, 32, 128), (4, 4, 32, 128)
+    hid, pre, content, p2 = call(
         encode, counts,
-        [(full, bf), (full, f32), (full, bf), ((192, 128), bf), ((64, 128), bf)],
-        [((10, 10, 32, 128), bf), ((8, 8, 32, 128), bf), ((8, 8, 32, 128), bf)],
-        pos, vol, vol_l, vol_r, cot, cot_l, cot_r,
-        forward_matrix(conv_first), forward_matrix(conv_second), backward_matrix(conv_final),
-    )
-    four = gathered(jnp.broadcast_to(p2, (4, 64, 128)), 0)
+        [(full, bf), (full, f32), ((128, 128), bf), ((4, 64, 128), bf)],
+        [((10, 10, 32, 128), bf), ((8, 8, 32, 128), bf), ((8, 6, 32, 128), f32), matrix],
+        pos, vol, vol_l, vol_r, forward_strips(conv_first), forward_matrix(conv_second),
+    )
+    four = gathered(p2, 0)
+    gj, total = call(
+        adjoint, counts, [(full, bf), ((64, 128), bf)], [((8, 8, 32, 128), bf), matrix],
+        pos, cot, cot_l, cot_r, backward_strips(conv_final),
+    )
     seg = lax.broadcasted_iota(jnp.int32, (64, 128), 1) // 32
     packed = four[0]
     for q in range(1, 4):
         packed = jnp.where(seg == q, four[q], packed)
-    content = jnp.concatenate([content, packed], axis=0)
+    content = jnp.concatenate([content, total, packed], axis=0)
     early = gathered(jnp.broadcast_to(content, (4, 256, 128)), 1)
     (content,) = call(
-        bottom, counts, [((4, 896, 128), bf)], [],
+        bottom, counts, [((4, 736, 128), bf)], [],
         pos, early, forward_matrix(conv_bottom), lift_weight,
     )
     got = gathered(content, 0)
-    cells = (4, 4, 32, 128)
-    features, content = call(
-        decode, counts, [(cells, bf), ((4, 256, 128), bf)],
+    content, hidden = call(
+        decode, counts, [((4, 256, 128), bf), ((256, 128), bf)],
         [
-            ((8, 4, 64, 128), bf), ((8, 3, 64, 128), bf), ((8, 4, 32, 128), bf),
+            ((8, 4, 64, 128), bf), ((8, 3, 64, 128), bf), ((6, 4, 32, 128), bf),
             ((6, 3, 32, 128), f32), ((6, 3, 32, 128), bf), ((4, 2, 64, 128), bf),
-            (full, bf),
         ],
-        pos, got, hid, forward_matrix(conv_decode), backward_matrix(conv_decode),
-        lift_weight.T, forward_matrix(conv_final),
+        pos, got, forward_matrix(conv_decode), backward_matrix(conv_decode), lift_weight.T,
     )
     got = gathered(content, 1)
-    (content,) = call(
-        deep_gradient, counts, [((4, 512, 128), bf)], [],
+    (features,) = call(
+        output, counts, [(cells, bf)], [(full, bf), matrix],
+        pos, hidden, hid, forward_strips(conv_final),
+    )
+    content, mine = call(
+        deep_gradient, counts, [((4, 256, 128), bf), ((8, 64, 128), bf)], [],
         pos, got, early, backward_matrix(conv_bottom),
     )
     got = gathered(content, 0)
     (grad,) = call(
-        finish, counts, [(cells, bf)], [((8, 4, 64, 128), bf), (full, bf)],
-        pos, got, gj, pre, backward_matrix(conv_second), backward_matrix(conv_first),
+        finish, counts, [(cells, bf)], [((6, 3, 64, 128), bf), (full, bf), matrix],
+        pos, got, mine, gj, pre, backward_matrix(conv_second), backward_strips(conv_first),
     )
     return features.transpose(2, 0, 1, 3), grad.transpose(2, 0, 1, 3)
 

time: 132 us -> 118 us (0.89)
  waiting for transfers between devices: 34.6 us -> 19.3 us
  starting transfers between devices: 60.7 us -> 65.3 us
  local copies, waits for them, and re-layouts: 14.6 us -> 11.7 us
    ppermute x8, waiting for transfers between devices: 9.11 us -> 0.02 us  [send(): return lax.ppermute(cells, axis, pairs)]
    all_to_all x5, waiting for transfers between devices: 25.5 us -> 19.3 us  [gathered(): lax.all_to_all(content, ('wide', 'narrow'), 0, 0, axis_index_groups=groups)]
    all_to_all x5, starting transfers between devices: 35.1 us -> 40.3 us  [gathered(): lax.all_to_all(content, ('wide', 'narrow'), 0, 0, axis_index_groups=groups)]
    reshape x7 -> x5, local copies, waits for them, and re-layouts: 5.12 us -> 3.7 us  [forward_matrix(): return kernel.transpose(2, 4, 0, 1, 3).reshape(3 * outs, 9 * chans)]
    pallas_call x5 -> x7, Pallas kernels: 20.1 us -> 19.8 us  [call(): pl.pallas_call(functools.partial(body, counts), out_shape=[jax.ShapeDtype...]
  transfers between devices with their start and end apart: 13 -> 13, of which waited for: 7 -> 5; matrix products, arithmetic and copies ran while one was open for 9% -> 8% of each run, Pallas kernels for 0% -> 7%
where the time goes in v2:
time: 118 us; the launch traced here: 117 us
  starting transfers between devices  65.3 us (55%)
  Pallas kernels  19.8 us (17%)
  waiting for transfers between devices  19.3 us (16%)
  local copies, waits for them, and re-layouts  11.7 us (10%)
    all_to_all x5, starting transfers between devices, gathered(): lax.all_to_all(content, ('wide', 'narrow'), 0, 0, axis_index_groups=groups)  40.3 us
    ppermute x8, starting transfers between devices, send(): return lax.ppermute(cells, axis, pairs)  25 us
    pallas_call x7, Pallas kernels, call(): pl.pallas_call(functools.partial(body, counts), out_shape=[jax.ShapeDtype...  19.8 us
    all_to_all x5, waiting for transfers between devices, gathered(): lax.all_to_all(content, ('wide', 'narrow'), 0, 0, axis_index_groups=groups)  19.3 us
    unnamed x21, local copies, waits for them, and re-layouts  3.71 us
    reshape x5, local copies, waits for them, and re-layouts, forward_matrix(): return kernel.transpose(2, 4, 0, 1, 3).reshape(3 * outs, 9 * chans)  3.7 us
  transfers between devices with their start and end apart: 13, of which 5 were waited for; matrix products, arithmetic and copies ran while one was open for 8% of the time, Pallas kernels for 7%

profile of v2, /device:TPU:1, one launch (start us, length us, event | category | flops | bytes accessed | tf_op | source)
XLA Modules:
  0.0 117.3 jit_solution(2070517365030740042)
XLA Ops:
  0.7 1.0 copy.48
  1.7 4.0 %collective-permute-start = (bf16[4,3,32,128]{3,2,1,0:T(8,128)(2,1)S(1)}, bf16[4,3,32,128]{3,2,1,0:T(8,128)(2,1)S(1)}, u32[]{:S(2)}, u32[]{:S(2)}) collective-permute-start(bf16[4,3,32,128]{3,2,1,0:T(8,128)(2,1)S(1)} %get-tuple-element.32), channel_id=1, source_target_pairs={{0,1},{1,2},{2,3},{3,4},{4,5},{5,6},{6,7},{7,8},{8,9},{9,10},{10,1... | collective-permute-start | bytes 294920 | tf_op jit(solution)/shard_map/ppermute | solution.py:507
  5.7 1.3 %collective-permute-start.1 = (bf16[4,3,32,128]{3,2,1,0:T(8,128)(2,1)S(1)}, bf16[4,3,32,128]{3,2,1,0:T(8,128)(2,1)S(1)}, u32[]{:S(2)}, u32[]{:S(2)}) collective-permute-start(bf16[4,3,32,128]{3,2,1,0:T(8,128)(2,1)S(1)} %get-tuple-element.33), channel_id=1, source_target_pairs={{1,0},{2,1},{3,2},{4,3},{5,4},{6,5},{7,6},{8,7},{9,8},{10,9},{11,1... | collective-permute-start | bytes 294920 | tf_op jit(solution)/shard_map/ppermute | solution.py:507
  7.0 0.9 copy.47
  8.0 4.6 %collective-permute-start.4 = (bf16[4,2,32,128]{3,2,1,0:T(8,128)(2,1)S(1)}, bf16[4,2,32,128]{3,2,1,0:T(8,128)(2,1)S(1)}, u32[]{:S(2)}, u32[]{:S(2)}) collective-permute-start(bf16[4,2,32,128]{3,2,1,0:T(8,128)(2,1)S(1)} %get-tuple-element.30), channel_id=1, source_target_pairs={{0,1},{1,2},{2,3},{3,4},{4,5},{5,6},{6,7},{7,8},{8,9},{9,10},{10,1... | collective-permute-start | bytes 196616 | tf_op jit(solution)/shard_map/ppermute | solution.py:507
  12.6 1.3 %collective-permute-start.5 = (bf16[4,2,32,128]{3,2,1,0:T(8,128)(2,1)S(1)}, bf16[4,2,32,128]{3,2,1,0:T(8,128)(2,1)S(1)}, u32[]{:S(2)}, u32[]{:S(2)}) collective-permute-start(bf16[4,2,32,128]{3,2,1,0:T(8,128)(2,1)S(1)} %get-tuple-element.31), channel_id=1, source_target_pairs={{1,0},{2,1},{3,2},{4,3},{5,4},{6,5},{7,6},{8,7},{9,8},{10,9},{11,1... | collective-permute-start | bytes 196616 | tf_op jit(solution)/shard_map/ppermute | solution.py:507
  14.1 0.2 reshape.35
  14.5 0.2 copy.26
  14.7 0.2 reshape.34.strips
  14.9 0.2 copy.30
  15.1 0.2 reshape.36.strips
  15.4 5.3 %collective-permute-start.2 = (bf16[3,10,32,128]{3,2,1,0:T(8,128)(2,1)S(1)}, bf16[3,10,32,128]{3,2,1,0:T(8,128)(2,1)S(1)}, u32[]{:S(2)}, u32[]{:S(2)}) collective-permute-start(bf16[3,10,32,128]{3,2,1,0:T(8,128)(2,1)S(1)} %get-tuple-element.27), channel_id=1, source_target_pairs={{0,16},{16,32},{32,48},{48,64},{64,80},{80,96},{96,112},{112,128},... | collective-permute-start | bytes 737288 | tf_op jit(solution)/shard_map/ppermute | solution.py:507
  20.8 2.0 %collective-permute-start.3 = (bf16[3,10,32,128]{3,2,1,0:T(8,128)(2,1)S(1)}, bf16[3,10,32,128]{3,2,1,0:T(8,128)(2,1)S(1)}, u32[]{:S(2)}, u32[]{:S(2)}) collective-permute-start(bf16[3,10,32,128]{3,2,1,0:T(8,128)(2,1)S(1)} %get-tuple-element.26), channel_id=1, source_target_pairs={{16,0},{32,16},{48,32},{64,48},{80,64},{96,80},{112,96},{128,112},... | collective-permute-start | bytes 737288 | tf_op jit(solution)/shard_map/ppermute | solution.py:507
  22.9 4.4 %collective-permute-start.6 = (bf16[2,8,32,128]{3,2,1,0:T(8,128)(2,1)S(1)}, bf16[2,8,32,128]{3,2,1,0:T(8,128)(2,1)S(1)}, u32[]{:S(2)}, u32[]{:S(2)}) collective-permute-start(bf16[2,8,32,128]{3,2,1,0:T(8,128)(2,1)S(1)} %get-tuple-element.29), channel_id=1, source_target_pairs={{0,16},{16,32},{32,48},{48,64},{64,80},{80,96},{96,112},{112,128},... | collective-permute-start | bytes 393224 | tf_op jit(solution)/shard_map/ppermute | solution.py:507
  27.4 1.9 %collective-permute-start.7 = (bf16[2,8,32,128]{3,2,1,0:T(8,128)(2,1)S(1)}, bf16[2,8,32,128]{3,2,1,0:T(8,128)(2,1)S(1)}, u32[]{:S(2)}, u32[]{:S(2)}) collective-permute-start(bf16[2,8,32,128]{3,2,1,0:T(8,128)(2,1)S(1)} %get-tuple-element.28), channel_id=1, source_target_pairs={{16,0},{32,16},{48,32},{64,48},{80,64},{96,80},{112,96},{128,112},... | collective-permute-start | bytes 393224 | tf_op jit(solution)/shard_map/ppermute | solution.py:507
  29.3 4.1 %encode.1 = (bf16[6,6,32,128]{3,2,1,0:T(8,128)(2,1)S(1)}, f32[6,6,32,128]{3,2,1,0:T(8,128)S(1)}, bf16[128,128]{1,0:T(8,128)(2,1)S(1)}, bf16[4,64,128]{2,1,0:T(8,128)(2,1)}) custom-call(s32[2]{0:T(128)S(1)} %pad_add_fusion.pos, bf16[4,10,32,128]{3,2,1,0:T(8,128)(2,1)S(1)} %pad_maximum_fusion.vol, bf16[3,10,32,128]{3,2,1,0:T(8,128)(2,1)S(1)} %collective-permute-done.2.vol_l, ...), custom_call_target="tpu_custom_call" | custom-call | flops 400000000 | bytes 2000000 | tf_op jit(solution)/shard_map/encode/pallas_call | solution.py:492
  33.4 7.6 %all-to-all-start = ((bf16[4,64,128]{2,1,0:T(8,128)(2,1)}), bf16[4,64,128]{2,1,0:T(8,128)(2,1)S(1)}, u32[]{:S(2)}, u32[]{:S(2)}) async-start(bf16[4,64,128]{2,1,0:T(8,128)(2,1)} %get-tuple-element.14), calls=%async_computation | async-start | bytes 131072 | tf_op jit(solution)/shard_map/all_to_all | solution.py:533
  41.0 2.2 %adjoint.1 = (bf16[6,6,32,128]{3,2,1,0:T(8,128)(2,1)S(1)}, bf16[64,128]{1,0:T(8,128)(2,1)S(1)}) custom-call(s32[2]{0:T(128)S(1)} %pad_add_fusion.pos, bf16[4,8,32,128]{3,2,1,0:T(8,128)(2,1)S(1)} %pad_maximum_fusion.1.cot, bf16[2,8,32,128]{3,2,1,0:T(8,128)(2,1)S(1)} %collective-permute-done.6.cot_l, bf16[2,8,32,128]{3,2,1,0:T(8,128)(2,1)S(1)} %collective-permute-done.7.cot_r, ...), custom_call_target="tpu_custom_call" | custom-call | flops 400000000 | bytes 2000000 | tf_op jit(solution)/shard_map/adjoint/pallas_call | solution.py:492
  43.2 1.0 all-to-all-done
  44.3 0.7 broadcast_in_dim.3
  45.0 13.5 %all-to-all-start.1 = ((bf16[4,256,128]{2,1,0:T(8,128)(2,1)}), bf16[4,256,128]{2,1,0:T(8,128)(2,1)S(1)}, u32[]{:S(2)}, u32[]{:S(2)}) async-start(bf16[4,256,128]{2,1,0:T(8,128)(2,1)} %broadcast_in_dim.3), calls=%async_computation.1 | async-start | bytes 524288 | tf_op jit(solution)/shard_map/all_to_all | solution.py:533
  58.5 2.3 %copy.43 = bf16[3,128,3,3,64]{4,3,2,1,0:T(4,128)(2,1)S(1)} copy(bf16[3,128,3,3,64]{1,4,0,3,2:T(8,128)(2,1)} %bitcast.49) | data formatting | bytes 884736 | tf_op jit(solution)/shard_map/reshape | solution.py:16
  60.8 0.8 reshape.44.weight
  61.7 2.6 %all-to-all-done.1.got.early = bf16[4,256,128]{2,1,0:T(8,128)(2,1)S(1)} async-done(((bf16[4,256,128]{2,1,0:T(8,128)(2,1)}), bf16[4,256,128]{2,1,0:T(8,128)(2,1)S(1)}, u32[]{:S(2)}, u32[]{:S(2)}) %all-to-all-start.1) | async-done | bytes 262176 | tf_op jit(solution)/shard_map/all_to_all | solution.py:533
  64.3 2.2 %bottom.1 = bf16[4,736,128]{2,1,0:T(8,128)(2,1)} custom-call(s32[2]{0:T(128)S(1)} %pad_add_fusion.pos, bf16[4,256,128]{2,1,0:T(8,128)(2,1)S(1)} %all-to-all-done.1.got.early, bf16[384,576]{1,0:T(8,128)(2,1)S(1)} %reshape.44.weight, bf16[64,128]{1,0:T(8,128)(2,1)S(1)} %copy-done), custom_call_target="tpu_custom_call" | custom-call | flops 400000000 | bytes 2000000 | tf_op jit(solution)/shard_map/bottom/pallas_call | solution.py:492
  66.5 5.3 %all-to-all-start.2 = ((bf16[4,736,128]{2,1,0:T(8,128)(2,1)}), bf16[4,736,128]{2,1,0:T(8,128)(2,1)S(1)}, u32[]{:S(2)}, u32[]{:S(2)}) async-start(bf16[4,736,128]{2,1,0:T(8,128)(2,1)} %bottom.1), calls=%async_computation.2 | async-start | bytes 1507328 | tf_op jit(solution)/shard_map/all_to_all | solution.py:533
  72.1 0.2 reshape.39
  72.5 0.2 copy.33
  72.6 0.2 reshape.38.weight
  72.9 9.2 %all-to-all-done.2.got = bf16[4,736,128]{2,1,0:T(8,128)(2,1)S(1)} async-done(((bf16[4,736,128]{2,1,0:T(8,128)(2,1)}), bf16[4,736,128]{2,1,0:T(8,128)(2,1)S(1)}, u32[]{:S(2)}, u32[]{:S(2)}) %all-to-all-start.2) | async-done | bytes 753696 | tf_op jit(solution)/shard_map/all_to_all | solution.py:533
  82.1 5.8 %decode.1 = (bf16[4,256,128]{2,1,0:T(8,128)(2,1)}, bf16[256,128]{1,0:T(8,128)(2,1)S(1)}) custom-call(s32[2]{0:T(128)S(1)} %pad_add_fusion.pos, bf16[4,736,128]{2,1,0:T(8,128)(2,1)S(1)} %all-to-all-done.2.got, bf16[96,576]{1,0:T(8,128)(2,1)S(1)} %reshape.38.weight, bf16[192,288]{1,0:T(8,128)(2,1)S(1)} %copy.36.weight_b, bf16[128,64]{1,0:T(8,128)(2,1)S(1)} %bitcast.48), custom_call_target="tpu_custom_call" | custom-call | flops 400000000 | bytes 2000000 | tf_op jit(solution)/shard_map/decode/pallas_call | solution.py:492
  87.9 7.0 %all-to-all-start.3 = ((bf16[4,256,128]{2,1,0:T(8,128)(2,1)}), bf16[4,256,128]{2,1,0:T(8,128)(2,1)S(1)}, u32[]{:S(2)}, u32[]{:S(2)}) async-start(bf16[4,256,128]{2,1,0:T(8,128)(2,1)} %get-tuple-element.17), calls=%async_computation.3 | async-start | bytes 524288 | tf_op jit(solution)/shard_map/all_to_all | solution.py:533
  94.9 0.4 copy.38
  95.3 0.4 reshape.41.weight
  95.6 4.9 %all-to-all-done.3.got = bf16[4,256,128]{2,1,0:T(8,128)(2,1)S(1)} async-done(((bf16[4,256,128]{2,1,0:T(8,128)(2,1)}), bf16[4,256,128]{2,1,0:T(8,128)(2,1)S(1)}, u32[]{:S(2)}, u32[]{:S(2)}) %all-to-all-start.3) | async-done | bytes 262176 | tf_op jit(solution)/shard_map/all_to_all | solution.py:533
  100.5 1.9 %deep_gradient.1 = (bf16[4,256,128]{2,1,0:T(8,128)(2,1)}, bf16[8,64,128]{2,1,0:T(8,128)(2,1)S(1)}) custom-call(s32[2]{0:T(128)S(1)} %pad_add_fusion.pos, bf16[4,256,128]{2,1,0:T(8,128)(2,1)S(1)} %all-to-all-done.3.got, bf16[4,256,128]{2,1,0:T(8,128)(2,1)S(1)} %all-to-all-done.1.got.early, bf16[192,1152]{1,0:T(8,128)(2,1)S(1)} %reshape.41.weight), custom_call_target="tpu_custom_call" | custom-call | flops 400000000 | bytes 2000000 | tf_op jit(solution)/shard_map/deep_gradient/pallas_call | solution.py:492
  102.4 7.1 %all-to-all-start.4 = ((bf16[4,256,128]{2,1,0:T(8,128)(2,1)}), bf16[4,256,128]{2,1,0:T(8,128)(2,1)S(1)}, u32[]{:S(2)}, u32[]{:S(2)}) async-start(bf16[4,256,128]{2,1,0:T(8,128)(2,1)} %get-tuple-element.18), calls=%async_computation.4 | async-start | bytes 524288 | tf_op jit(solution)/shard_map/all_to_all | solution.py:533
  109.5 0.2 copy.39
  109.7 0.2 reshape.42.second_b
  110.1 0.2 reshape.43.strips
  110.2 0.2 copy-done.7
  110.4 0.2 copy.37
  110.6 0.2 reshape.40.strips
  110.8 1.4 %output.1 = bf16[4,4,32,128]{3,2,1,0:T(8,128)(2,1)S(1)} custom-call(s32[2]{0:T(128)S(1)} %pad_add_fusion.pos, bf16[256,128]{1,0:T(8,128)(2,1)S(1)} %get-tuple-element.15.hidden, bf16[6,6,32,128]{3,2,1,0:T(8,128)(2,1)S(1)} %get-tuple-element.16.hid, bf16[3,96,96]{2,1,0:T(8,128)(2,1)S(1)} %reshape.40.strips), custom_call_target="tpu_custom_call" | custom-call | flops 400000000 | bytes 2000000 | tf_op jit(solution)/shard_map/output/pallas_call | solution.py:492
  112.2 0.7 copy.41
  113.0 1.5 %all-to-all-done.4.got = bf16[4,256,128]{2,1,0:T(8,128)(2,1)S(1)} async-done(((bf16[4,256,128]{2,1,0:T(8,128)(2,1)}), bf16[4,256,128]{2,1,0:T(8,128)(2,1)S(1)}, u32[]{:S(2)}, u32[]{:S(2)}) %all-to-all-start.4) | async-done | bytes 262176 | tf_op jit(solution)/shard_map/all_to_all | solution.py:533
  114.5 2.1 %finish.1 = bf16[4,4,32,128]{3,2,1,0:T(8,128)(2,1)S(1)} custom-call(s32[2]{0:T(128)S(1)} %pad_add_fusion.pos, bf16[4,256,128]{2,1,0:T(8,128)(2,1)S(1)} %all-to-all-done.4.got, bf16[8,64,128]{2,1,0:T(8,128)(2,1)S(1)} %get-tuple-element.19.mine, bf16[6,6,32,128]{3,2,1,0:T(8,128)(2,1)S(1)} %get-tuple-element.20.gj, ...), custom_call_target="tpu_custom_call" | custom-call | flops 400000000 | bytes 2000000 | tf_op jit(solution)/shard_map/finish/pallas_call | solution.py:492
  116.6 0.7 copy.42
  (45 shorter events, 1.3 us)
Async XLA Ops:
  0.6 13.3 %copy-start.3 = (bf16[3,3,3,32,64]{4,3,2,1,0:T(8,128)(2,1)S(1)}, bf16[3,3,3,32,64]{4,3,2,1,0:T(8,128)(2,1)}, u32[]{:S(2)}) copy-start(bf16[3,3,3,32,64]{4,3,2,1,0:T(8,128)(2,1)} %param.11) | copy-start | bytes 331780
  0.6 13.8 %copy-start.4 = (bf16[3,3,3,32,32]{4,3,2,1,0:T(8,128)(2,1)S(1)}, bf16[3,3,3,32,32]{4,3,2,1,0:T(8,128)(2,1)}, u32[]{:S(2)}) copy-start(bf16[3,3,3,32,32]{4,3,2,1,0:T(8,128)(2,1)} %param.10) | copy-start | bytes 165892
  1.7 13.6 %collective-permute-start = (bf16[4,3,32,128]{3,2,1,0:T(8,128)(2,1)S(1)}, bf16[4,3,32,128]{3,2,1,0:T(8,128)(2,1)S(1)}, u32[]{:S(2)}, u32[]{:S(2)}) collective-permute-start(bf16[4,3,32,128]{3,2,1,0:T(8,128)(2,1)S(1)} %get-tuple-element.32), channel_id=1, source_target_pairs={{0,1},{1,2},{2,3},{3,4},{4,5},{5,6},{6,7},{7,8},{8,9},{9,10},{10,1... | collective-permute-start | bytes 294920 | tf_op jit(solution)/shard_map/ppermute | solution.py:507
  5.7 9.6 %collective-permute-start.1 = (bf16[4,3,32,128]{3,2,1,0:T(8,128)(2,1)S(1)}, bf16[4,3,32,128]{3,2,1,0:T(8,128)(2,1)S(1)}, u32[]{:S(2)}, u32[]{:S(2)}) collective-permute-start(bf16[4,3,32,128]{3,2,1,0:T(8,128)(2,1)S(1)} %get-tuple-element.33), channel_id=1, source_target_pairs={{1,0},{2,1},{3,2},{4,3},{5,4},{6,5},{7,6},{8,7},{9,8},{10,9},{11,1... | collective-permute-start | bytes 294920 | tf_op jit(solution)/shard_map/ppermute | solution.py:507
  8.0 6.9 %copy-start.6 = (bf16[3,3,3,32,32]{4,3,2,1,0:T(8,128)(2,1)S(1)}, bf16[3,3,3,32,32]{4,3,2,1,0:T(8,128)(2,1)}, u32[]{:S(2)}) copy-start(bf16[3,3,3,32,32]{4,3,2,1,0:T(8,128)(2,1)} %param.15) | copy-start | bytes 165892
  8.0 14.8 %collective-permute-start.4 = (bf16[4,2,32,128]{3,2,1,0:T(8,128)(2,1)S(1)}, bf16[4,2,32,128]{3,2,1,0:T(8,128)(2,1)S(1)}, u32[]{:S(2)}, u32[]{:S(2)}) collective-permute-start(bf16[4,2,32,128]{3,2,1,0:T(8,128)(2,1)S(1)} %get-tuple-element.30), channel_id=1, source_target_pairs={{0,1},{1,2},{2,3},{3,4},{4,5},{5,6},{6,7},{7,8},{8,9},{9,10},{10,1... | collective-permute-start | bytes 196616 | tf_op jit(solution)/shard_map/ppermute | solution.py:507
  12.6 10.2 %collective-permute-start.5 = (bf16[4,2,32,128]{3,2,1,0:T(8,128)(2,1)S(1)}, bf16[4,2,32,128]{3,2,1,0:T(8,128)(2,1)S(1)}, u32[]{:S(2)}, u32[]{:S(2)}) collective-permute-start(bf16[4,2,32,128]{3,2,1,0:T(8,128)(2,1)S(1)} %get-tuple-element.31), channel_id=1, source_target_pairs={{1,0},{2,1},{3,2},{4,3},{5,4},{6,5},{7,6},{8,7},{9,8},{10,9},{11,1... | collective-permute-start | bytes 196616 | tf_op jit(solution)/shard_map/ppermute | solution.py:507
  15.4 13.8 %collective-permute-start.2 = (bf16[3,10,32,128]{3,2,1,0:T(8,128)(2,1)S(1)}, bf16[3,10,32,128]{3,2,1,0:T(8,128)(2,1)S(1)}, u32[]{:S(2)}, u32[]{:S(2)}) collective-permute-start(bf16[3,10,32,128]{3,2,1,0:T(8,128)(2,1)S(1)} %get-tuple-element.27), channel_id=1, source_target_pairs={{0,16},{16,32},{32,48},{48,64},{64,80},{80,96},{96,112},{112,128},... | collective-permute-start | bytes 737288 | tf_op jit(solution)/shard_map/ppermute | solution.py:507
  20.8 8.5 %collective-permute-start.3 = (bf16[3,10,32,128]{3,2,1,0:T(8,128)(2,1)S(1)}, bf16[3,10,32,128]{3,2,1,0:T(8,128)(2,1)S(1)}, u32[]{:S(2)}, u32[]{:S(2)}) collective-permute-start(bf16[3,10,32,128]{3,2,1,0:T(8,128)(2,1)S(1)} %get-tuple-element.26), channel_id=1, source_target_pairs={{16,0},{32,16},{48,32},{64,48},{80,64},{96,80},{112,96},{128,112},... | collective-permute-start | bytes 737288 | tf_op jit(solution)/shard_map/ppermute | solution.py:507
  22.9 18.1 %collective-permute-start.6 = (bf16[2,8,32,128]{3,2,1,0:T(8,128)(2,1)S(1)}, bf16[2,8,32,128]{3,2,1,0:T(8,128)(2,1)S(1)}, u32[]{:S(2)}, u32[]{:S(2)}) collective-permute-start(bf16[2,8,32,128]{3,2,1,0:T(8,128)(2,1)S(1)} %get-tuple-element.29), channel_id=1, source_target_pairs={{0,16},{16,32},{32,48},{48,64},{64,80},{80,96},{96,112},{112,128},... | collective-permute-start | bytes 393224 | tf_op jit(solution)/shard_map/ppermute | solution.py:507
  27.4 13.6 %collective-permute-start.7 = (bf16[2,8,32,128]{3,2,1,0:T(8,128)(2,1)S(1)}, bf16[2,8,32,128]{3,2,1,0:T(8,128)(2,1)S(1)}, u32[]{:S(2)}, u32[]{:S(2)}) collective-permute-start(bf16[2,8,32,128]{3,2,1,0:T(8,128)(2,1)S(1)} %get-tuple-element.28), channel_id=1, source_target_pairs={{16,0},{32,16},{48,32},{64,48},{80,64},{96,80},{112,96},{128,112},... | collective-permute-start | bytes 393224 | tf_op jit(solution)/shard_map/ppermute | solution.py:507
  33.4 10.8 %all-to-all-start = ((bf16[4,64,128]{2,1,0:T(8,128)(2,1)}), bf16[4,64,128]{2,1,0:T(8,128)(2,1)S(1)}, u32[]{:S(2)}, u32[]{:S(2)}) async-start(bf16[4,64,128]{2,1,0:T(8,128)(2,1)} %get-tuple-element.14), calls=%async_computation | async-start | bytes 131072 | tf_op jit(solution)/shard_map/all_to_all | solution.py:533
  45.0 19.2 %all-to-all-start.1 = ((bf16[4,256,128]{2,1,0:T(8,128)(2,1)}), bf16[4,256,128]{2,1,0:T(8,128)(2,1)S(1)}, u32[]{:S(2)}, u32[]{:S(2)}) async-start(bf16[4,256,128]{2,1,0:T(8,128)(2,1)} %broadcast_in_dim.3), calls=%async_computation.1 | async-start | bytes 524288 | tf_op jit(solution)/shard_map/all_to_all | solution.py:533
  60.8 3.5 %copy-start = (bf16[64,128]{1,0:T(8,128)(2,1)S(1)}, bf16[64,128]{1,0:T(8,128)(2,1)}, u32[]{:S(2)}) copy-start(bf16[64,128]{1,0:T(8,128)(2,1)} %lift.1) | copy-start | bytes 49156
  61.6 10.3 %copy-start.2 = (bf16[3,3,3,64,32]{3,4,2,1,0:T(8,128)(2,1)S(1)}, bf16[3,3,3,64,32]{3,4,2,1,0:T(8,128)(2,1)}, u32[]{:S(2)}) copy-start(bf16[3,3,3,64,32]{3,4,2,1,0:T(8,128)(2,1)} %param.14) | copy-start | bytes 331780
  66.5 15.6 %all-to-all-start.2 = ((bf16[4,736,128]{2,1,0:T(8,128)(2,1)}), bf16[4,736,128]{2,1,0:T(8,128)(2,1)S(1)}, u32[]{:S(2)}, u32[]{:S(2)}) async-start(bf16[4,736,128]{2,1,0:T(8,128)(2,1)} %bottom.1), calls=%async_computation.2 | async-start | bytes 1507328 | tf_op jit(solution)/shard_map/all_to_all | solution.py:533
  72.6 22.2 %copy-start.1 = (bf16[3,3,3,64,128]{4,3,2,1,0:T(8,128)(2,1)S(1)}, bf16[3,3,3,64,128]{4,3,2,1,0:T(8,128)(2,1)}, u32[]{:S(2)}) copy-start(bf16[3,3,3,64,128]{4,3,2,1,0:T(8,128)(2,1)} %param.12) | copy-start | bytes 1327108
  87.9 12.6 %all-to-all-start.3 = ((bf16[4,256,128]{2,1,0:T(8,128)(2,1)}), bf16[4,256,128]{2,1,0:T(8,128)(2,1)S(1)}, u32[]{:S(2)}, u32[]{:S(2)}) async-start(bf16[4,256,128]{2,1,0:T(8,128)(2,1)} %get-tuple-element.17), calls=%async_computation.3 | async-start | bytes 524288 | tf_op jit(solution)/shard_map/all_to_all | solution.py:533
  102.4 7.5 %copy-start.5 = (bf16[3,3,3,32,32]{4,3,2,1,0:T(8,128)(2,1)S(1)}, bf16[3,3,3,32,32]{4,3,2,1,0:T(8,128)(2,1)}, u32[]{:S(2)}) copy-start(bf16[3,3,3,32,32]{4,3,2,1,0:T(8,128)(2,1)} %param.10) | copy-start | bytes 165892
  102.4 12.1 %all-to-all-start.4 = ((bf16[4,256,128]{2,1,0:T(8,128)(2,1)}), bf16[4,256,128]{2,1,0:T(8,128)(2,1)S(1)}, u32[]{:S(2)}, u32[]{:S(2)}) async-start(bf16[4,256,128]{2,1,0:T(8,128)(2,1)} %get-tuple-element.18), calls=%async_computation.4 | async-start | bytes 524288 | tf_op jit(solution)/shard_map/all_to_all | solution.py:533
  109.5 0.9 copy-start.7

commit v3 on v2

--- a/solution.py
+++ b/solution.py
@@ -192,12 +192,27 @@
     return cols_of([field[x + i, y + j] for j in range(2) for i in range(2)])
 
 
+def beside(pos, full, mine, near, far):
+    rows = near.shape[0]
+    full[rows : rows + 4] = mine[...]
+    odd = pos[0] & 1
+
+    @pl.when(odd == 1)
+    def _():
+        full[0:rows] = near[...]
+        full[rows + 4 : 2 * rows + 4] = far[...]
+
+    @pl.when(odd == 0)
+    def _():
+        full[0:rows] = far[...]
+        full[rows + 4 : 2 * rows + 4] = near[...]
+
+
 def adjoint(counts, pos, cot, cot_l, cot_r, strips, gj, total, ec, matrix):
     square_matrix(strips, matrix)
-    ec[0:2], ec[2:6], ec[6:8] = cot_l[...], cot[...], cot_r[...]
-
-    @pl.loop(0, 3)
-    def _(i):
+    beside(pos, ec, cot, cot_l, cot_r)
+
+    for i in range(3):
         for dx, y, value in squares(matrix, ec, 2 * i, 6):
             gj[2 * i + dx, y] = value.astype(bf)
 
@@ -216,10 +231,9 @@
 ):
     square_matrix(strips, matrix)
     w, n = place(pos)
-    ev[0:3], ev[3:7], ev[7:10] = vol_l[...], vol[...], vol_r[...]
-
-    @pl.loop(0, 4)
-    def _(i):
+    beside(pos, ev, vol, vol_l, vol_r)
+
+    for i in range(4):
         for dx, y, value in squares(matrix, ev, 2 * i, 8):
             h8[2 * i + dx, y] = silu(value).astype(bf)
             if 1 <= y <= 6:
@@ -273,22 +287,19 @@
     for k in range(4):
         moved = pltpu.roll(grad[32 * k : 32 * k + 32], ((k - own) * 32) & 127, 1)
         packed = moved if packed is None else jnp.where(seg == k, moved, packed)
-    for t in range(4):
-        out[t, 512:544] = packed.astype(bf)
+    out[512:544] = packed.astype(bf)
     for s in range(4):
         for x in range(2):
             hidden = silu(got[s, 64 * x : 64 * x + 64].astype(f32)).astype(bf)
             joined = (up[:, 128 * s : 128 * s + 128] + hidden.astype(f32)).astype(bf)
             at = (2 * s + x) * 64
-            for t in range(4):
-                out[t, at : at + 64] = joined
+            out[at : at + 64] = joined
     for r in range(3):
         row = 1 - ra + r
         for b in range(2):
             start = pl.multiple_of(128 + 32 * (row & 1), 32)
-            sums = got[(row >> 1) * 2 + b, pl.ds(start, 32)]
-            for t in range(4):
-                out[t, 544 + 64 * r + 32 * b : 576 + 64 * r + 32 * b] = sums
+            at = 544 + 64 * r + 32 * b
+            out[at : at + 32] = got[(row >> 1) * 2 + b, pl.ds(start, 32)]
 
 
 def spread_quadrants(got, place_of, rows, base_x, base_y, counts, store):
@@ -310,10 +321,15 @@
 
 
 def decode(
-    counts, pos, got, weight, weight_b, lift_t, out, hidden, dom, mid, sums, pd, gd, gs
+    counts, pos, mine, chip, side, both, weight, weight_b, lift_t, out, hidden,
+    dom, mid, sums, pd, gd, gs, got,
 ):
     w, n = place(pos)
     ra, rb = w & 1, n & 1
+    got[2 * ra + rb] = mine[...]
+    got[2 * (1 - ra) + rb] = chip[...]
+    got[2 * ra + 1 - rb] = side[...]
+    got[2 * (1 - ra) + 1 - rb] = both[...]
     bx, by = w - ra - 1, n - rb - 1
 
     def put(row, pair, tile):
@@ -333,35 +349,33 @@
     spread_quadrants(got, joined_at, 64, bx, by, counts, put)
     spread_quadrants(got, sum_at, 32, bx, by, counts, put_sum)
 
-    @pl.loop(0, 8)
-    def _(row):
+    for row in range(8):
         for o in range(3):
             mid[row, o] = cross(dom[row, o], dom[row, o + 1])
 
-    @pl.loop(0, 6)
-    def _(i):
-        stack = []
+    stack = []
+    for i in range(6):
         for o in range(3):
             taps = []
             for dx in range(3):
                 taps += [dom[i + dx, o], mid[i + dx, o], dom[i + dx, o + 1]]
             stack.append(rows_of(taps))
-        for o, value in enumerate(zsum(dot(weight[...], cols_of(stack)), 32, 64)):
-            pd[i, o] = value
-            total = cross(sums[i, o].astype(f32), sums[i, o + 1].astype(f32))
-            gd[i, o] = (total * slope(value)).astype(bf)
-
-    @pl.loop(0, 4)
-    def _(j):
-        stack = []
+    for at, value in enumerate(zsum(dot(weight[...], cols_of(stack)), 32, 64)):
+        i, o = at // 3, at % 3
+        pd[i, o] = value
+        total = cross(sums[i, o].astype(f32), sums[i, o + 1].astype(f32))
+        gd[i, o] = (total * slope(value)).astype(bf)
+
+    stack = []
+    for j in range(4):
         for p in range(2):
             taps = []
             for dx in range(3):
                 left, right = gd[j + dx, p], gd[j + dx, p + 1]
                 taps += [left, cross(left, right), right]
             stack.append(rows_of(taps))
-        for p, value in enumerate(zsum(dot(weight_b[...], cols_of(stack)), 64, 64)):
-            gs[j, p] = value.astype(bf)
+    for at, value in enumerate(zsum(dot(weight_b[...], cols_of(stack)), 64, 64)):
+        gs[at // 2, at % 2] = value.astype(bf)
 
     parts = cols_of(
         [gs[2 * a + x, b] for a in range(2) for b in range(2) for x in range(2)]
@@ -409,8 +423,7 @@
                 value = value if edge is None else value * edge
             jf[x, y] = value.astype(bf)
 
-    @pl.loop(0, 2)
-    def _(i):
+    for i in range(2):
         for dx, y, value in squares(matrix, jf, 2 * i, 4):
             feat[2 * i + dx, y] = value.astype(bf)
 
@@ -459,15 +472,14 @@
     put(far_x, far_y, part(2 * (1 - ra) + 1 - rb, 0))
     own = [[dom[row, p] for p in range(3)] for row in range(6)]
     mixed = [[cross(line[o], line[o + 1]) for o in range(2)] for line in own]
-    grads = []
+    stack = []
     for r in range(4):
-        stack = []
         for o in range(2):
             taps = []
             for dx in range(3):
                 taps += [own[r + dx][o], mixed[r + dx][o], own[r + dx][o + 1]]
             stack.append(rows_of(taps))
-        grads += zsum(dot(second_b[...], cols_of(stack)), 32, 64)
+    grads = zsum(dot(second_b[...], cols_of(stack)), 32, 64)
     up = exact_up(rows_of(grads) * 0.125, pair_up())
     fx, fy = edges(pos, counts)
     for x in range(6):
@@ -480,8 +492,7 @@
                 value = value if edge is None else value * edge
             gf[x, y] = value.astype(bf)
 
-    @pl.loop(0, 2)
-    def _(i):
+    for i in range(2):
         for dx, y, value in squares(matrix, gf, 2 * i, 4):
             out[2 * i + dx, y] = value.astype(bf)
 
@@ -507,6 +518,14 @@
     return lax.ppermute(cells, axis, pairs)
 
 
+def swap(cells, axis, shift):
+    count = lax.axis_size(axis)
+    lower = range(shift, count - 1, 2)
+    return lax.ppermute(
+        cells, axis, [(i, i + 1) for i in lower] + [(i + 1, i) for i in lower]
+    )
+
+
 def widened(cells, axis, dim, width):
     size = cells.shape[dim]
     head = lax.slice_in_dim(cells, 0, width, axis=dim)
@@ -540,8 +559,17 @@
     cl, cr = widened(cot, "narrow", 1, 2)
     vol = jnp.concatenate([vl, vol, vr], axis=1)
     cot = jnp.concatenate([cl, cot, cr], axis=1)
-    vol_l, vol_r = widened(vol, "wide", 0, 3)
-    cot_l, cot_r = widened(cot, "wide", 0, 2)
+    odd = pos[0] & 1
+
+    def halves(cells, width):
+        start = 4 - width
+        near = lax.dynamic_slice_in_dim(cells, (1 - odd) * start, width, axis=0)
+        far = lax.dynamic_slice_in_dim(cells, odd * start, width, axis=0)
+        far = swap(far, "wide", 1)
+        return swap(near, "wide", 0), far
+
+    vol_l, vol_r = halves(vol, 3)
+    cot_l, cot_r = halves(cot, 2)
 
     matrix = ((384, 512), bf)
     full, cells = (6, 6, 32, 128), (4, 4, 32, 128)
@@ -563,17 +591,20 @@
     content = jnp.concatenate([content, total, packed], axis=0)
     early = gathered(jnp.broadcast_to(content, (4, 256, 128)), 1)
     (content,) = call(
-        bottom, counts, [((4, 736, 128), bf)], [],
+        bottom, counts, [((736, 128), bf)], [],
         pos, early, forward_matrix(conv_bottom), lift_weight,
     )
-    got = gathered(content, 0)
+    side = swap(content, "narrow", 0)
+    chip = swap(content, "wide", 0)
+    both = swap(side, "wide", 0)
     content, hidden = call(
         decode, counts, [((4, 256, 128), bf), ((256, 128), bf)],
         [
             ((8, 4, 64, 128), bf), ((8, 3, 64, 128), bf), ((6, 4, 32, 128), bf),
             ((6, 3, 32, 128), f32), ((6, 3, 32, 128), bf), ((4, 2, 64, 128), bf),
+            ((4, 736, 128), bf),
         ],
-        pos, got, forward_matrix(conv_decode), backward_matrix(conv_decode), lift_weight.T,
+        pos, content, chip, side, both, forward_matrix(conv_decode), backward_matrix(conv_decode), lift_weight.T,
     )
     got = gathered(content, 1)
     (features,) = call(

time: 118 us -> 110 us (0.932)
  Pallas kernels: 19.8 us -> 14.2 us
  waiting for transfers between devices: 19.3 us -> 16.3 us
    ppermute x0 -> x7, starting transfers between devices: none -> 29.3 us  [swap(): lax.ppermute(cells, axis, [(i, i + 1) for i in lower] + [(i + 1, i) for i...]
    all_to_all x5 -> x4, starting transfers between devices: 40.3 us -> 25.4 us  [gathered(): lax.all_to_all(content, ('wide', 'narrow'), 0, 0, axis_index_groups=groups)]
    ppermute x8 -> x4, starting transfers between devices: 25 us -> 11.1 us  [send(): return lax.ppermute(cells, axis, pairs)]
    all_to_all x5 -> x4, waiting for transfers between devices: 19.3 us -> 10.6 us  [gathered(): lax.all_to_all(content, ('wide', 'narrow'), 0, 0, axis_index_groups=groups)]
    ppermute x8 -> x4, waiting for transfers between devices: 0.02 us -> 5.73 us  [send(): return lax.ppermute(cells, axis, pairs)]
    pallas_call x7, Pallas kernels: 19.8 us -> 14.2 us  [call(): pl.pallas_call(functools.partial(body, counts), out_shape=[jax.ShapeDtype...]
    unnamed x21 -> x23, local copies, waits for them, and re-layouts: 3.71 us -> 3.71 us
  transfers between devices with their start and end apart: 13 -> 15, of which waited for: 5 -> 6; matrix products, arithmetic and copies ran while one was open for 8% -> 8% of each run, Pallas kernels for 7% -> 6%
where the time goes in v3:
time: 110 us; the launch traced here: 109 us
  starting transfers between devices  65.8 us (60%)
  waiting for transfers between devices  16.3 us (15%)
  Pallas kernels  14.2 us (13%)
  local copies, waits for them, and re-layouts  11.6 us (11%)
  between operations  1.17 us (1%)
    ppermute x7, starting transfers between devices, swap(): lax.ppermute(cells, axis, [(i, i + 1) for i in lower] + [(i + 1, i) for i...  29.3 us
    all_to_all x4, starting transfers between devices, gathered(): lax.all_to_all(content, ('wide', 'narrow'), 0, 0, axis_index_groups=groups)  25.4 us
    pallas_call x7, Pallas kernels, call(): pl.pallas_call(functools.partial(body, counts), out_shape=[jax.ShapeDtype...  14.2 us
    ppermute x4, starting transfers between devices, send(): return lax.ppermute(cells, axis, pairs)  11.1 us
    all_to_all x4, waiting for transfers between devices, gathered(): lax.all_to_all(content, ('wide', 'narrow'), 0, 0, axis_index_groups=groups)  10.6 us
    ppermute x4, waiting for transfers between devices, send(): return lax.ppermute(cells, axis, pairs)  5.73 us
    unnamed x23, local copies, waits for them, and re-layouts  3.71 us
    reshape x5, local copies, waits for them, and re-layouts, forward_matrix(): return kernel.transpose(2, 4, 0, 1, 3).reshape(3 * outs, 9 * chans)  3.7 us
  transfers between devices with their start and end apart: 15, of which 6 were waited for; matrix products, arithmetic and copies ran while one was open for 8% of the time, Pallas kernels for 6%

profile of v3, /device:TPU:1, one launch (start us, length us, event | category | flops | bytes accessed | tf_op | source)
XLA Modules:
  0.0 109.4 jit_solution(9895965398876243727)
XLA Ops:
  0.6 1.0 copy.47
  1.6 4.0 %collective-permute-start.4 = (bf16[4,2,32,128]{3,2,1,0:T(8,128)(2,1)S(1)}, bf16[4,2,32,128]{3,2,1,0:T(8,128)(2,1)S(1)}, u32[]{:S(2)}, u32[]{:S(2)}) collective-permute-start(bf16[4,2,32,128]{3,2,1,0:T(8,128)(2,1)S(1)} %get-tuple-element.30), channel_id=1, source_target_pairs={{0,1},{1,2},{2,3},{3,4},{4,5},{5,6},{6,7},{7,8},{8,9},{9,10},{10,1... | collective-permute-start | bytes 196616 | tf_op jit(solution)/shard_map/ppermute | solution.py:518
  5.7 1.3 %collective-permute-start.5 = (bf16[4,2,32,128]{3,2,1,0:T(8,128)(2,1)S(1)}, bf16[4,2,32,128]{3,2,1,0:T(8,128)(2,1)S(1)}, u32[]{:S(2)}, u32[]{:S(2)}) collective-permute-start(bf16[4,2,32,128]{3,2,1,0:T(8,128)(2,1)S(1)} %get-tuple-element.31), channel_id=1, source_target_pairs={{1,0},{2,1},{3,2},{4,3},{5,4},{6,5},{7,6},{8,7},{9,8},{10,9},{11,1... | collective-permute-start | bytes 196616 | tf_op jit(solution)/shard_map/ppermute | solution.py:518
  7.0 0.9 copy.48
  7.9 4.5 %collective-permute-start = (bf16[4,3,32,128]{3,2,1,0:T(8,128)(2,1)S(1)}, bf16[4,3,32,128]{3,2,1,0:T(8,128)(2,1)S(1)}, u32[]{:S(2)}, u32[]{:S(2)}) collective-permute-start(bf16[4,3,32,128]{3,2,1,0:T(8,128)(2,1)S(1)} %get-tuple-element.32), channel_id=1, source_target_pairs={{0,1},{1,2},{2,3},{3,4},{4,5},{5,6},{6,7},{7,8},{8,9},{9,10},{10,1... | collective-permute-start | bytes 294920 | tf_op jit(solution)/shard_map/ppermute | solution.py:518
  12.5 1.3 %collective-permute-start.1 = (bf16[4,3,32,128]{3,2,1,0:T(8,128)(2,1)S(1)}, bf16[4,3,32,128]{3,2,1,0:T(8,128)(2,1)S(1)}, u32[]{:S(2)}, u32[]{:S(2)}) collective-permute-start(bf16[4,3,32,128]{3,2,1,0:T(8,128)(2,1)S(1)} %get-tuple-element.33), channel_id=1, source_target_pairs={{1,0},{2,1},{3,2},{4,3},{5,4},{6,5},{7,6},{8,7},{9,8},{10,9},{11,1... | collective-permute-start | bytes 294920 | tf_op jit(solution)/shard_map/ppermute | solution.py:518
  13.8 0.3 collective-permute-done
  14.1 5.5 %collective-permute-done.1 = bf16[4,3,32,128]{3,2,1,0:T(8,128)(2,1)S(1)} collective-permute-done((bf16[4,3,32,128]{3,2,1,0:T(8,128)(2,1)S(1)}, bf16[4,3,32,128]{3,2,1,0:T(8,128)(2,1)S(1)}, u32[]{:S(2)}, u32[]{:S(2)}) %collective-permute-start.1) | collective-permute-done | bytes 98336 | tf_op jit(solution)/shard_map/ppermute | solution.py:518
  19.7 5.6 %collective-permute-start.2 = (bf16[3,10,32,128]{3,2,1,0:T(8,128)(2,1)S(1)}, bf16[3,10,32,128]{3,2,1,0:T(8,128)(2,1)S(1)}, u32[]{:S(2)}, u32[]{:S(2)}) collective-permute-start(bf16[3,10,32,128]{3,2,1,0:T(8,128)(2,1)S(1)} %get-tuple-element.27), channel_id=1, source_target_pairs={{0,16},{32,48},{64,80},{96,112},{128,144},{160,176},{192,208},{224... | collective-permute-start | bytes 737288 | tf_op jit(solution)/shard_map/ppermute | solution.py:524
  25.3 2.3 %collective-permute-start.3 = (bf16[3,10,32,128]{3,2,1,0:T(8,128)(2,1)S(1)}, bf16[3,10,32,128]{3,2,1,0:T(8,128)(2,1)S(1)}, u32[]{:S(2)}, u32[]{:S(2)}) collective-permute-start(bf16[3,10,32,128]{3,2,1,0:T(8,128)(2,1)S(1)} %get-tuple-element.26), channel_id=1, source_target_pairs={{16,32},{48,64},{80,96},{112,128},{144,160},{176,192},{208,224},{2... | collective-permute-start | bytes 737288 | tf_op jit(solution)/shard_map/ppermute | solution.py:524
  27.8 0.2 reshape.36.strips
  28.1 0.2 reshape.35
  28.5 0.2 copy.26
  28.7 0.2 reshape.34.strips
  29.0 1.9 %collective-permute-start.6 = (bf16[2,8,32,128]{3,2,1,0:T(8,128)(2,1)S(1)}, bf16[2,8,32,128]{3,2,1,0:T(8,128)(2,1)S(1)}, u32[]{:S(2)}, u32[]{:S(2)}) collective-permute-start(bf16[2,8,32,128]{3,2,1,0:T(8,128)(2,1)S(1)} %get-tuple-element.29), channel_id=1, source_target_pairs={{0,16},{32,48},{64,80},{96,112},{128,144},{160,176},{192,208},{224... | collective-permute-start | bytes 393224 | tf_op jit(solution)/shard_map/ppermute | solution.py:524
  30.9 5.8 %collective-permute-start.7 = (bf16[2,8,32,128]{3,2,1,0:T(8,128)(2,1)S(1)}, bf16[2,8,32,128]{3,2,1,0:T(8,128)(2,1)S(1)}, u32[]{:S(2)}, u32[]{:S(2)}) collective-permute-start(bf16[2,8,32,128]{3,2,1,0:T(8,128)(2,1)S(1)} %get-tuple-element.28), channel_id=1, source_target_pairs={{16,32},{48,64},{80,96},{112,128},{144,160},{176,192},{208,224},{2... | collective-permute-start | bytes 393224 | tf_op jit(solution)/shard_map/ppermute | solution.py:524
  36.8 3.4 %encode.1 = (bf16[6,6,32,128]{3,2,1,0:T(8,128)(2,1)S(1)}, f32[6,6,32,128]{3,2,1,0:T(8,128)S(1)}, bf16[128,128]{1,0:T(8,128)(2,1)S(1)}, bf16[4,64,128]{2,1,0:T(8,128)(2,1)}) custom-call(s32[2]{0:T(128)S(1)} %pad_add_fusion.pos, bf16[4,10,32,128]{3,2,1,0:T(8,128)(2,1)S(1)} %pad_maximum_fusion.vol, bf16[3,10,32,128]{3,2,1,0:T(8,128)(2,1)S(1)} %collective-permute-done.2.vol_l, ...), custom_call_target="tpu_custom_call" | custom-call | flops 400000000 | bytes 2000000 | tf_op jit(solution)/shard_map/encode/pallas_call | solution.py:503
  40.2 4.1 %all-to-all-start = ((bf16[4,64,128]{2,1,0:T(8,128)(2,1)}), bf16[4,64,128]{2,1,0:T(8,128)(2,1)S(1)}, u32[]{:S(2)}, u32[]{:S(2)}) async-start(bf16[4,64,128]{2,1,0:T(8,128)(2,1)} %get-tuple-element.14), calls=%async_computation | async-start | bytes 131072 | tf_op jit(solution)/shard_map/all_to_all | solution.py:552
  44.3 1.6 %adjoint.1 = (bf16[6,6,32,128]{3,2,1,0:T(8,128)(2,1)S(1)}, bf16[64,128]{1,0:T(8,128)(2,1)S(1)}) custom-call(s32[2]{0:T(128)S(1)} %pad_add_fusion.pos, bf16[4,8,32,128]{3,2,1,0:T(8,128)(2,1)S(1)} %pad_maximum_fusion.1.cot, bf16[2,8,32,128]{3,2,1,0:T(8,128)(2,1)S(1)} %collective-permute-done.6.cot_l, bf16[2,8,32,128]{3,2,1,0:T(8,128)(2,1)S(1)} %collective-permute-done.7.cot_r, ...), custom_call_target="tpu_custom_call" | custom-call | flops 400000000 | bytes 2000000 | tf_op jit(solution)/shard_map/adjoint/pallas_call | solution.py:503
  45.9 1.7 %all-to-all-done = bf16[4,64,128]{2,1,0:T(8,128)(2,1)S(1)} async-done(((bf16[4,64,128]{2,1,0:T(8,128)(2,1)}), bf16[4,64,128]{2,1,0:T(8,128)(2,1)S(1)}, u32[]{:S(2)}, u32[]{:S(2)}) %all-to-all-start) | async-done | bytes 65568 | tf_op jit(solution)/shard_map/all_to_all | solution.py:552
  47.6 0.7 broadcast_in_dim.3
  48.3 9.0 %all-to-all-start.1 = ((bf16[4,256,128]{2,1,0:T(8,128)(2,1)}), bf16[4,256,128]{2,1,0:T(8,128)(2,1)S(1)}, u32[]{:S(2)}, u32[]{:S(2)}) async-start(bf16[4,256,128]{2,1,0:T(8,128)(2,1)} %broadcast_in_dim.3), calls=%async_computation.1 | async-start | bytes 524288 | tf_op jit(solution)/shard_map/all_to_all | solution.py:552
  57.4 2.3 %copy.43 = bf16[3,128,3,3,64]{4,3,2,1,0:T(4,128)(2,1)S(1)} copy(bf16[3,128,3,3,64]{1,4,0,3,2:T(8,128)(2,1)} %bitcast.49) | data formatting | bytes 884736 | tf_op jit(solution)/shard_map/reshape | solution.py:16
  59.7 0.8 reshape.44.weight
  60.5 2.4 %all-to-all-done.1.got.early = bf16[4,256,128]{2,1,0:T(8,128)(2,1)S(1)} async-done(((bf16[4,256,128]{2,1,0:T(8,128)(2,1)}), bf16[4,256,128]{2,1,0:T(8,128)(2,1)S(1)}, u32[]{:S(2)}, u32[]{:S(2)}) %all-to-all-start.1) | async-done | bytes 262176 | tf_op jit(solution)/shard_map/all_to_all | solution.py:552
  62.9 1.3 %bottom.1.mine = bf16[736,128]{1,0:T(8,128)(2,1)S(1)} custom-call(s32[2]{0:T(128)S(1)} %pad_add_fusion.pos, bf16[4,256,128]{2,1,0:T(8,128)(2,1)S(1)} %all-to-all-done.1.got.early, bf16[384,576]{1,0:T(8,128)(2,1)S(1)} %reshape.44.weight, bf16[64,128]{1,0:T(8,128)(2,1)S(1)} %copy-done), custom_call_target="tpu_custom_call" | custom-call | flops 400000000 | bytes 2000000 | tf_op jit(solution)/shard_map/bottom/pallas_call | solution.py:503
  64.3 1.9 %collective-permute-start.9 = (bf16[736,128]{1,0:T(8,128)(2,1)S(1)}, bf16[736,128]{1,0:T(8,128)(2,1)S(1)}, u32[]{:S(2)}, u32[]{:S(2)}) collective-permute-start(bf16[736,128]{1,0:T(8,128)(2,1)S(1)} %bottom.1.mine), channel_id=1, source_target_pairs={{0,1},{2,3},{4,5},{6,7},{8,9},{10,11},{12,13},{14,15},{1,0},{3,2},... | collective-permute-start | bytes 565256 | tf_op jit(solution)/shard_map/ppermute | solution.py:524
  66.2 6.3 %collective-permute-start.8 = (bf16[736,128]{1,0:T(8,128)(2,1)S(1)}, bf16[736,128]{1,0:T(8,128)(2,1)S(1)}, u32[]{:S(2)}, u32[]{:S(2)}) collective-permute-start(bf16[736,128]{1,0:T(8,128)(2,1)S(1)} %bottom.1.mine), channel_id=1, source_target_pairs={{0,16},{32,48},{64,80},{96,112},{128,144},{160,176},{192,208},{224... | collective-permute-start | bytes 565256 | tf_op jit(solution)/shard_map/ppermute | solution.py:524
  72.5 5.5 %collective-permute-start.10 = (bf16[736,128]{1,0:T(8,128)(2,1)S(1)}, bf16[736,128]{1,0:T(8,128)(2,1)S(1)}, u32[]{:S(2)}, u32[]{:S(2)}) collective-permute-start(bf16[736,128]{1,0:T(8,128)(2,1)S(1)} %collective-permute-done.9.side), channel_id=1, source_target_pairs={{0,16},{32,48},{64,80},{96,112},{128,144},{160,176},{192,208},{224... | collective-permute-start | bytes 565256 | tf_op jit(solution)/shard_map/ppermute | solution.py:524
  78.3 0.2 reshape.39
  78.9 0.2 reshape.38.weight
  79.1 3.0 %decode.1 = (bf16[4,256,128]{2,1,0:T(8,128)(2,1)}, bf16[256,128]{1,0:T(8,128)(2,1)S(1)}) custom-call(s32[2]{0:T(128)S(1)} %pad_add_fusion.pos, bf16[736,128]{1,0:T(8,128)(2,1)S(1)} %bottom.1.mine, bf16[736,128]{1,0:T(8,128)(2,1)S(1)} %collective-permute-done.8.chip, bf16[736,128]{1,0:T(8,128)(2,1)S(1)} %collective-permute-done.9.side, ...), custom_call_target="tpu_custom_call" | custom-call | flops 400000000 | bytes 2000000 | tf_op jit(solution)/shard_map/decode/pallas_call | solution.py:503
  82.1 4.9 %all-to-all-start.2 = ((bf16[4,256,128]{2,1,0:T(8,128)(2,1)}), bf16[4,256,128]{2,1,0:T(8,128)(2,1)S(1)}, u32[]{:S(2)}, u32[]{:S(2)}) async-start(bf16[4,256,128]{2,1,0:T(8,128)(2,1)} %get-tuple-element.17), calls=%async_computation.2 | async-start | bytes 524288 | tf_op jit(solution)/shard_map/all_to_all | solution.py:552
  87.0 0.4 copy.38
  87.4 0.4 reshape.41.weight
  87.8 4.8 %all-to-all-done.2.got = bf16[4,256,128]{2,1,0:T(8,128)(2,1)S(1)} async-done(((bf16[4,256,128]{2,1,0:T(8,128)(2,1)}), bf16[4,256,128]{2,1,0:T(8,128)(2,1)S(1)}, u32[]{:S(2)}, u32[]{:S(2)}) %all-to-all-start.2) | async-done | bytes 262176 | tf_op jit(solution)/shard_map/all_to_all | solution.py:552
  92.6 1.9 %deep_gradient.1 = (bf16[4,256,128]{2,1,0:T(8,128)(2,1)}, bf16[8,64,128]{2,1,0:T(8,128)(2,1)S(1)}) custom-call(s32[2]{0:T(128)S(1)} %pad_add_fusion.pos, bf16[4,256,128]{2,1,0:T(8,128)(2,1)S(1)} %all-to-all-done.2.got, bf16[4,256,128]{2,1,0:T(8,128)(2,1)S(1)} %all-to-all-done.1.got.early, bf16[192,1152]{1,0:T(8,128)(2,1)S(1)} %reshape.41.weight), custom_call_target="tpu_custom_call" | custom-call | flops 400000000 | bytes 2000000 | tf_op jit(solution)/shard_map/deep_gradient/pallas_call | solution.py:503
  94.5 7.3 %all-to-all-start.3 = ((bf16[4,256,128]{2,1,0:T(8,128)(2,1)}), bf16[4,256,128]{2,1,0:T(8,128)(2,1)S(1)}, u32[]{:S(2)}, u32[]{:S(2)}) async-start(bf16[4,256,128]{2,1,0:T(8,128)(2,1)} %get-tuple-element.18), calls=%async_computation.3 | async-start | bytes 524288 | tf_op jit(solution)/shard_map/all_to_all | solution.py:552
  102.0 0.2 reshape.42.second_b
  102.5 0.2 reshape.43.strips
  102.6 0.2 copy-done.8
  102.8 0.2 copy.37
  103.0 0.2 reshape.40.strips
  103.2 1.2 %output.1 = bf16[4,4,32,128]{3,2,1,0:T(8,128)(2,1)S(1)} custom-call(s32[2]{0:T(128)S(1)} %pad_add_fusion.pos, bf16[256,128]{1,0:T(8,128)(2,1)S(1)} %get-tuple-element.15.hidden, bf16[6,6,32,128]{3,2,1,0:T(8,128)(2,1)S(1)} %get-tuple-element.16.hid, bf16[3,96,96]{2,1,0:T(8,128)(2,1)S(1)} %reshape.40.strips), custom_call_target="tpu_custom_call" | custom-call | flops 400000000 | bytes 2000000 | tf_op jit(solution)/shard_map/output/pallas_call | solution.py:503
  104.4 0.7 copy.41
  105.1 1.8 %all-to-all-done.3.got = bf16[4,256,128]{2,1,0:T(8,128)(2,1)S(1)} async-done(((bf16[4,256,128]{2,1,0:T(8,128)(2,1)}), bf16[4,256,128]{2,1,0:T(8,128)(2,1)S(1)}, u32[]{:S(2)}, u32[]{:S(2)}) %all-to-all-start.3) | async-done | bytes 262176 | tf_op jit(solution)/shard_map/all_to_all | solution.py:552
  106.9 1.8 %finish.1 = bf16[4,4,32,128]{3,2,1,0:T(8,128)(2,1)S(1)} custom-call(s32[2]{0:T(128)S(1)} %pad_add_fusion.pos, bf16[4,256,128]{2,1,0:T(8,128)(2,1)S(1)} %all-to-all-done.3.got, bf16[8,64,128]{2,1,0:T(8,128)(2,1)S(1)} %get-tuple-element.19.mine, bf16[6,6,32,128]{3,2,1,0:T(8,128)(2,1)S(1)} %get-tuple-element.20.gj, ...), custom_call_target="tpu_custom_call" | custom-call | flops 400000000 | bytes 2000000 | tf_op jit(solution)/shard_map/finish/pallas_call | solution.py:503
  108.7 0.7 copy.42
  (51 shorter events, 1.8 us)
Async XLA Ops:
  0.6 13.2 %copy-start.7 = (bf16[3,3,3,32,32]{4,3,2,1,0:T(8,128)(2,1)S(1)}, bf16[3,3,3,32,32]{4,3,2,1,0:T(8,128)(2,1)}, u32[]{:S(2)}) copy-start(bf16[3,3,3,32,32]{4,3,2,1,0:T(8,128)(2,1)} %param.15) | copy-start | bytes 165892
  1.6 27.3 %collective-permute-start.4 = (bf16[4,2,32,128]{3,2,1,0:T(8,128)(2,1)S(1)}, bf16[4,2,32,128]{3,2,1,0:T(8,128)(2,1)S(1)}, u32[]{:S(2)}, u32[]{:S(2)}) collective-permute-start(bf16[4,2,32,128]{3,2,1,0:T(8,128)(2,1)S(1)} %get-tuple-element.30), channel_id=1, source_target_pairs={{0,1},{1,2},{2,3},{3,4},{4,5},{5,6},{6,7},{7,8},{8,9},{9,10},{10,1... | collective-permute-start | bytes 196616 | tf_op jit(solution)/shard_map/ppermute | solution.py:518
  5.7 23.2 %collective-permute-start.5 = (bf16[4,2,32,128]{3,2,1,0:T(8,128)(2,1)S(1)}, bf16[4,2,32,128]{3,2,1,0:T(8,128)(2,1)S(1)}, u32[]{:S(2)}, u32[]{:S(2)}) collective-permute-start(bf16[4,2,32,128]{3,2,1,0:T(8,128)(2,1)S(1)} %get-tuple-element.31), channel_id=1, source_target_pairs={{1,0},{2,1},{3,2},{4,3},{5,4},{6,5},{7,6},{8,7},{9,8},{10,9},{11,1... | collective-permute-start | bytes 196616 | tf_op jit(solution)/shard_map/ppermute | solution.py:518
  7.9 6.1 %collective-permute-start = (bf16[4,3,32,128]{3,2,1,0:T(8,128)(2,1)S(1)}, bf16[4,3,32,128]{3,2,1,0:T(8,128)(2,1)S(1)}, u32[]{:S(2)}, u32[]{:S(2)}) collective-permute-start(bf16[4,3,32,128]{3,2,1,0:T(8,128)(2,1)S(1)} %get-tuple-element.32), channel_id=1, source_target_pairs={{0,1},{1,2},{2,3},{3,4},{4,5},{5,6},{6,7},{7,8},{8,9},{9,10},{10,1... | collective-permute-start | bytes 294920 | tf_op jit(solution)/shard_map/ppermute | solution.py:518
  12.5 7.1 %collective-permute-start.1 = (bf16[4,3,32,128]{3,2,1,0:T(8,128)(2,1)S(1)}, bf16[4,3,32,128]{3,2,1,0:T(8,128)(2,1)S(1)}, u32[]{:S(2)}, u32[]{:S(2)}) collective-permute-start(bf16[4,3,32,128]{3,2,1,0:T(8,128)(2,1)S(1)} %get-tuple-element.33), channel_id=1, source_target_pairs={{1,0},{2,1},{3,2},{4,3},{5,4},{6,5},{7,6},{8,7},{9,8},{10,9},{11,1... | collective-permute-start | bytes 294920 | tf_op jit(solution)/shard_map/ppermute | solution.py:518
  13.8 14.2 %copy-start.3 = (bf16[3,3,3,32,64]{4,3,2,1,0:T(8,128)(2,1)S(1)}, bf16[3,3,3,32,64]{4,3,2,1,0:T(8,128)(2,1)}, u32[]{:S(2)}) copy-start(bf16[3,3,3,32,64]{4,3,2,1,0:T(8,128)(2,1)} %param.11) | copy-start | bytes 331780
  19.7 8.9 %copy-start.5 = (bf16[3,3,3,32,32]{4,3,2,1,0:T(8,128)(2,1)S(1)}, bf16[3,3,3,32,32]{4,3,2,1,0:T(8,128)(2,1)}, u32[]{:S(2)}) copy-start(bf16[3,3,3,32,32]{4,3,2,1,0:T(8,128)(2,1)} %param.10) | copy-start | bytes 165892
  19.7 17.1 %collective-permute-start.2 = (bf16[3,10,32,128]{3,2,1,0:T(8,128)(2,1)S(1)}, bf16[3,10,32,128]{3,2,1,0:T(8,128)(2,1)S(1)}, u32[]{:S(2)}, u32[]{:S(2)}) collective-permute-start(bf16[3,10,32,128]{3,2,1,0:T(8,128)(2,1)S(1)} %get-tuple-element.27), channel_id=1, source_target_pairs={{0,16},{32,48},{64,80},{96,112},{128,144},{160,176},{192,208},{224... | collective-permute-start | bytes 737288 | tf_op jit(solution)/shard_map/ppermute | solution.py:524
  25.3 11.5 %collective-permute-start.3 = (bf16[3,10,32,128]{3,2,1,0:T(8,128)(2,1)S(1)}, bf16[3,10,32,128]{3,2,1,0:T(8,128)(2,1)S(1)}, u32[]{:S(2)}, u32[]{:S(2)}) collective-permute-start(bf16[3,10,32,128]{3,2,1,0:T(8,128)(2,1)S(1)} %get-tuple-element.26), channel_id=1, source_target_pairs={{16,32},{48,64},{80,96},{112,128},{144,160},{176,192},{208,224},{2... | collective-permute-start | bytes 737288 | tf_op jit(solution)/shard_map/ppermute | solution.py:524
  29.0 15.3 %collective-permute-start.6 = (bf16[2,8,32,128]{3,2,1,0:T(8,128)(2,1)S(1)}, bf16[2,8,32,128]{3,2,1,0:T(8,128)(2,1)S(1)}, u32[]{:S(2)}, u32[]{:S(2)}) collective-permute-start(bf16[2,8,32,128]{3,2,1,0:T(8,128)(2,1)S(1)} %get-tuple-element.29), channel_id=1, source_target_pairs={{0,16},{32,48},{64,80},{96,112},{128,144},{160,176},{192,208},{224... | collective-permute-start | bytes 393224 | tf_op jit(solution)/shard_map/ppermute | solution.py:524
  30.9 13.4 %collective-permute-start.7 = (bf16[2,8,32,128]{3,2,1,0:T(8,128)(2,1)S(1)}, bf16[2,8,32,128]{3,2,1,0:T(8,128)(2,1)S(1)}, u32[]{:S(2)}, u32[]{:S(2)}) collective-permute-start(bf16[2,8,32,128]{3,2,1,0:T(8,128)(2,1)S(1)} %get-tuple-element.28), channel_id=1, source_target_pairs={{16,32},{48,64},{80,96},{112,128},{144,160},{176,192},{208,224},{2... | collective-permute-start | bytes 393224 | tf_op jit(solution)/shard_map/ppermute | solution.py:524
  40.2 7.4 %all-to-all-start = ((bf16[4,64,128]{2,1,0:T(8,128)(2,1)}), bf16[4,64,128]{2,1,0:T(8,128)(2,1)S(1)}, u32[]{:S(2)}, u32[]{:S(2)}) async-start(bf16[4,64,128]{2,1,0:T(8,128)(2,1)} %get-tuple-element.14), calls=%async_computation | async-start | bytes 131072 | tf_op jit(solution)/shard_map/all_to_all | solution.py:552
  48.3 14.6 %all-to-all-start.1 = ((bf16[4,256,128]{2,1,0:T(8,128)(2,1)}), bf16[4,256,128]{2,1,0:T(8,128)(2,1)S(1)}, u32[]{:S(2)}, u32[]{:S(2)}) async-start(bf16[4,256,128]{2,1,0:T(8,128)(2,1)} %broadcast_in_dim.3), calls=%async_computation.1 | async-start | bytes 524288 | tf_op jit(solution)/shard_map/all_to_all | solution.py:552
  59.7 3.3 %copy-start = (bf16[64,128]{1,0:T(8,128)(2,1)S(1)}, bf16[64,128]{1,0:T(8,128)(2,1)}, u32[]{:S(2)}) copy-start(bf16[64,128]{1,0:T(8,128)(2,1)} %lift.1) | copy-start | bytes 49156
  60.5 17.6 %copy-start.2 = (bf16[3,3,3,64,32]{3,4,2,1,0:T(8,128)(2,1)S(1)}, bf16[3,3,3,64,32]{3,4,2,1,0:T(8,128)(2,1)}, u32[]{:S(2)}) copy-start(bf16[3,3,3,64,32]{3,4,2,1,0:T(8,128)(2,1)} %param.14) | copy-start | bytes 331780
  64.3 8.2 %collective-permute-start.9 = (bf16[736,128]{1,0:T(8,128)(2,1)S(1)}, bf16[736,128]{1,0:T(8,128)(2,1)S(1)}, u32[]{:S(2)}, u32[]{:S(2)}) collective-permute-start(bf16[736,128]{1,0:T(8,128)(2,1)S(1)} %bottom.1.mine), channel_id=1, source_target_pairs={{0,1},{2,3},{4,5},{6,7},{8,9},{10,11},{12,13},{14,15},{1,0},{3,2},... | collective-permute-start | bytes 565256 | tf_op jit(solution)/shard_map/ppermute | solution.py:524
  66.2 12.9 %collective-permute-start.8 = (bf16[736,128]{1,0:T(8,128)(2,1)S(1)}, bf16[736,128]{1,0:T(8,128)(2,1)S(1)}, u32[]{:S(2)}, u32[]{:S(2)}) collective-permute-start(bf16[736,128]{1,0:T(8,128)(2,1)S(1)} %bottom.1.mine), channel_id=1, source_target_pairs={{0,16},{32,48},{64,80},{96,112},{128,144},{160,176},{192,208},{224... | collective-permute-start | bytes 565256 | tf_op jit(solution)/shard_map/ppermute | solution.py:524
  72.5 6.6 %collective-permute-start.10 = (bf16[736,128]{1,0:T(8,128)(2,1)S(1)}, bf16[736,128]{1,0:T(8,128)(2,1)S(1)}, u32[]{:S(2)}, u32[]{:S(2)}) collective-permute-start(bf16[736,128]{1,0:T(8,128)(2,1)S(1)} %collective-permute-done.9.side), channel_id=1, source_target_pairs={{0,16},{32,48},{64,80},{96,112},{128,144},{160,176},{192,208},{224... | collective-permute-start | bytes 565256 | tf_op jit(solution)/shard_map/ppermute | solution.py:524
  78.9 8.1 %copy-start.1 = (bf16[3,3,3,64,128]{4,3,2,1,0:T(8,128)(2,1)S(1)}, bf16[3,3,3,64,128]{4,3,2,1,0:T(8,128)(2,1)}, u32[]{:S(2)}) copy-start(bf16[3,3,3,64,128]{4,3,2,1,0:T(8,128)(2,1)} %param.12) | copy-start | bytes 1327108
  82.1 10.5 %all-to-all-start.2 = ((bf16[4,256,128]{2,1,0:T(8,128)(2,1)}), bf16[4,256,128]{2,1,0:T(8,128)(2,1)S(1)}, u32[]{:S(2)}, u32[]{:S(2)}) async-start(bf16[4,256,128]{2,1,0:T(8,128)(2,1)} %get-tuple-element.17), calls=%async_computation.2 | async-start | bytes 524288 | tf_op jit(solution)/shard_map/all_to_all | solution.py:552
  87.8 14.0 %copy-start.4 = (bf16[3,3,3,32,64]{4,3,2,1,0:T(8,128)(2,1)S(1)}, bf16[3,3,3,32,64]{4,3,2,1,0:T(8,128)(2,1)}, u32[]{:S(2)}) copy-start(bf16[3,3,3,32,64]{4,3,2,1,0:T(8,128)(2,1)} %param.11) | copy-start | bytes 331780
  94.5 7.7 %copy-start.6 = (bf16[3,3,3,32,32]{4,3,2,1,0:T(8,128)(2,1)S(1)}, bf16[3,3,3,32,32]{4,3,2,1,0:T(8,128)(2,1)}, u32[]{:S(2)}) copy-start(bf16[3,3,3,32,32]{4,3,2,1,0:T(8,128)(2,1)} %param.10) | copy-start | bytes 165892
  94.5 12.4 %all-to-all-start.3 = ((bf16[4,256,128]{2,1,0:T(8,128)(2,1)}), bf16[4,256,128]{2,1,0:T(8,128)(2,1)S(1)}, u32[]{:S(2)}, u32[]{:S(2)}) async-start(bf16[4,256,128]{2,1,0:T(8,128)(2,1)} %get-tuple-element.18), calls=%async_computation.3 | async-start | bytes 524288 | tf_op jit(solution)/shard_map/all_to_all | solution.py:552
  101.9 0.9 copy-start.8

commit v4 on v3

--- a/solution.py
+++ b/solution.py
@@ -6,6 +6,7 @@
 from jax.experimental import pallas as pl
 from jax.experimental.pallas import tpu as pltpu
 from jax.sharding import PartitionSpec as P
+
 
 bf = jnp.bfloat16
 f32 = jnp.float32
@@ -192,25 +193,26 @@
     return cols_of([field[x + i, y + j] for j in range(2) for i in range(2)])
 
 
-def beside(pos, full, mine, near, far):
-    rows = near.shape[0]
+def beside(pos, full, mine, close, start, far):
+    rows, wide = far.shape[:2]
+    near = close[start : start + rows * wide].reshape(far.shape)
     full[rows : rows + 4] = mine[...]
     odd = pos[0] & 1
 
     @pl.when(odd == 1)
     def _():
-        full[0:rows] = near[...]
+        full[0:rows] = near
         full[rows + 4 : 2 * rows + 4] = far[...]
 
     @pl.when(odd == 0)
     def _():
         full[0:rows] = far[...]
-        full[rows + 4 : 2 * rows + 4] = near[...]
-
-
-def adjoint(counts, pos, cot, cot_l, cot_r, strips, gj, total, ec, matrix):
+        full[rows + 4 : 2 * rows + 4] = near
+
+
+def adjoint(counts, pos, cot, close, far, strips, gj, total, ec, matrix):
     square_matrix(strips, matrix)
-    beside(pos, ec, cot, cot_l, cot_r)
+    beside(pos, ec, cot, close, 30, far)
 
     for i in range(3):
         for dx, y, value in squares(matrix, ec, 2 * i, 6):
@@ -226,12 +228,12 @@
 
 
 def encode(
-    counts, pos, vol, vol_l, vol_r, strips, second,
+    counts, pos, vol, close, far, strips, second,
     hid, pre, early, p2, ev, h8, pre8, matrix,
 ):
     square_matrix(strips, matrix)
     w, n = place(pos)
-    beside(pos, ev, vol, vol_l, vol_r)
+    beside(pos, ev, vol, close, 0, far)
 
     for i in range(4):
         for dx, y, value in squares(matrix, ev, 2 * i, 8):
@@ -507,7 +509,6 @@
         out_specs=[vmem] * len(outs),
         scratch_shapes=[pltpu.VMEM(s, d) for s, d in scratch],
         compiler_params=pltpu.CompilerParams(vmem_limit_bytes=48 * 1024 * 1024),
-        name=body.__name__,
         cost_estimate=pl.CostEstimate(flops=400000000, bytes_accessed=2000000, transcendentals=0),
     )(*args)
 
@@ -524,13 +525,6 @@
     return lax.ppermute(
         cells, axis, [(i, i + 1) for i in lower] + [(i + 1, i) for i in lower]
     )
-
-
-def widened(cells, axis, dim, width):
-    size = cells.shape[dim]
-    head = lax.slice_in_dim(cells, 0, width, axis=dim)
-    tail = lax.slice_in_dim(cells, size - width, size, axis=dim)
-    return send(tail, axis, 1), send(head, axis, -1)
 
 
 def shards(
@@ -555,21 +549,20 @@
 
     vol = volume.transpose(1, 2, 0, 3)
     cot = cotangent.transpose(1, 2, 0, 3)
-    vl, vr = widened(vol, "narrow", 1, 3)
-    cl, cr = widened(cot, "narrow", 1, 2)
-    vol = jnp.concatenate([vl, vol, vr], axis=1)
-    cot = jnp.concatenate([cl, cot, cr], axis=1)
+    low = send(jnp.concatenate([vol[:, 1:], cot[:, 2:]], axis=1), "narrow", 1)
+    high = send(jnp.concatenate([vol[:, :3], cot[:, :2]], axis=1), "narrow", -1)
+    vol = jnp.concatenate([low[:, :3], vol, high[:, :3]], axis=1)
+    cot = jnp.concatenate([low[:, 3:], cot, high[:, 3:]], axis=1)
     odd = pos[0] & 1
 
-    def halves(cells, width):
-        start = 4 - width
-        near = lax.dynamic_slice_in_dim(cells, (1 - odd) * start, width, axis=0)
-        far = lax.dynamic_slice_in_dim(cells, odd * start, width, axis=0)
-        far = swap(far, "wide", 1)
-        return swap(near, "wide", 0), far
-
-    vol_l, vol_r = halves(vol, 3)
-    cot_l, cot_r = halves(cot, 2)
+    def edge(cells, width, side):
+        return lax.dynamic_slice_in_dim(cells, side * (4 - width), width, axis=0)
+
+    vol_far = swap(edge(vol, 3, odd), "wide", 1)
+    flat = lambda cells: cells.reshape(-1, 32, 128)
+    near = [flat(edge(vol, 3, 1 - odd)), flat(edge(cot, 2, 1 - odd))]
+    near = swap(jnp.concatenate(near, axis=0), "wide", 0)
+    cot_far = swap(edge(cot, 2, odd), "wide", 1)
 
     matrix = ((384, 512), bf)
     full, cells = (6, 6, 32, 128), (4, 4, 32, 128)
@@ -577,12 +570,12 @@
         encode, counts,
         [(full, bf), (full, f32), ((128, 128), bf), ((4, 64, 128), bf)],
         [((10, 10, 32, 128), bf), ((8, 8, 32, 128), bf), ((8, 6, 32, 128), f32), matrix],
-        pos, vol, vol_l, vol_r, forward_strips(conv_first), forward_matrix(conv_second),
+        pos, vol, near, vol_far, forward_strips(conv_first), forward_matrix(conv_second),
     )
     four = gathered(p2, 0)
     gj, total = call(
         adjoint, counts, [(full, bf), ((64, 128), bf)], [((8, 8, 32, 128), bf), matrix],
-        pos, cot, cot_l, cot_r, backward_strips(conv_final),
+        pos, cot, near, cot_far, backward_strips(conv_final),
     )
     seg = lax.broadcasted_iota(jnp.int32, (64, 128), 1) // 32
     packed = four[0]
@@ -625,6 +618,7 @@
 
 def solution(mesh):
     field = P(None, "wide", "narrow", None)
+
     return jax.shard_map(
         shards,
         mesh=mesh,

time: 110 us -> 105 us (0.955)
  starting transfers between devices: 65.8 us -> 57.2 us
  waiting for transfers between devices: 16.3 us -> 19.4 us
    ppermute x4 -> x2, starting transfers between devices: 11.1 us -> 5.32 us  [send(): return lax.ppermute(cells, axis, pairs)]
    ppermute x7 -> x6, starting transfers between devices: 29.3 us -> 24.3 us  [swap(): lax.ppermute(cells, axis, [(i, i + 1) for i in lower] + [(i + 1, i) for i...]
    ppermute x7 -> x6, waiting for transfers between devices: 0.02 us -> 3.16 us  [swap(): lax.ppermute(cells, axis, [(i, i + 1) for i in lower] + [(i + 1, i) for i...]
    all_to_all x4, starting transfers between devices: 25.4 us -> 27.6 us  [gathered(): lax.all_to_all(content, ('wide', 'narrow'), 0, 0, axis_index_groups=groups)]
    all_to_all x4, waiting for transfers between devices: 10.6 us -> 9.42 us  [gathered(): lax.all_to_all(content, ('wide', 'narrow'), 0, 0, axis_index_groups=groups)]
    ppermute x4 -> x2, waiting for transfers between devices: 5.73 us -> 6.82 us  [send(): return lax.ppermute(cells, axis, pairs)]
  transfers between devices with their start and end apart: 15 -> 12, of which waited for: 6 -> 7; matrix products, arithmetic and copies ran while one was open for 8% -> 8% of each run, Pallas kernels for 6% -> 6%
where the time goes in v4:
time: 105 us; the launch traced here: 104 us
  starting transfers between devices  57.2 us (54%)
  waiting for transfers between devices  19.4 us (18%)
  Pallas kernels  14.2 us (14%)
  local copies, waits for them, and re-layouts  11.7 us (11%)
  between operations  1.16 us (1%)
    all_to_all x4, starting transfers between devices, gathered(): lax.all_to_all(content, ('wide', 'narrow'), 0, 0, axis_index_groups=groups)  27.6 us
    ppermute x6, starting transfers between devices, swap(): lax.ppermute(cells, axis, [(i, i + 1) for i in lower] + [(i + 1, i) for i...  24.3 us
    pallas_call x7, Pallas kernels, call(): pl.pallas_call(functools.partial(body, counts), out_shape=[jax.ShapeDtype...  14.2 us
    all_to_all x4, waiting for transfers between devices, gathered(): lax.all_to_all(content, ('wide', 'narrow'), 0, 0, axis_index_groups=groups)  9.42 us
    ppermute x2, waiting for transfers between devices, send(): return lax.ppermute(cells, axis, pairs)  6.82 us
    ppermute x2, starting transfers between devices, send(): return lax.ppermute(cells, axis, pairs)  5.32 us
    unnamed x23, local copies, waits for them, and re-layouts  3.74 us
    reshape x5, local copies, waits for them, and re-layouts, forward_matrix(): return kernel.transpose(2, 4, 0, 1, 3).reshape(3 * outs, 9 * chans)  3.7 us
  transfers between devices with their start and end apart: 12, of which 7 were waited for; matrix products, arithmetic and copies ran while one was open for 8% of the time, Pallas kernels for 6%

profile of v4, /device:TPU:1, one launch (start us, length us, event | category | flops | bytes accessed | tf_op | source)
XLA Modules:
  0.0 103.9 jit_solution(2106286666254780097)
XLA Ops:
  0.6 0.9 copy.48
  1.6 0.9 copy.47
  2.6 4.0 %collective-permute-start = (bf16[4,5,32,128]{3,2,1,0:T(8,128)(2,1)S(1)}, bf16[4,5,32,128]{3,2,1,0:T(8,128)(2,1)S(1)}, u32[]{:S(2)}, u32[]{:S(2)}) collective-permute-start(bf16[4,5,32,128]{3,2,1,0:T(8,128)(2,1)S(1)} %pad_maximum_fusion.3), channel_id=1, source_target_pairs={{0,1},{1,2},{2,3},{3,4},{4,5},{5,6},{6,7},{7,8},{8,9},{9,10},{10,1... | collective-permute-start | bytes 491528 | tf_op jit(solution)/shard_map/ppermute | solution.py:519
  6.7 1.3 %collective-permute-start.1 = (bf16[4,5,32,128]{3,2,1,0:T(8,128)(2,1)S(1)}, bf16[4,5,32,128]{3,2,1,0:T(8,128)(2,1)S(1)}, u32[]{:S(2)}, u32[]{:S(2)}) collective-permute-start(bf16[4,5,32,128]{3,2,1,0:T(8,128)(2,1)S(1)} %pad_maximum_fusion.4), channel_id=1, source_target_pairs={{1,0},{2,1},{3,2},{4,3},{5,4},{6,5},{7,6},{8,7},{9,8},{10,9},{11,1... | collective-permute-start | bytes 491528 | tf_op jit(solution)/shard_map/ppermute | solution.py:519
  8.0 0.9 collective-permute-done
  8.9 5.9 %collective-permute-done.1 = bf16[4,5,32,128]{3,2,1,0:T(8,128)(2,1)S(1)} collective-permute-done((bf16[4,5,32,128]{3,2,1,0:T(8,128)(2,1)S(1)}, bf16[4,5,32,128]{3,2,1,0:T(8,128)(2,1)S(1)}, u32[]{:S(2)}, u32[]{:S(2)}) %collective-permute-start.1) | collective-permute-done | bytes 163872 | tf_op jit(solution)/shard_map/ppermute | solution.py:519
  15.1 5.2 %collective-permute-start.2 = (bf16[46,32,128]{2,1,0:T(8,128)(2,1)S(1)}, bf16[46,32,128]{2,1,0:T(8,128)(2,1)S(1)}, u32[]{:S(2)}, u32[]{:S(2)}) collective-permute-start(bf16[46,32,128]{2,1,0:T(8,128)(2,1)S(1)} %pad_maximum_fusion), channel_id=1, source_target_pairs={{0,16},{32,48},{64,80},{96,112},{128,144},{160,176},{192,208},{224... | collective-permute-start | bytes 1130504 | tf_op jit(solution)/shard_map/ppermute | solution.py:525
  20.3 3.4 %collective-permute-start.3 = (bf16[3,10,32,128]{3,2,1,0:T(8,128)(2,1)S(1)}, bf16[3,10,32,128]{3,2,1,0:T(8,128)(2,1)S(1)}, u32[]{:S(2)}, u32[]{:S(2)}) collective-permute-start(bf16[3,10,32,128]{3,2,1,0:T(8,128)(2,1)S(1)} %get-tuple-element.26), channel_id=1, source_target_pairs={{16,32},{48,64},{80,96},{112,128},{144,160},{176,192},{208,224},{2... | collective-permute-start | bytes 737288 | tf_op jit(solution)/shard_map/ppermute | solution.py:525
  23.7 0.2 copy.30
  23.9 0.2 reshape.44.strips
  24.2 0.2 reshape.43
  24.7 0.2 copy.27
  24.9 0.2 reshape.42.strips
  25.1 3.1 %collective-permute-start.4 = (bf16[2,8,32,128]{3,2,1,0:T(8,128)(2,1)S(1)}, bf16[2,8,32,128]{3,2,1,0:T(8,128)(2,1)S(1)}, u32[]{:S(2)}, u32[]{:S(2)}) collective-permute-start(bf16[2,8,32,128]{3,2,1,0:T(8,128)(2,1)S(1)} %get-tuple-element.28), channel_id=1, source_target_pairs={{16,32},{48,64},{80,96},{112,128},{144,160},{176,192},{208,224},{2... | collective-permute-start | bytes 393224 | tf_op jit(solution)/shard_map/ppermute | solution.py:525
  28.2 3.1 %collective-permute-done.3.far = bf16[3,10,32,128]{3,2,1,0:T(8,128)(2,1)S(1)} collective-permute-done((bf16[3,10,32,128]{3,2,1,0:T(8,128)(2,1)S(1)}, bf16[3,10,32,128]{3,2,1,0:T(8,128)(2,1)S(1)}, u32[]{:S(2)}, u32[]{:S(2)}) %collective-permute-start.3) | collective-permute-done | bytes 245792 | tf_op jit(solution)/shard_map/ppermute | solution.py:525
  31.4 3.4 %shard_map.95 = (bf16[6,6,32,128]{3,2,1,0:T(8,128)(2,1)S(1)}, f32[6,6,32,128]{3,2,1,0:T(8,128)S(1)}, bf16[128,128]{1,0:T(8,128)(2,1)S(1)}, bf16[4,64,128]{2,1,0:T(8,128)(2,1)}) custom-call(s32[2]{0:T(128)S(1)} %pad_add_fusion.pos, bf16[4,10,32,128]{3,2,1,0:T(8,128)(2,1)S(1)} %pad_maximum_fusion.1.vol, bf16[46,32,128]{2,1,0:T(8,128)(2,1)S(1)} %collective-permute-done.2.close, ...), custom_call_target="tpu_custom_call" | custom-call | flops 400000000 | bytes 2000000 | tf_op jit(solution)/shard_map/pallas_call | solution.py:505
  34.8 3.3 %all-to-all-start = ((bf16[4,64,128]{2,1,0:T(8,128)(2,1)}), bf16[4,64,128]{2,1,0:T(8,128)(2,1)S(1)}, u32[]{:S(2)}, u32[]{:S(2)}) async-start(bf16[4,64,128]{2,1,0:T(8,128)(2,1)} %get-tuple-element.14), calls=%async_computation | async-start | bytes 131072 | tf_op jit(solution)/shard_map/all_to_all | solution.py:546
  38.1 1.6 %shard_map.96 = (bf16[6,6,32,128]{3,2,1,0:T(8,128)(2,1)S(1)}, bf16[64,128]{1,0:T(8,128)(2,1)S(1)}) custom-call(s32[2]{0:T(128)S(1)} %pad_add_fusion.pos, bf16[4,8,32,128]{3,2,1,0:T(8,128)(2,1)S(1)} %pad_maximum_fusion.2.cot, bf16[46,32,128]{2,1,0:T(8,128)(2,1)S(1)} %collective-permute-done.2.close, bf16[2,8,32,128]{3,2,1,0:T(8,128)(2,1)S(1)} %collective-permute-done.4.far, ...), custom_call_target="tpu_custom_call" | custom-call | flops 400000000 | bytes 2000000 | tf_op jit(solution)/shard_map/pallas_call | solution.py:505
  39.9 0.7 broadcast_in_dim.3
  40.6 11.6 %all-to-all-start.1 = ((bf16[4,256,128]{2,1,0:T(8,128)(2,1)}), bf16[4,256,128]{2,1,0:T(8,128)(2,1)S(1)}, u32[]{:S(2)}, u32[]{:S(2)}) async-start(bf16[4,256,128]{2,1,0:T(8,128)(2,1)} %broadcast_in_dim.3), calls=%async_computation.1 | async-start | bytes 524288 | tf_op jit(solution)/shard_map/all_to_all | solution.py:546
  52.2 2.3 %copy.43 = bf16[3,128,3,3,64]{4,3,2,1,0:T(4,128)(2,1)S(1)} copy(bf16[3,128,3,3,64]{1,4,0,3,2:T(8,128)(2,1)} %bitcast.51) | data formatting | bytes 884736 | tf_op jit(solution)/shard_map/reshape | solution.py:17
  54.5 0.8 reshape.52.weight
  55.4 2.6 %all-to-all-done.1.got.early = bf16[4,256,128]{2,1,0:T(8,128)(2,1)S(1)} async-done(((bf16[4,256,128]{2,1,0:T(8,128)(2,1)}), bf16[4,256,128]{2,1,0:T(8,128)(2,1)S(1)}, u32[]{:S(2)}, u32[]{:S(2)}) %all-to-all-start.1) | async-done | bytes 262176 | tf_op jit(solution)/shard_map/all_to_all | solution.py:546
  58.1 1.3 %shard_map.97.mine = bf16[736,128]{1,0:T(8,128)(2,1)S(1)} custom-call(s32[2]{0:T(128)S(1)} %pad_add_fusion.pos, bf16[4,256,128]{2,1,0:T(8,128)(2,1)S(1)} %all-to-all-done.1.got.early, bf16[384,576]{1,0:T(8,128)(2,1)S(1)} %reshape.52.weight, bf16[64,128]{1,0:T(8,128)(2,1)S(1)} %copy-done), custom_call_target="tpu_custom_call" | custom-call | flops 400000000 | bytes 2000000 | tf_op jit(solution)/shard_map/pallas_call | solution.py:505
  59.4 1.9 %collective-permute-start.6 = (bf16[736,128]{1,0:T(8,128)(2,1)S(1)}, bf16[736,128]{1,0:T(8,128)(2,1)S(1)}, u32[]{:S(2)}, u32[]{:S(2)}) collective-permute-start(bf16[736,128]{1,0:T(8,128)(2,1)S(1)} %shard_map.97.mine), channel_id=1, source_target_pairs={{0,1},{2,3},{4,5},{6,7},{8,9},{10,11},{12,13},{14,15},{1,0},{3,2},... | collective-permute-start | bytes 565256 | tf_op jit(solution)/shard_map/ppermute | solution.py:525
  61.3 5.2 %collective-permute-start.5 = (bf16[736,128]{1,0:T(8,128)(2,1)S(1)}, bf16[736,128]{1,0:T(8,128)(2,1)S(1)}, u32[]{:S(2)}, u32[]{:S(2)}) collective-permute-start(bf16[736,128]{1,0:T(8,128)(2,1)S(1)} %shard_map.97.mine), channel_id=1, source_target_pairs={{0,16},{32,48},{64,80},{96,112},{128,144},{160,176},{192,208},{224... | collective-permute-start | bytes 565256 | tf_op jit(solution)/shard_map/ppermute | solution.py:525
  66.5 5.5 %collective-permute-start.7 = (bf16[736,128]{1,0:T(8,128)(2,1)S(1)}, bf16[736,128]{1,0:T(8,128)(2,1)S(1)}, u32[]{:S(2)}, u32[]{:S(2)}) collective-permute-start(bf16[736,128]{1,0:T(8,128)(2,1)S(1)} %collective-permute-done.6.side), channel_id=1, source_target_pairs={{0,16},{32,48},{64,80},{96,112},{128,144},{160,176},{192,208},{224... | collective-permute-start | bytes 565256 | tf_op jit(solution)/shard_map/ppermute | solution.py:525
  72.4 0.2 reshape.47
  72.7 0.2 copy.33
  72.9 0.2 reshape.46.weight
  73.1 3.0 %shard_map.98 = (bf16[4,256,128]{2,1,0:T(8,128)(2,1)}, bf16[256,128]{1,0:T(8,128)(2,1)S(1)}) custom-call(s32[2]{0:T(128)S(1)} %pad_add_fusion.pos, bf16[736,128]{1,0:T(8,128)(2,1)S(1)} %shard_map.97.mine, bf16[736,128]{1,0:T(8,128)(2,1)S(1)} %collective-permute-done.5.chip, bf16[736,128]{1,0:T(8,128)(2,1)S(1)} %collective-permute-done.6.side, ...), custom_call_target="tpu_custom_call" | custom-call | flops 400000000 | bytes 2000000 | tf_op jit(solution)/shard_map/pallas_call | solution.py:505
  76.1 5.0 %all-to-all-start.2 = ((bf16[4,256,128]{2,1,0:T(8,128)(2,1)}), bf16[4,256,128]{2,1,0:T(8,128)(2,1)S(1)}, u32[]{:S(2)}, u32[]{:S(2)}) async-start(bf16[4,256,128]{2,1,0:T(8,128)(2,1)} %get-tuple-element.17), calls=%async_computation.2 | async-start | bytes 524288 | tf_op jit(solution)/shard_map/all_to_all | solution.py:546
  81.1 0.4 copy.38
  81.5 0.4 reshape.49.weight
  81.9 4.9 %all-to-all-done.2.got = bf16[4,256,128]{2,1,0:T(8,128)(2,1)S(1)} async-done(((bf16[4,256,128]{2,1,0:T(8,128)(2,1)}), bf16[4,256,128]{2,1,0:T(8,128)(2,1)S(1)}, u32[]{:S(2)}, u32[]{:S(2)}) %all-to-all-start.2) | async-done | bytes 262176 | tf_op jit(solution)/shard_map/all_to_all | solution.py:546
  86.8 1.9 %shard_map.100 = (bf16[4,256,128]{2,1,0:T(8,128)(2,1)}, bf16[8,64,128]{2,1,0:T(8,128)(2,1)S(1)}) custom-call(s32[2]{0:T(128)S(1)} %pad_add_fusion.pos, bf16[4,256,128]{2,1,0:T(8,128)(2,1)S(1)} %all-to-all-done.2.got, bf16[4,256,128]{2,1,0:T(8,128)(2,1)S(1)} %all-to-all-done.1.got.early, bf16[192,1152]{1,0:T(8,128)(2,1)S(1)} %reshape.49.weight), custom_call_target="tpu_custom_call" | custom-call | flops 400000000 | bytes 2000000 | tf_op jit(solution)/shard_map/pallas_call | solution.py:505
  88.7 7.6 %all-to-all-start.3 = ((bf16[4,256,128]{2,1,0:T(8,128)(2,1)}), bf16[4,256,128]{2,1,0:T(8,128)(2,1)S(1)}, u32[]{:S(2)}, u32[]{:S(2)}) async-start(bf16[4,256,128]{2,1,0:T(8,128)(2,1)} %get-tuple-element.18), calls=%async_computation.3 | async-start | bytes 524288 | tf_op jit(solution)/shard_map/all_to_all | solution.py:546
  96.4 0.2 copy.39
  96.5 0.2 reshape.50.second_b
  96.9 0.2 reshape.51.strips
  97.1 0.2 copy-done.8
  97.3 0.2 copy.37
  97.5 0.2 reshape.48.strips
  97.7 1.2 %shard_map.99 = bf16[4,4,32,128]{3,2,1,0:T(8,128)(2,1)S(1)} custom-call(s32[2]{0:T(128)S(1)} %pad_add_fusion.pos, bf16[256,128]{1,0:T(8,128)(2,1)S(1)} %get-tuple-element.15.hidden, bf16[6,6,32,128]{3,2,1,0:T(8,128)(2,1)S(1)} %get-tuple-element.16.hid, bf16[3,96,96]{2,1,0:T(8,128)(2,1)S(1)} %reshape.48.strips), custom_call_target="tpu_custom_call" | custom-call | flops 400000000 | bytes 2000000 | tf_op jit(solution)/shard_map/pallas_call | solution.py:505
  98.9 0.7 copy.41
  99.6 1.8 %all-to-all-done.3.got = bf16[4,256,128]{2,1,0:T(8,128)(2,1)S(1)} async-done(((bf16[4,256,128]{2,1,0:T(8,128)(2,1)}), bf16[4,256,128]{2,1,0:T(8,128)(2,1)S(1)}, u32[]{:S(2)}, u32[]{:S(2)}) %all-to-all-start.3) | async-done | bytes 262176 | tf_op jit(solution)/shard_map/all_to_all | solution.py:546
  101.4 1.8 %shard_map.101 = bf16[4,4,32,128]{3,2,1,0:T(8,128)(2,1)S(1)} custom-call(s32[2]{0:T(128)S(1)} %pad_add_fusion.pos, bf16[4,256,128]{2,1,0:T(8,128)(2,1)S(1)} %all-to-all-done.3.got, bf16[8,64,128]{2,1,0:T(8,128)(2,1)S(1)} %get-tuple-element.19.mine, bf16[6,6,32,128]{3,2,1,0:T(8,128)(2,1)S(1)} %get-tuple-element.20.gj, ...), custom_call_target="tpu_custom_call" | custom-call | flops 400000000 | bytes 2000000 | tf_op jit(solution)/shard_map/pallas_call | solution.py:505
  103.2 0.7 copy.42
  (52 shorter events, 1.6 us)
Async XLA Ops:
  2.6 6.3 %collective-permute-start = (bf16[4,5,32,128]{3,2,1,0:T(8,128)(2,1)S(1)}, bf16[4,5,32,128]{3,2,1,0:T(8,128)(2,1)S(1)}, u32[]{:S(2)}, u32[]{:S(2)}) collective-permute-start(bf16[4,5,32,128]{3,2,1,0:T(8,128)(2,1)S(1)} %pad_maximum_fusion.3), channel_id=1, source_target_pairs={{0,1},{1,2},{2,3},{3,4},{4,5},{5,6},{6,7},{7,8},{8,9},{9,10},{10,1... | collective-permute-start | bytes 491528 | tf_op jit(solution)/shard_map/ppermute | solution.py:519
  6.7 8.1 %collective-permute-start.1 = (bf16[4,5,32,128]{3,2,1,0:T(8,128)(2,1)S(1)}, bf16[4,5,32,128]{3,2,1,0:T(8,128)(2,1)S(1)}, u32[]{:S(2)}, u32[]{:S(2)}) collective-permute-start(bf16[4,5,32,128]{3,2,1,0:T(8,128)(2,1)S(1)} %pad_maximum_fusion.4), channel_id=1, source_target_pairs={{1,0},{2,1},{3,2},{4,3},{5,4},{6,5},{7,6},{8,7},{9,8},{10,9},{11,1... | collective-permute-start | bytes 491528 | tf_op jit(solution)/shard_map/ppermute | solution.py:519
  14.9 8.8 %copy-start.7 = (bf16[3,3,3,32,32]{4,3,2,1,0:T(8,128)(2,1)S(1)}, bf16[3,3,3,32,32]{4,3,2,1,0:T(8,128)(2,1)}, u32[]{:S(2)}) copy-start(bf16[3,3,3,32,32]{4,3,2,1,0:T(8,128)(2,1)} %param.15) | copy-start | bytes 165892
  15.0 9.1 %copy-start.3 = (bf16[3,3,3,32,64]{4,3,2,1,0:T(8,128)(2,1)S(1)}, bf16[3,3,3,32,64]{4,3,2,1,0:T(8,128)(2,1)}, u32[]{:S(2)}) copy-start(bf16[3,3,3,32,64]{4,3,2,1,0:T(8,128)(2,1)} %param.11) | copy-start | bytes 331780
  15.1 16.3 %collective-permute-start.2 = (bf16[46,32,128]{2,1,0:T(8,128)(2,1)S(1)}, bf16[46,32,128]{2,1,0:T(8,128)(2,1)S(1)}, u32[]{:S(2)}, u32[]{:S(2)}) collective-permute-start(bf16[46,32,128]{2,1,0:T(8,128)(2,1)S(1)} %pad_maximum_fusion), channel_id=1, source_target_pairs={{0,16},{32,48},{64,80},{96,112},{128,144},{160,176},{192,208},{224... | collective-permute-start | bytes 1130504 | tf_op jit(solution)/shard_map/ppermute | solution.py:525
  20.3 11.0 %collective-permute-start.3 = (bf16[3,10,32,128]{3,2,1,0:T(8,128)(2,1)S(1)}, bf16[3,10,32,128]{3,2,1,0:T(8,128)(2,1)S(1)}, u32[]{:S(2)}, u32[]{:S(2)}) collective-permute-start(bf16[3,10,32,128]{3,2,1,0:T(8,128)(2,1)S(1)} %get-tuple-element.26), channel_id=1, source_target_pairs={{16,32},{48,64},{80,96},{112,128},{144,160},{176,192},{208,224},{2... | collective-permute-start | bytes 737288 | tf_op jit(solution)/shard_map/ppermute | solution.py:525
  23.7 0.9 copy-start.5
  25.1 13.0 %collective-permute-start.4 = (bf16[2,8,32,128]{3,2,1,0:T(8,128)(2,1)S(1)}, bf16[2,8,32,128]{3,2,1,0:T(8,128)(2,1)S(1)}, u32[]{:S(2)}, u32[]{:S(2)}) collective-permute-start(bf16[2,8,32,128]{3,2,1,0:T(8,128)(2,1)S(1)} %get-tuple-element.28), channel_id=1, source_target_pairs={{16,32},{48,64},{80,96},{112,128},{144,160},{176,192},{208,224},{2... | collective-permute-start | bytes 393224 | tf_op jit(solution)/shard_map/ppermute | solution.py:525
  34.8 5.0 %all-to-all-start = ((bf16[4,64,128]{2,1,0:T(8,128)(2,1)}), bf16[4,64,128]{2,1,0:T(8,128)(2,1)S(1)}, u32[]{:S(2)}, u32[]{:S(2)}) async-start(bf16[4,64,128]{2,1,0:T(8,128)(2,1)} %get-tuple-element.14), calls=%async_computation | async-start | bytes 131072 | tf_op jit(solution)/shard_map/all_to_all | solution.py:546
  40.6 17.5 %all-to-all-start.1 = ((bf16[4,256,128]{2,1,0:T(8,128)(2,1)}), bf16[4,256,128]{2,1,0:T(8,128)(2,1)S(1)}, u32[]{:S(2)}, u32[]{:S(2)}) async-start(bf16[4,256,128]{2,1,0:T(8,128)(2,1)} %broadcast_in_dim.3), calls=%async_computation.1 | async-start | bytes 524288 | tf_op jit(solution)/shard_map/all_to_all | solution.py:546
  54.5 3.5 %copy-start = (bf16[64,128]{1,0:T(8,128)(2,1)S(1)}, bf16[64,128]{1,0:T(8,128)(2,1)}, u32[]{:S(2)}) copy-start(bf16[64,128]{1,0:T(8,128)(2,1)} %lift.1) | copy-start | bytes 49156
  55.4 16.8 %copy-start.2 = (bf16[3,3,3,64,32]{3,4,2,1,0:T(8,128)(2,1)S(1)}, bf16[3,3,3,64,32]{3,4,2,1,0:T(8,128)(2,1)}, u32[]{:S(2)}) copy-start(bf16[3,3,3,64,32]{3,4,2,1,0:T(8,128)(2,1)} %param.14) | copy-start | bytes 331780
  59.4 7.1 %collective-permute-start.6 = (bf16[736,128]{1,0:T(8,128)(2,1)S(1)}, bf16[736,128]{1,0:T(8,128)(2,1)S(1)}, u32[]{:S(2)}, u32[]{:S(2)}) collective-permute-start(bf16[736,128]{1,0:T(8,128)(2,1)S(1)} %shard_map.97.mine), channel_id=1, source_target_pairs={{0,1},{2,3},{4,5},{6,7},{8,9},{10,11},{12,13},{14,15},{1,0},{3,2},... | collective-permute-start | bytes 565256 | tf_op jit(solution)/shard_map/ppermute | solution.py:525
  61.3 11.8 %collective-permute-start.5 = (bf16[736,128]{1,0:T(8,128)(2,1)S(1)}, bf16[736,128]{1,0:T(8,128)(2,1)S(1)}, u32[]{:S(2)}, u32[]{:S(2)}) collective-permute-start(bf16[736,128]{1,0:T(8,128)(2,1)S(1)} %shard_map.97.mine), channel_id=1, source_target_pairs={{0,16},{32,48},{64,80},{96,112},{128,144},{160,176},{192,208},{224... | collective-permute-start | bytes 565256 | tf_op jit(solution)/shard_map/ppermute | solution.py:525
  66.5 6.6 %collective-permute-start.7 = (bf16[736,128]{1,0:T(8,128)(2,1)S(1)}, bf16[736,128]{1,0:T(8,128)(2,1)S(1)}, u32[]{:S(2)}, u32[]{:S(2)}) collective-permute-start(bf16[736,128]{1,0:T(8,128)(2,1)S(1)} %collective-permute-done.6.side), channel_id=1, source_target_pairs={{0,16},{32,48},{64,80},{96,112},{128,144},{160,176},{192,208},{224... | collective-permute-start | bytes 565256 | tf_op jit(solution)/shard_map/ppermute | solution.py:525
  72.9 8.2 %copy-start.1 = (bf16[3,3,3,64,128]{4,3,2,1,0:T(8,128)(2,1)S(1)}, bf16[3,3,3,64,128]{4,3,2,1,0:T(8,128)(2,1)}, u32[]{:S(2)}) copy-start(bf16[3,3,3,64,128]{4,3,2,1,0:T(8,128)(2,1)} %param.12) | copy-start | bytes 1327108
  76.1 10.7 %all-to-all-start.2 = ((bf16[4,256,128]{2,1,0:T(8,128)(2,1)}), bf16[4,256,128]{2,1,0:T(8,128)(2,1)S(1)}, u32[]{:S(2)}, u32[]{:S(2)}) async-start(bf16[4,256,128]{2,1,0:T(8,128)(2,1)} %get-tuple-element.17), calls=%async_computation.2 | async-start | bytes 524288 | tf_op jit(solution)/shard_map/all_to_all | solution.py:546
  81.9 14.4 %copy-start.4 = (bf16[3,3,3,32,64]{4,3,2,1,0:T(8,128)(2,1)S(1)}, bf16[3,3,3,32,64]{4,3,2,1,0:T(8,128)(2,1)}, u32[]{:S(2)}) copy-start(bf16[3,3,3,32,64]{4,3,2,1,0:T(8,128)(2,1)} %param.11) | copy-start | bytes 331780
  88.7 8.0 %copy-start.6 = (bf16[3,3,3,32,32]{4,3,2,1,0:T(8,128)(2,1)S(1)}, bf16[3,3,3,32,32]{4,3,2,1,0:T(8,128)(2,1)}, u32[]{:S(2)}) copy-start(bf16[3,3,3,32,32]{4,3,2,1,0:T(8,128)(2,1)} %param.10) | copy-start | bytes 165892
  88.7 12.7 %all-to-all-start.3 = ((bf16[4,256,128]{2,1,0:T(8,128)(2,1)}), bf16[4,256,128]{2,1,0:T(8,128)(2,1)S(1)}, u32[]{:S(2)}, u32[]{:S(2)}) async-start(bf16[4,256,128]{2,1,0:T(8,128)(2,1)} %get-tuple-element.18), calls=%async_computation.3 | async-start | bytes 524288 | tf_op jit(solution)/shard_map/all_to_all | solution.py:546
  96.3 0.9 copy-start.8

commit v5 on v4

--- a/solution.py
+++ b/solution.py
@@ -495,8 +495,10 @@
             gf[x, y] = value.astype(bf)
 
     for i in range(2):
-        for dx, y, value in squares(matrix, gf, 2 * i, 4):
-            out[2 * i + dx, y] = value.astype(bf)
+        rows = {(dx, y): value for dx, y, value in squares(matrix, gf, 2 * i, 4)}
+        for dx in range(2):
+            line = jnp.stack([rows[dx, y] for y in range(4)])
+            out[:, 2 * i + dx] = jnp.swapaxes(line, 0, 1).astype(bf)
 
 
 def call(body, counts, outs, scratch, *args):
@@ -610,10 +612,10 @@
     )
     got = gathered(content, 0)
     (grad,) = call(
-        finish, counts, [(cells, bf)], [((6, 3, 64, 128), bf), (full, bf), matrix],
+        finish, counts, [((32, 4, 4, 128), bf)], [((6, 3, 64, 128), bf), (full, bf), matrix],
         pos, got, mine, gj, pre, backward_matrix(conv_second), backward_strips(conv_first),
     )
-    return features.transpose(2, 0, 1, 3), grad.transpose(2, 0, 1, 3)
+    return features.transpose(2, 0, 1, 3), grad
 
 
 def solution(mesh):

time: 105 us -> 105 us (level)
    unnamed x23 -> x22, local copies, waits for them, and re-layouts: 3.74 us -> 3.01 us
where the time goes in v5:
time: 105 us; the launch traced here: 104 us
  starting transfers between devices  57.2 us (54%)
  waiting for transfers between devices  19.4 us (18%)
  Pallas kernels  14.9 us (14%)
  local copies, waits for them, and re-layouts  11 us (10%)
  between operations  1.15 us (1%)
    all_to_all x4, starting transfers between devices, gathered(): lax.all_to_all(content, ('wide', 'narrow'), 0, 0, axis_index_groups=groups)  27.6 us
    ppermute x6, starting transfers between devices, swap(): lax.ppermute(cells, axis, [(i, i + 1) for i in lower] + [(i + 1, i) for i...  24.3 us
    pallas_call x7, Pallas kernels, call(): pl.pallas_call(functools.partial(body, counts), out_shape=[jax.ShapeDtype...  14.9 us
    all_to_all x4, waiting for transfers between devices, gathered(): lax.all_to_all(content, ('wide', 'narrow'), 0, 0, axis_index_groups=groups)  9.42 us
    ppermute x2, waiting for transfers between devices, send(): return lax.ppermute(cells, axis, pairs)  6.82 us
    ppermute x2, starting transfers between devices, send(): return lax.ppermute(cells, axis, pairs)  5.32 us
    reshape x5, local copies, waits for them, and re-layouts, forward_matrix(): return kernel.transpose(2, 4, 0, 1, 3).reshape(3 * outs, 9 * chans)  3.7 us
    ppermute x6, waiting for transfers between devices, swap(): lax.ppermute(cells, axis, [(i, i + 1) for i in lower] + [(i + 1, i) for i...  3.16 us
  transfers between devices with their start and end apart: 12, of which 7 were waited for; matrix products, arithmetic and copies ran while one was open for 8% of the time, Pallas kernels for 6%

profile of v5, /device:TPU:1, one launch (start us, length us, event | category | flops | bytes accessed | tf_op | source)
XLA Modules:
  0.0 103.8 jit_solution(9026850889888641567)
XLA Ops:
  0.6 0.9 copy.46
  1.6 0.9 copy.45
  2.6 4.0 %collective-permute-start = (bf16[4,5,32,128]{3,2,1,0:T(8,128)(2,1)S(1)}, bf16[4,5,32,128]{3,2,1,0:T(8,128)(2,1)S(1)}, u32[]{:S(2)}, u32[]{:S(2)}) collective-permute-start(bf16[4,5,32,128]{3,2,1,0:T(8,128)(2,1)S(1)} %pad_maximum_fusion.3), channel_id=1, source_target_pairs={{0,1},{1,2},{2,3},{3,4},{4,5},{5,6},{6,7},{7,8},{8,9},{9,10},{10,1... | collective-permute-start | bytes 491528 | tf_op jit(solution)/shard_map/ppermute | solution.py:521
  6.7 1.3 %collective-permute-start.1 = (bf16[4,5,32,128]{3,2,1,0:T(8,128)(2,1)S(1)}, bf16[4,5,32,128]{3,2,1,0:T(8,128)(2,1)S(1)}, u32[]{:S(2)}, u32[]{:S(2)}) collective-permute-start(bf16[4,5,32,128]{3,2,1,0:T(8,128)(2,1)S(1)} %pad_maximum_fusion.4), channel_id=1, source_target_pairs={{1,0},{2,1},{3,2},{4,3},{5,4},{6,5},{7,6},{8,7},{9,8},{10,9},{11,1... | collective-permute-start | bytes 491528 | tf_op jit(solution)/shard_map/ppermute | solution.py:521
  8.0 0.9 collective-permute-done
  8.9 5.9 %collective-permute-done.1 = bf16[4,5,32,128]{3,2,1,0:T(8,128)(2,1)S(1)} collective-permute-done((bf16[4,5,32,128]{3,2,1,0:T(8,128)(2,1)S(1)}, bf16[4,5,32,128]{3,2,1,0:T(8,128)(2,1)S(1)}, u32[]{:S(2)}, u32[]{:S(2)}) %collective-permute-start.1) | collective-permute-done | bytes 163872 | tf_op jit(solution)/shard_map/ppermute | solution.py:521
  15.1 5.2 %collective-permute-start.2 = (bf16[46,32,128]{2,1,0:T(8,128)(2,1)S(1)}, bf16[46,32,128]{2,1,0:T(8,128)(2,1)S(1)}, u32[]{:S(2)}, u32[]{:S(2)}) collective-permute-start(bf16[46,32,128]{2,1,0:T(8,128)(2,1)S(1)} %pad_maximum_fusion), channel_id=1, source_target_pairs={{0,16},{32,48},{64,80},{96,112},{128,144},{160,176},{192,208},{224... | collective-permute-start | bytes 1130504 | tf_op jit(solution)/shard_map/ppermute | solution.py:527
  20.3 3.4 %collective-permute-start.3 = (bf16[3,10,32,128]{3,2,1,0:T(8,128)(2,1)S(1)}, bf16[3,10,32,128]{3,2,1,0:T(8,128)(2,1)S(1)}, u32[]{:S(2)}, u32[]{:S(2)}) collective-permute-start(bf16[3,10,32,128]{3,2,1,0:T(8,128)(2,1)S(1)} %get-tuple-element.26), channel_id=1, source_target_pairs={{16,32},{48,64},{80,96},{112,128},{144,160},{176,192},{208,224},{2... | collective-permute-start | bytes 737288 | tf_op jit(solution)/shard_map/ppermute | solution.py:527
  23.7 0.2 copy.29
  23.9 0.2 reshape.44.strips
  24.1 0.2 copy.27
  24.2 0.2 reshape.43
  24.7 0.2 copy.26
  24.9 0.2 reshape.42.strips
  25.1 3.1 %collective-permute-start.4 = (bf16[2,8,32,128]{3,2,1,0:T(8,128)(2,1)S(1)}, bf16[2,8,32,128]{3,2,1,0:T(8,128)(2,1)S(1)}, u32[]{:S(2)}, u32[]{:S(2)}) collective-permute-start(bf16[2,8,32,128]{3,2,1,0:T(8,128)(2,1)S(1)} %get-tuple-element.28), channel_id=1, source_target_pairs={{16,32},{48,64},{80,96},{112,128},{144,160},{176,192},{208,224},{2... | collective-permute-start | bytes 393224 | tf_op jit(solution)/shard_map/ppermute | solution.py:527
  28.2 3.1 %collective-permute-done.3.far = bf16[3,10,32,128]{3,2,1,0:T(8,128)(2,1)S(1)} collective-permute-done((bf16[3,10,32,128]{3,2,1,0:T(8,128)(2,1)S(1)}, bf16[3,10,32,128]{3,2,1,0:T(8,128)(2,1)S(1)}, u32[]{:S(2)}, u32[]{:S(2)}) %collective-permute-start.3) | collective-permute-done | bytes 245792 | tf_op jit(solution)/shard_map/ppermute | solution.py:527
  31.4 3.4 %shard_map.95 = (bf16[6,6,32,128]{3,2,1,0:T(8,128)(2,1)S(1)}, f32[6,6,32,128]{3,2,1,0:T(8,128)S(1)}, bf16[128,128]{1,0:T(8,128)(2,1)S(1)}, bf16[4,64,128]{2,1,0:T(8,128)(2,1)}) custom-call(s32[2]{0:T(128)S(1)} %pad_add_fusion.pos, bf16[4,10,32,128]{3,2,1,0:T(8,128)(2,1)S(1)} %pad_maximum_fusion.1.vol, bf16[46,32,128]{2,1,0:T(8,128)(2,1)S(1)} %collective-permute-done.2.close, ...), custom_call_target="tpu_custom_call" | custom-call | flops 400000000 | bytes 2000000 | tf_op jit(solution)/shard_map/pallas_call | solution.py:507
  34.8 3.3 %all-to-all-start = ((bf16[4,64,128]{2,1,0:T(8,128)(2,1)}), bf16[4,64,128]{2,1,0:T(8,128)(2,1)S(1)}, u32[]{:S(2)}, u32[]{:S(2)}) async-start(bf16[4,64,128]{2,1,0:T(8,128)(2,1)} %get-tuple-element.14), calls=%async_computation | async-start | bytes 131072 | tf_op jit(solution)/shard_map/all_to_all | solution.py:548
  38.1 1.6 %shard_map.96 = (bf16[6,6,32,128]{3,2,1,0:T(8,128)(2,1)S(1)}, bf16[64,128]{1,0:T(8,128)(2,1)S(1)}) custom-call(s32[2]{0:T(128)S(1)} %pad_add_fusion.pos, bf16[4,8,32,128]{3,2,1,0:T(8,128)(2,1)S(1)} %pad_maximum_fusion.2.cot, bf16[46,32,128]{2,1,0:T(8,128)(2,1)S(1)} %collective-permute-done.2.close, bf16[2,8,32,128]{3,2,1,0:T(8,128)(2,1)S(1)} %collective-permute-done.4.far, ...), custom_call_target="tpu_custom_call" | custom-call | flops 400000000 | bytes 2000000 | tf_op jit(solution)/shard_map/pallas_call | solution.py:507
  39.9 0.7 broadcast_in_dim.3
  40.6 11.6 %all-to-all-start.1 = ((bf16[4,256,128]{2,1,0:T(8,128)(2,1)}), bf16[4,256,128]{2,1,0:T(8,128)(2,1)S(1)}, u32[]{:S(2)}, u32[]{:S(2)}) async-start(bf16[4,256,128]{2,1,0:T(8,128)(2,1)} %broadcast_in_dim.3), calls=%async_computation.1 | async-start | bytes 524288 | tf_op jit(solution)/shard_map/all_to_all | solution.py:548
  52.2 2.3 %copy.41 = bf16[3,128,3,3,64]{4,3,2,1,0:T(4,128)(2,1)S(1)} copy(bf16[3,128,3,3,64]{1,4,0,3,2:T(8,128)(2,1)} %bitcast.49) | data formatting | bytes 884736 | tf_op jit(solution)/shard_map/reshape | solution.py:17
  54.5 0.8 reshape.52.weight
  55.4 2.6 %all-to-all-done.1.got.early = bf16[4,256,128]{2,1,0:T(8,128)(2,1)S(1)} async-done(((bf16[4,256,128]{2,1,0:T(8,128)(2,1)}), bf16[4,256,128]{2,1,0:T(8,128)(2,1)S(1)}, u32[]{:S(2)}, u32[]{:S(2)}) %all-to-all-start.1) | async-done | bytes 262176 | tf_op jit(solution)/shard_map/all_to_all | solution.py:548
  58.1 1.3 %shard_map.97.mine = bf16[736,128]{1,0:T(8,128)(2,1)S(1)} custom-call(s32[2]{0:T(128)S(1)} %pad_add_fusion.pos, bf16[4,256,128]{2,1,0:T(8,128)(2,1)S(1)} %all-to-all-done.1.got.early, bf16[384,576]{1,0:T(8,128)(2,1)S(1)} %reshape.52.weight, bf16[64,128]{1,0:T(8,128)(2,1)S(1)} %copy-done), custom_call_target="tpu_custom_call" | custom-call | flops 400000000 | bytes 2000000 | tf_op jit(solution)/shard_map/pallas_call | solution.py:507
  59.4 1.9 %collective-permute-start.6 = (bf16[736,128]{1,0:T(8,128)(2,1)S(1)}, bf16[736,128]{1,0:T(8,128)(2,1)S(1)}, u32[]{:S(2)}, u32[]{:S(2)}) collective-permute-start(bf16[736,128]{1,0:T(8,128)(2,1)S(1)} %shard_map.97.mine), channel_id=1, source_target_pairs={{0,1},{2,3},{4,5},{6,7},{8,9},{10,11},{12,13},{14,15},{1,0},{3,2},... | collective-permute-start | bytes 565256 | tf_op jit(solution)/shard_map/ppermute | solution.py:527
  61.3 5.2 %collective-permute-start.5 = (bf16[736,128]{1,0:T(8,128)(2,1)S(1)}, bf16[736,128]{1,0:T(8,128)(2,1)S(1)}, u32[]{:S(2)}, u32[]{:S(2)}) collective-permute-start(bf16[736,128]{1,0:T(8,128)(2,1)S(1)} %shard_map.97.mine), channel_id=1, source_target_pairs={{0,16},{32,48},{64,80},{96,112},{128,144},{160,176},{192,208},{224... | collective-permute-start | bytes 565256 | tf_op jit(solution)/shard_map/ppermute | solution.py:527
  66.5 5.5 %collective-permute-start.7 = (bf16[736,128]{1,0:T(8,128)(2,1)S(1)}, bf16[736,128]{1,0:T(8,128)(2,1)S(1)}, u32[]{:S(2)}, u32[]{:S(2)}) collective-permute-start(bf16[736,128]{1,0:T(8,128)(2,1)S(1)} %collective-permute-done.6.side), channel_id=1, source_target_pairs={{0,16},{32,48},{64,80},{96,112},{128,144},{160,176},{192,208},{224... | collective-permute-start | bytes 565256 | tf_op jit(solution)/shard_map/ppermute | solution.py:527
  72.4 0.2 reshape.47
  72.7 0.2 copy.32
  72.9 0.2 reshape.46.weight
  73.1 3.0 %shard_map.98 = (bf16[4,256,128]{2,1,0:T(8,128)(2,1)}, bf16[256,128]{1,0:T(8,128)(2,1)S(1)}) custom-call(s32[2]{0:T(128)S(1)} %pad_add_fusion.pos, bf16[736,128]{1,0:T(8,128)(2,1)S(1)} %shard_map.97.mine, bf16[736,128]{1,0:T(8,128)(2,1)S(1)} %collective-permute-done.5.chip, bf16[736,128]{1,0:T(8,128)(2,1)S(1)} %collective-permute-done.6.side, ...), custom_call_target="tpu_custom_call" | custom-call | flops 400000000 | bytes 2000000 | tf_op jit(solution)/shard_map/pallas_call | solution.py:507
  76.1 5.0 %all-to-all-start.2 = ((bf16[4,256,128]{2,1,0:T(8,128)(2,1)}), bf16[4,256,128]{2,1,0:T(8,128)(2,1)S(1)}, u32[]{:S(2)}, u32[]{:S(2)}) async-start(bf16[4,256,128]{2,1,0:T(8,128)(2,1)} %get-tuple-element.17), calls=%async_computation.2 | async-start | bytes 524288 | tf_op jit(solution)/shard_map/all_to_all | solution.py:548
  81.1 0.4 copy.37
  81.5 0.4 reshape.49.weight
  81.9 4.9 %all-to-all-done.2.got = bf16[4,256,128]{2,1,0:T(8,128)(2,1)S(1)} async-done(((bf16[4,256,128]{2,1,0:T(8,128)(2,1)}), bf16[4,256,128]{2,1,0:T(8,128)(2,1)S(1)}, u32[]{:S(2)}, u32[]{:S(2)}) %all-to-all-start.2) | async-done | bytes 262176 | tf_op jit(solution)/shard_map/all_to_all | solution.py:548
  86.8 1.9 %shard_map.100 = (bf16[4,256,128]{2,1,0:T(8,128)(2,1)}, bf16[8,64,128]{2,1,0:T(8,128)(2,1)S(1)}) custom-call(s32[2]{0:T(128)S(1)} %pad_add_fusion.pos, bf16[4,256,128]{2,1,0:T(8,128)(2,1)S(1)} %all-to-all-done.2.got, bf16[4,256,128]{2,1,0:T(8,128)(2,1)S(1)} %all-to-all-done.1.got.early, bf16[192,1152]{1,0:T(8,128)(2,1)S(1)} %reshape.49.weight), custom_call_target="tpu_custom_call" | custom-call | flops 400000000 | bytes 2000000 | tf_op jit(solution)/shard_map/pallas_call | solution.py:507
  88.7 7.6 %all-to-all-start.3 = ((bf16[4,256,128]{2,1,0:T(8,128)(2,1)}), bf16[4,256,128]{2,1,0:T(8,128)(2,1)S(1)}, u32[]{:S(2)}, u32[]{:S(2)}) async-start(bf16[4,256,128]{2,1,0:T(8,128)(2,1)} %get-tuple-element.18), calls=%async_computation.3 | async-start | bytes 524288 | tf_op jit(solution)/shard_map/all_to_all | solution.py:548
  96.4 0.2 copy.38
  96.5 0.2 reshape.50.second_b
  96.9 0.2 reshape.51.strips
  97.1 0.2 copy-done.8
  97.3 0.2 copy.36
  97.5 0.2 reshape.48.strips
  97.7 1.2 %shard_map.99 = bf16[4,4,32,128]{3,2,1,0:T(8,128)(2,1)S(1)} custom-call(s32[2]{0:T(128)S(1)} %pad_add_fusion.pos, bf16[256,128]{1,0:T(8,128)(2,1)S(1)} %get-tuple-element.15.hidden, bf16[6,6,32,128]{3,2,1,0:T(8,128)(2,1)S(1)} %get-tuple-element.16.hid, bf16[3,96,96]{2,1,0:T(8,128)(2,1)S(1)} %reshape.48.strips), custom_call_target="tpu_custom_call" | custom-call | flops 400000000 | bytes 2000000 | tf_op jit(solution)/shard_map/pallas_call | solution.py:507
  98.9 0.7 copy.40
  99.6 1.8 %all-to-all-done.3.got = bf16[4,256,128]{2,1,0:T(8,128)(2,1)S(1)} async-done(((bf16[4,256,128]{2,1,0:T(8,128)(2,1)}), bf16[4,256,128]{2,1,0:T(8,128)(2,1)S(1)}, u32[]{:S(2)}, u32[]{:S(2)}) %all-to-all-start.3) | async-done | bytes 262176 | tf_op jit(solution)/shard_map/all_to_all | solution.py:548
  101.4 2.5 %shard_map.101 = bf16[32,4,4,128]{3,2,1,0:T(4,128)(2,1)} custom-call(s32[2]{0:T(128)S(1)} %pad_add_fusion.pos, bf16[4,256,128]{2,1,0:T(8,128)(2,1)S(1)} %all-to-all-done.3.got, bf16[8,64,128]{2,1,0:T(8,128)(2,1)S(1)} %get-tuple-element.19.mine, bf16[6,6,32,128]{3,2,1,0:T(8,128)(2,1)S(1)} %get-tuple-element.20.gj, ...), custom_call_target="tpu_custom_call" | custom-call | flops 400000000 | bytes 2000000 | tf_op jit(solution)/shard_map/pallas_call | solution.py:507
  (51 shorter events, 1.4 us)
Async XLA Ops:
  2.6 6.3 %collective-permute-start = (bf16[4,5,32,128]{3,2,1,0:T(8,128)(2,1)S(1)}, bf16[4,5,32,128]{3,2,1,0:T(8,128)(2,1)S(1)}, u32[]{:S(2)}, u32[]{:S(2)}) collective-permute-start(bf16[4,5,32,128]{3,2,1,0:T(8,128)(2,1)S(1)} %pad_maximum_fusion.3), channel_id=1, source_target_pairs={{0,1},{1,2},{2,3},{3,4},{4,5},{5,6},{6,7},{7,8},{8,9},{9,10},{10,1... | collective-permute-start | bytes 491528 | tf_op jit(solution)/shard_map/ppermute | solution.py:521
  6.7 8.1 %collective-permute-start.1 = (bf16[4,5,32,128]{3,2,1,0:T(8,128)(2,1)S(1)}, bf16[4,5,32,128]{3,2,1,0:T(8,128)(2,1)S(1)}, u32[]{:S(2)}, u32[]{:S(2)}) collective-permute-start(bf16[4,5,32,128]{3,2,1,0:T(8,128)(2,1)S(1)} %pad_maximum_fusion.4), channel_id=1, source_target_pairs={{1,0},{2,1},{3,2},{4,3},{5,4},{6,5},{7,6},{8,7},{9,8},{10,9},{11,1... | collective-permute-start | bytes 491528 | tf_op jit(solution)/shard_map/ppermute | solution.py:521
  14.9 8.8 %copy-start.7 = (bf16[3,3,3,32,32]{4,3,2,1,0:T(8,128)(2,1)S(1)}, bf16[3,3,3,32,32]{4,3,2,1,0:T(8,128)(2,1)}, u32[]{:S(2)}) copy-start(bf16[3,3,3,32,32]{4,3,2,1,0:T(8,128)(2,1)} %param.15) | copy-start | bytes 165892
  15.0 9.1 %copy-start.3 = (bf16[3,3,3,32,64]{4,3,2,1,0:T(8,128)(2,1)S(1)}, bf16[3,3,3,32,64]{4,3,2,1,0:T(8,128)(2,1)}, u32[]{:S(2)}) copy-start(bf16[3,3,3,32,64]{4,3,2,1,0:T(8,128)(2,1)} %param.11) | copy-start | bytes 331780
  15.1 16.3 %collective-permute-start.2 = (bf16[46,32,128]{2,1,0:T(8,128)(2,1)S(1)}, bf16[46,32,128]{2,1,0:T(8,128)(2,1)S(1)}, u32[]{:S(2)}, u32[]{:S(2)}) collective-permute-start(bf16[46,32,128]{2,1,0:T(8,128)(2,1)S(1)} %pad_maximum_fusion), channel_id=1, source_target_pairs={{0,16},{32,48},{64,80},{96,112},{128,144},{160,176},{192,208},{224... | collective-permute-start | bytes 1130504 | tf_op jit(solution)/shard_map/ppermute | solution.py:527
  20.3 11.0 %collective-permute-start.3 = (bf16[3,10,32,128]{3,2,1,0:T(8,128)(2,1)S(1)}, bf16[3,10,32,128]{3,2,1,0:T(8,128)(2,1)S(1)}, u32[]{:S(2)}, u32[]{:S(2)}) collective-permute-start(bf16[3,10,32,128]{3,2,1,0:T(8,128)(2,1)S(1)} %get-tuple-element.26), channel_id=1, source_target_pairs={{16,32},{48,64},{80,96},{112,128},{144,160},{176,192},{208,224},{2... | collective-permute-start | bytes 737288 | tf_op jit(solution)/shard_map/ppermute | solution.py:527
  23.7 0.9 copy-start.5
  25.1 13.0 %collective-permute-start.4 = (bf16[2,8,32,128]{3,2,1,0:T(8,128)(2,1)S(1)}, bf16[2,8,32,128]{3,2,1,0:T(8,128)(2,1)S(1)}, u32[]{:S(2)}, u32[]{:S(2)}) collective-permute-start(bf16[2,8,32,128]{3,2,1,0:T(8,128)(2,1)S(1)} %get-tuple-element.28), channel_id=1, source_target_pairs={{16,32},{48,64},{80,96},{112,128},{144,160},{176,192},{208,224},{2... | collective-permute-start | bytes 393224 | tf_op jit(solution)/shard_map/ppermute | solution.py:527
  34.8 5.0 %all-to-all-start = ((bf16[4,64,128]{2,1,0:T(8,128)(2,1)}), bf16[4,64,128]{2,1,0:T(8,128)(2,1)S(1)}, u32[]{:S(2)}, u32[]{:S(2)}) async-start(bf16[4,64,128]{2,1,0:T(8,128)(2,1)} %get-tuple-element.14), calls=%async_computation | async-start | bytes 131072 | tf_op jit(solution)/shard_map/all_to_all | solution.py:548
  40.6 17.5 %all-to-all-start.1 = ((bf16[4,256,128]{2,1,0:T(8,128)(2,1)}), bf16[4,256,128]{2,1,0:T(8,128)(2,1)S(1)}, u32[]{:S(2)}, u32[]{:S(2)}) async-start(bf16[4,256,128]{2,1,0:T(8,128)(2,1)} %broadcast_in_dim.3), calls=%async_computation.1 | async-start | bytes 524288 | tf_op jit(solution)/shard_map/all_to_all | solution.py:548
  54.5 3.5 %copy-start = (bf16[64,128]{1,0:T(8,128)(2,1)S(1)}, bf16[64,128]{1,0:T(8,128)(2,1)}, u32[]{:S(2)}) copy-start(bf16[64,128]{1,0:T(8,128)(2,1)} %lift.1) | copy-start | bytes 49156
  55.4 16.8 %copy-start.2 = (bf16[3,3,3,64,32]{3,4,2,1,0:T(8,128)(2,1)S(1)}, bf16[3,3,3,64,32]{3,4,2,1,0:T(8,128)(2,1)}, u32[]{:S(2)}) copy-start(bf16[3,3,3,64,32]{3,4,2,1,0:T(8,128)(2,1)} %param.14) | copy-start | bytes 331780
  59.4 7.1 %collective-permute-start.6 = (bf16[736,128]{1,0:T(8,128)(2,1)S(1)}, bf16[736,128]{1,0:T(8,128)(2,1)S(1)}, u32[]{:S(2)}, u32[]{:S(2)}) collective-permute-start(bf16[736,128]{1,0:T(8,128)(2,1)S(1)} %shard_map.97.mine), channel_id=1, source_target_pairs={{0,1},{2,3},{4,5},{6,7},{8,9},{10,11},{12,13},{14,15},{1,0},{3,2},... | collective-permute-start | bytes 565256 | tf_op jit(solution)/shard_map/ppermute | solution.py:527
  61.3 11.8 %collective-permute-start.5 = (bf16[736,128]{1,0:T(8,128)(2,1)S(1)}, bf16[736,128]{1,0:T(8,128)(2,1)S(1)}, u32[]{:S(2)}, u32[]{:S(2)}) collective-permute-start(bf16[736,128]{1,0:T(8,128)(2,1)S(1)} %shard_map.97.mine), channel_id=1, source_target_pairs={{0,16},{32,48},{64,80},{96,112},{128,144},{160,176},{192,208},{224... | collective-permute-start | bytes 565256 | tf_op jit(solution)/shard_map/ppermute | solution.py:527
  66.5 6.6 %collective-permute-start.7 = (bf16[736,128]{1,0:T(8,128)(2,1)S(1)}, bf16[736,128]{1,0:T(8,128)(2,1)S(1)}, u32[]{:S(2)}, u32[]{:S(2)}) collective-permute-start(bf16[736,128]{1,0:T(8,128)(2,1)S(1)} %collective-permute-done.6.side), channel_id=1, source_target_pairs={{0,16},{32,48},{64,80},{96,112},{128,144},{160,176},{192,208},{224... | collective-permute-start | bytes 565256 | tf_op jit(solution)/shard_map/ppermute | solution.py:527
  72.9 8.2 %copy-start.1 = (bf16[3,3,3,64,128]{4,3,2,1,0:T(8,128)(2,1)S(1)}, bf16[3,3,3,64,128]{4,3,2,1,0:T(8,128)(2,1)}, u32[]{:S(2)}) copy-start(bf16[3,3,3,64,128]{4,3,2,1,0:T(8,128)(2,1)} %param.12) | copy-start | bytes 1327108
  76.1 10.7 %all-to-all-start.2 = ((bf16[4,256,128]{2,1,0:T(8,128)(2,1)}), bf16[4,256,128]{2,1,0:T(8,128)(2,1)S(1)}, u32[]{:S(2)}, u32[]{:S(2)}) async-start(bf16[4,256,128]{2,1,0:T(8,128)(2,1)} %get-tuple-element.17), calls=%async_computation.2 | async-start | bytes 524288 | tf_op jit(solution)/shard_map/all_to_all | solution.py:548
  81.9 14.4 %copy-start.4 = (bf16[3,3,3,32,64]{4,3,2,1,0:T(8,128)(2,1)S(1)}, bf16[3,3,3,32,64]{4,3,2,1,0:T(8,128)(2,1)}, u32[]{:S(2)}) copy-start(bf16[3,3,3,32,64]{4,3,2,1,0:T(8,128)(2,1)} %param.11) | copy-start | bytes 331780
  88.7 8.0 %copy-start.6 = (bf16[3,3,3,32,32]{4,3,2,1,0:T(8,128)(2,1)S(1)}, bf16[3,3,3,32,32]{4,3,2,1,0:T(8,128)(2,1)}, u32[]{:S(2)}) copy-start(bf16[3,3,3,32,32]{4,3,2,1,0:T(8,128)(2,1)} %param.10) | copy-start | bytes 165892
  88.7 12.7 %all-to-all-start.3 = ((bf16[4,256,128]{2,1,0:T(8,128)(2,1)}), bf16[4,256,128]{2,1,0:T(8,128)(2,1)S(1)}, u32[]{:S(2)}, u32[]{:S(2)}) async-start(bf16[4,256,128]{2,1,0:T(8,128)(2,1)} %get-tuple-element.18), calls=%async_computation.3 | async-start | bytes 524288 | tf_op jit(solution)/shard_map/all_to_all | solution.py:548
  96.3 0.9 copy-start.8
